TPU v7x, 128 devices: a whole 4x4x4 slice. The times are simulated.
128 devices in a mesh: ctx: 16 (over z_hi, y, core), exp: 8 (over z_lo, x).
Axes of the slice: x: 4, y: 4, z: 4 (z_hi: 2, z_lo: 2; z = z_hi * 2 + z_lo), core: 2. Of those that a mesh axis runs over, the one named last changes fastest.
Arguments:
- hidden: bfloat16 [16384, 2048], P(('ctx', 'exp')), may hold values from -6 to 6
- queries: bfloat16 [16384, 2048], P(('ctx', 'exp')), may hold values from -16 to 16
- keys: bfloat16 [16384, 256], P(('ctx', 'exp')), may hold values from -4 to 4
- values: bfloat16 [16384, 256], P(('ctx', 'exp')), may hold values from -6 to 6
- w_out: bfloat16 [2048, 2048], replicated, may hold values from -0.125 to 0.125
- norm_gain: float32 [2048], replicated, may hold values from 0.5 to 1.5
- w_router: bfloat16 [2048, 128], replicated, may hold values from -0.125 to 0.125
- expert_ids: int32 [16384, 8], P(('ctx', 'exp')), may hold values from 0 to 127, all different within a row; in each aligned block of 128 rows (0 to 127, 128 to 255, ...) at most 9 rows name the same one
- w_gate: bfloat16 [128, 2048, 768], P(('ctx', 'exp')), may hold values from -0.125 to 0.125
- w_up: bfloat16 [128, 2048, 768], P(('ctx', 'exp')), may hold values from -0.125 to 0.125
- w_down: bfloat16 [128, 768, 2048], P(('ctx', 'exp')), may hold values from -0.21875 to 0.21875
Outputs:
- mixed: bfloat16 [16384, 2048], P(('ctx', 'exp'))
Inputs may be any that keep to these rules, and one draw needn't show every extreme that they name: `expert_ids`: within the 128 tokens of one device, no expert is named by more than 9 of their routes, a bound that some block reaches of them; a token's experts are distinct.
All inputs are finite; a program needn't handle non-finite values.
Results may differ from a plain program's by a relative error of at most 0.01.
Values may be sent and summed in bfloat16 or wider, within the bound.
No kernel may reach another device: no remote copies, remote signals or barrier semaphores. Data moves between devices by JAX's collectives and lax.ppermute only.
A program may use at most 192 MiB of HBM per device.

v0:
```python
import math

import jax
import jax.numpy as jnp
from jax import lax
from jax.sharding import PartitionSpec as P

DH = 128
TOP = 8
CAP = 9


rope_base = 1000000.0
yarn_factor = 4.0
orig_len = 32768.0
beta_fast = 32.0
beta_slow = 1.0
mscale_yarn = 0.1 * math.log(4.0) + 1.0


def yarn_tables(positions, head_size):
    half_size = head_size // 2
    index_f = jnp.arange(half_size, dtype=jnp.float32)
    pos_freq = rope_base ** (2.0 * index_f / head_size)
    inv_extra = 1.0 / pos_freq
    inv_inter = 1.0 / (yarn_factor * pos_freq)
    low_dim = max(
        math.floor(
            head_size
            * math.log(orig_len / (beta_fast * 2.0 * math.pi))
            / (2.0 * math.log(rope_base))
        ),
        0,
    )
    high_dim = min(
        math.ceil(
            head_size
            * math.log(orig_len / (beta_slow * 2.0 * math.pi))
            / (2.0 * math.log(rope_base))
        ),
        head_size - 1,
    )
    ramp_part = jnp.clip((index_f - low_dim) / max(high_dim - low_dim, 0.001), 0.0, 1.0)
    extra_part = 1.0 - ramp_part
    inverse = inv_inter * (1.0 - extra_part) + inv_extra * extra_part
    angles = positions.astype(jnp.float32)[:, None] * inverse[None, :]
    angles = jnp.concatenate([angles, angles], axis=-1)
    return (jnp.cos(angles) * mscale_yarn, jnp.sin(angles) * mscale_yarn)


def rotate(vectors, cos_table, sin_table):
    values_f = vectors.astype(jnp.float32)
    half_size = values_f.shape[-1] // 2
    turned = jnp.concatenate([-values_f[..., half_size:], values_f[..., :half_size]], axis=-1)
    return (values_f * cos_table[:, None, :] + turned * sin_table[:, None, :]).astype(jnp.bfloat16)


def local(
    hidden, queries, keys, values, w_out, norm_gain, w_router, expert_ids, w_gate, w_up, w_down
):
    tok_rows = hidden.shape[0]
    kv_heads = keys.shape[1] // DH
    q_heads = queries.shape[1] // DH
    group = q_heads // kv_heads
    experts_all = w_router.shape[1]
    width = hidden.shape[1]
    device = lax.axis_index(("ctx", "exp"))
    first_row = device * tok_rows
    positions = first_row + jnp.arange(tok_rows, dtype=jnp.int32)
    cos_table, sin_table = yarn_tables(positions, DH)
    q_four = rotate(queries.reshape(tok_rows, q_heads, DH), cos_table, sin_table).reshape(
        tok_rows, kv_heads, group, DH
    )
    k_flat = rotate(keys.reshape(tok_rows, kv_heads, DH), cos_table, sin_table).reshape(
        tok_rows, kv_heads * DH
    )
    q_rows = first_row + jnp.arange(tok_rows, dtype=jnp.int32)
    scale = 1.0 / math.sqrt(DH)

    def update(carry, operands):
        run_max, run_sum, run_acc = carry
        key_block, value_block, block_start = operands
        block_len = key_block.shape[0]
        scores = (
            jnp.einsum("thgd,phd->thgp", q_four, key_block, preferred_element_type=jnp.float32)
            * scale
        )
        key_rows = block_start + jnp.arange(block_len, dtype=jnp.int32)
        allowed = (key_rows[None, :] <= q_rows[:, None])[:, None, None, :]
        scores = jnp.where(allowed, scores, -1e30)
        new_max = jnp.maximum(run_max, jnp.max(scores, axis=-1))
        weights = jnp.where(allowed, jnp.exp(scores - new_max[..., None]), 0.0)
        factor = jnp.exp(run_max - new_max)
        new_sum = run_sum * factor + jnp.sum(weights, axis=-1)
        added = jnp.einsum(
            "thgp,phd->thgd",
            weights.astype(jnp.bfloat16),
            value_block,
            preferred_element_type=jnp.float32,
        )
        return ((new_max, new_sum, run_acc * factor[..., None] + added), None)

    initial = (
        jnp.full((tok_rows, kv_heads, group), -1e30, jnp.float32),
        jnp.zeros((tok_rows, kv_heads, group), jnp.float32),
        jnp.zeros((tok_rows, kv_heads, group, DH), jnp.float32),
    )
    key_piece = lax.all_gather(k_flat, ("ctx", "exp"), axis=0, tiled=True)
    value_piece = lax.all_gather(values, ("ctx", "exp"), axis=0, tiled=True)
    piece_len = key_piece.shape[0]
    block_len = math.gcd(piece_len, 1024)
    count = piece_len // block_len
    key_blocks = key_piece.reshape(count, block_len, kv_heads, DH)
    value_blocks = value_piece.reshape(count, block_len, kv_heads, DH)
    offsets = jnp.arange(count, dtype=jnp.int32) * block_len
    result, unused = lax.scan(update, initial, (key_blocks, value_blocks, offsets))
    final_max, final_sum, final_acc = result
    attn = (final_acc / final_sum[..., None]).astype(jnp.bfloat16).reshape(tok_rows, q_heads * DH)
    h1 = (
        jnp.dot(attn, w_out, preferred_element_type=jnp.float32) + hidden.astype(jnp.float32)
    ).astype(jnp.bfloat16)
    h1_f = h1.astype(jnp.float32)
    normed = (
        h1_f / jnp.sqrt(jnp.mean(h1_f * h1_f, axis=-1, keepdims=True) + 1e-06) * norm_gain[None, :]
    )
    hn = normed.astype(jnp.bfloat16)
    logits = jnp.dot(hn, w_router, preferred_element_type=jnp.float32)
    onehot = expert_ids[:, :, None] == jnp.arange(experts_all, dtype=jnp.int32)[None, None, :]
    chosen = jnp.sum(jnp.where(onehot, logits[:, None, :], 0.0), axis=-1)
    raised = jnp.exp(chosen)
    route_w = (raised / jnp.sum(raised, axis=-1, keepdims=True)).astype(jnp.bfloat16)
    counts = jnp.cumsum(
        onehot.reshape(tok_rows * TOP, experts_all).astype(jnp.int32), axis=0
    ).reshape(tok_rows, TOP, experts_all)
    slot = jnp.sum(jnp.where(onehot, counts, 0), axis=-1) - 1
    target = expert_ids * CAP + slot
    slot_ids = jnp.arange(experts_all * CAP, dtype=jnp.int32)
    match = slot_ids[:, None, None] == target[None, :, :]
    filled = jnp.any(match, axis=(1, 2))
    owner = jnp.sum(
        jnp.where(match, jnp.arange(tok_rows, dtype=jnp.int32)[None, :, None], 0), axis=(1, 2)
    )
    send = jnp.where(filled[:, None], hn[owner], jnp.zeros((), jnp.bfloat16)).reshape(
        experts_all, CAP, width
    )
    local_experts = w_gate.shape[0]
    arrived = lax.all_to_all(send, ("ctx", "exp"), split_axis=0, concat_axis=0, tiled=True)
    items = arrived.shape[1]
    sources = arrived.shape[0] // local_experts
    grouped_rows = arrived.reshape(sources, local_experts, items, width)
    gate_v = jnp.einsum("neid,edf->neif", grouped_rows, w_gate, preferred_element_type=jnp.float32)
    up_v = jnp.einsum("neid,edf->neif", grouped_rows, w_up, preferred_element_type=jnp.float32)
    active = (jax.nn.silu(gate_v) * up_v).astype(jnp.bfloat16)
    produced = jnp.einsum(
        "neif,efd->neid", active, w_down, preferred_element_type=jnp.float32
    ).astype(jnp.bfloat16)
    produced = produced.reshape(sources * local_experts, items, width)
    returned = lax.all_to_all(
        produced, ("ctx", "exp"), split_axis=0, concat_axis=0, tiled=True
    ).reshape(experts_all * CAP, width)
    combine = jnp.sum(
        jnp.where(
            slot_ids[None, None, :] == target[:, :, None],
            route_w.astype(jnp.float32)[:, :, None],
            0.0,
        ),
        axis=1,
    ).astype(jnp.bfloat16)
    total_out = jnp.dot(combine, returned, preferred_element_type=jnp.float32) + h1_f
    return total_out.astype(jnp.bfloat16)


def solution(mesh):
    in_specs = (
        P(("ctx", "exp"), None),
        P(("ctx", "exp"), None),
        P(("ctx", "exp"), None),
        P(("ctx", "exp"), None),
        P(),
        P(),
        P(),
        P(("ctx", "exp"), None),
        P(("ctx", "exp"), None, None),
        P(("ctx", "exp"), None, None),
        P(("ctx", "exp"), None, None),
    )
    out_specs = P(("ctx", "exp"), None)
    return jax.shard_map(local, mesh=mesh, in_specs=in_specs, out_specs=out_specs, check_vma=False)
```

profile of v0, /device:TPU:9, one launch (start us, length us, event | category | flops | bytes accessed | tf_op | source)
XLA Modules:
  0.0 1331.3 jit_solution(17168790541100619867)
XLA Ops:
  22.7 20.5 %fusion.20 = pred[1152]{0:T(1024)(128)(4,1)S(1)} fusion(s32[128,8]{0,1:T(8,128)S(1)} %multiply_add_fusion), kind=kLoop, calls=%fused_computation.30 | loop fusion | flops 2358144 | bytes 5248 | tf_op jit(solution)/shard_map/reduce_or | solution.py:139
  43.5 20.7 %select_reduce_fusion = s32[1152]{0:T(1024)S(1)} fusion(s32[128,8]{0,1:T(8,128)S(1)} %multiply_add_fusion), kind=kLoop, calls=%fused_computation.28 | loop fusion | flops 3537792 | bytes 8704 | tf_op jit(solution)/shard_map/reduce_sum | solution.py:140
  64.3 261.0 %all-gather.3.cloned.1.call-done = bf16[16384,256]{1,0:T(8,128)(2,1)} async-done(((bf16[128,256]{1,0:T(8,128)(2,1)}), bf16[16384,256]{1,0:T(8,128)(2,1)}) %all-gather.3.cloned.1.call-update) | async-done | bytes 8388624 | tf_op jit(solution)/shard_map/all_gather | solution.py:108
  325.3 12.5 reshape.258
  337.8 299.4 %all-gather.5.cloned.1.call-done = bf16[16384,256]{1,0:T(8,128)(2,1)} async-done(((bf16[128,256]{1,0:T(8,128)(2,1)}), bf16[16384,256]{1,0:T(8,128)(2,1)}) %all-gather.5.cloned.1.call-update) | async-done | bytes 8388624 | tf_op jit(solution)/shard_map/all_gather | solution.py:109
  637.2 12.5 reshape.259
  649.8 373.1 %while.15 = (s32[]{:T(128)}, f32[128,2,8]{0,2,1:T(8,128)S(1)}, f32[128,2,8]{0,2,1:T(8,128)S(1)}, f32[128,2,8,128]{0,3,2,1:T(8,128)}, s32[16]{0:T(128)S(1)}, /*in...) while((s32[]{:T(128)}, f32[128,2,8]{0,2,1:T(8,128)S(1)}, ...), condition=%wide.region_6.7_spmd.clone, body=%wide.region_3.6_spmd.clone.sunk | while | flops 1101933696 | bytes 32646288 | solution.py:116
  654.3 5.6 fusion.81
  666.5 6.8 fusion.84
  677.4 5.6 fusion.81
  689.6 7.0 fusion.84
  700.8 5.6 fusion.81
  712.9 7.0 fusion.84
  724.1 5.6 fusion.81
  736.2 7.0 fusion.84
  747.4 5.6 fusion.81
  759.5 7.0 fusion.84
  770.7 5.6 fusion.81
  782.8 7.0 fusion.84
  794.0 5.6 fusion.81
  806.1 7.0 fusion.84
  829.4 7.0 fusion.84
  840.6 5.6 fusion.81
  852.7 7.0 fusion.84
  863.9 5.6 fusion.81
  876.0 7.0 fusion.84
  887.2 5.6 fusion.81
  899.3 7.0 fusion.84
  910.5 5.6 fusion.81
  922.7 7.0 fusion.84
  933.8 5.6 fusion.81
  946.0 7.0 fusion.84
  957.2 5.6 fusion.81
  969.3 7.0 fusion.84
  980.5 5.6 fusion.81
  992.6 7.0 fusion.84
  1003.8 5.6 fusion.81
  1015.9 7.0 fusion.84
  1031.1 11.8 gather_fusion
  1042.8 8.0 gather.6
  1050.9 7.3 broadcast_select_fusion
  1058.2 104.6 %all_to_all.10 = bf16[128,9,2048]{2,1,0:T(8,128)(2,1)S(1)} all-to-all(bf16[128,9,2048]{2,1,0:T(8,128)(2,1)} %broadcast_select_fusion), channel_id=1, replica_groups=mesh['ctx'=16,'exp'=8] {'ctx','exp'}, dimensions={0} | all-to-all | bytes 9437184 | tf_op jit(solution)/shard_map/all_to_all | solution.py:147
  1162.7 9.2 fusion.26
  1171.9 9.9 fusion.21
  1185.9 6.3 copy.97
  1192.2 7.9 all-to-all-start.1
  1205.3 106.0 %all-to-all-done.1 = bf16[128,9,2048]{2,1,0:T(8,128)(2,1)} async-done(((bf16[128,9,2048]{2,1,0:T(8,128)(2,1)}), bf16[128,9,2048]{2,1,0:T(8,128)(2,1)}, u32[]{:S(2)}, u32[]{:S(2)}) %all-to-all-start.1) | async-done | bytes 4718624 | tf_op jit(solution)/shard_map/all_to_all | solution.py:158
  1311.3 8.4 reshape.241
  (231 shorter events, 213.9 us)
Async XLA Ops:
  6.5 1175.3 %copy-start = (bf16[1,768,2048]{2,1,0:T(8,128)(2,1)S(1)}, bf16[1,768,2048]{2,1,0:T(8,128)(2,1)}, u32[]{:S(2)}) copy-start(bf16[1,768,2048]{2,1,0:T(8,128)(2,1)} %param.23) | copy-start | bytes 9437188
  6.5 318.8 %all-gather.3.cloned.1.call-start = ((), (), s32[]{:S(2)}) async-start(), calls=%async_computation.2 | async-start | bytes 8454144 | tf_op jit(solution)/shard_map/all_gather | solution.py:108
  11.8 625.4 %all-gather.5.cloned.1.call-start = ((), (), s32[]{:S(2)}) async-start(), calls=%async_computation.3 | async-start | bytes 8454144 | tf_op jit(solution)/shard_map/all_gather | solution.py:109
  16.8 6.0 copy-start.3
  20.2 0.8 copy-start.2
  1024.3 5.8 copy-start.4
  1029.1 1.0 copy-start.1
  1058.2 104.6 %copy-start.5 = (bf16[1,2048,768]{2,1,0:T(8,128)(2,1)S(1)}, bf16[1,2048,768]{2,1,0:T(8,128)(2,1)}, u32[]{:S(2)}) copy-start(bf16[1,2048,768]{2,1,0:T(8,128)(2,1)} %param.22) | copy-start | bytes 9437188
  1162.7 9.2 copy-start.6
  1192.2 119.1 %all-to-all-start.1 = ((bf16[128,9,2048]{2,1,0:T(8,128)(2,1)}), bf16[128,9,2048]{2,1,0:T(8,128)(2,1)}, u32[]{:S(2)}, u32[]{:S(2)}) async-start(bf16[128,9,2048]{2,1,0:T(8,128)(2,1)} %copy.97), calls=%async_computation.1 | async-start | bytes 16777216 | tf_op jit(solution)/shard_map/all_to_all | solution.py:158
Sparse Core Ops, SparseCore 0:
  12.0 313.2 all-gather.2
  327.0 310.2 all-gather.4
where the time goes:
time: 1340 us; the launch traced here: 1330 us
  waiting for transfers between devices  667 us (50%)
  matrix products  235 us (18%)
  local copies, waits for them, and re-layouts  154 us (11%)
  other arithmetic  147 us (11%)
  blocking collectives  105 us (8%)
  between operations  14.1 us (1%)
    all_gather x1, waiting for transfers between devices, local(): value_piece = lax.all_gather(values, ('ctx', 'exp'), axis=0, tiled=True)  299 us
    all_gather x1, waiting for transfers between devices, local(): key_piece = lax.all_gather(k_flat, ('ctx', 'exp'), axis=0, tiled=True)  261 us
    dot_general x16, matrix products, update(): jnp.einsum('thgp,phd->thgd', weights.astype(jnp.bfloat16), value_block, p...  112 us
    all_to_all x1, waiting for transfers between devices, local(): lax.all_to_all(produced, ('ctx', 'exp'), split_axis=0, concat_axis=0, til...  106 us
    all_to_all x1, blocking collectives, local(): lax.all_to_all(send, ('ctx', 'exp'), split_axis=0, concat_axis=0, tiled=T...  105 us
    dot_general x16, matrix products, update(): jnp.einsum('thgd,phd->thgp', q_four, key_block, preferred_element_type=jn...  89.8 us
    dynamic_slice x48, local copies, waits for them, and re-layouts, local(): lax.scan(update, initial, (key_blocks, value_blocks, offsets))  85 us
    reduce_sum x16, other arithmetic, update(): new_sum = run_sum * factor + jnp.sum(weights, axis=-1)  71.3 us
  transfers between devices with their start and end apart: 3, of which 3 were waited for; matrix products, arithmetic and copies ran while one was open for 5% of the time, Pallas kernels for 0%

commit v1 on v0

v1 whole, which is shorter than its diff:
```python
import functools
import math

import jax
import jax.numpy as jnp
from jax import lax
from jax.experimental import pallas as pl
from jax.experimental.pallas import tpu as pltpu
from jax.sharding import Mesh, PartitionSpec as P

DH = 128
TOP = 8
CAP = 9
MAIN = 8
BLOCK = 128
BLOCKS = 128
CHUNK_BLOCKS = 8
AXES = ("zh", "y", "c", "zl", "x")
TORUS = ("zh", "zl", "y", "x", "c")

rope_base = 1000000.0
yarn_factor = 4.0
orig_len = 32768.0
beta_fast = 32.0
beta_slow = 1.0
mscale_yarn = 0.1 * math.log(4.0) + 1.0

F32 = jnp.float32
BF16 = jnp.bfloat16
VMEM_LIMIT = 60 * 1024 * 1024


def params(*semantics):
    return pltpu.CompilerParams(
        dimension_semantics=semantics, vmem_limit_bytes=VMEM_LIMIT
    )


def yarn_tables(positions, head_size):
    half_size = head_size // 2
    index_f = jnp.arange(half_size, dtype=jnp.float32)
    pos_freq = rope_base ** (2.0 * index_f / head_size)
    inv_extra = 1.0 / pos_freq
    inv_inter = 1.0 / (yarn_factor * pos_freq)
    low_dim = max(
        math.floor(
            head_size
            * math.log(orig_len / (beta_fast * 2.0 * math.pi))
            / (2.0 * math.log(rope_base))
        ),
        0,
    )
    high_dim = min(
        math.ceil(
            head_size
            * math.log(orig_len / (beta_slow * 2.0 * math.pi))
            / (2.0 * math.log(rope_base))
        ),
        head_size - 1,
    )
    ramp_part = jnp.clip((index_f - low_dim) / max(high_dim - low_dim, 0.001), 0.0, 1.0)
    extra_part = 1.0 - ramp_part
    inverse = inv_inter * (1.0 - extra_part) + inv_extra * extra_part
    angles = positions.astype(jnp.float32)[:, None] * inverse[None, :]
    cos_half = jnp.cos(angles) * mscale_yarn
    sin_half = jnp.sin(angles) * mscale_yarn
    return (
        jnp.concatenate([cos_half, cos_half], axis=-1),
        jnp.concatenate([-sin_half, sin_half], axis=-1),
    )


def rotate_kernel(core_ref, q_ref, k_ref, v_ref, cos_ref, sin_ref, keep_ref, give_ref, kv_ref):
    core = core_ref[0]
    cos_t = cos_ref[...]
    sin_t = sin_ref[...]

    def rotated(part):
        value = part.astype(F32)
        return (value * cos_t + pltpu.roll(value, DH // 2, 1) * sin_t).astype(BF16)

    for head in range(2):
        columns = pl.ds(head * DH, DH)
        kv_ref[:, columns] = rotated(k_ref[:, columns])
    kv_ref[:, pl.ds(2 * DH, 2 * DH)] = v_ref[...]
    half = keep_ref.shape[1]
    for out_ref, which in ((keep_ref, core), (give_ref, 1 - core)):
        for head in range(half // DH):
            source = pl.ds(pl.multiple_of(which * half + head * DH, DH), DH)
            out_ref[:, pl.ds(head * DH, DH)] = rotated(q_ref[:, source])


def rotate_all(core, queries, keys, values, cos_t, sin_t):
    rows, width = queries.shape
    vmem = pl.BlockSpec(memory_space=pltpu.VMEM)
    return pl.pallas_call(
        rotate_kernel,
        in_specs=[pl.BlockSpec(memory_space=pltpu.SMEM)] + [vmem] * 5,
        out_specs=[vmem] * 3,
        out_shape=[
            jax.ShapeDtypeStruct((rows, width // 2), BF16),
            jax.ShapeDtypeStruct((rows, width // 2), BF16),
            jax.ShapeDtypeStruct((rows, 4 * DH), BF16),
        ],
        compiler_params=params(),
        name="rotate_all",
    )(core, queries, keys, values, cos_t, sin_t)


def attend_kernel(
    meta_ref, q_ref, k_ref, v_ref, out_ref, max_ref, sum_ref, acc_ref, *, heads, tile_heads
):
    step = pl.program_id(0)
    first_steps = meta_ref[2]
    second = step >= first_steps
    chunk = jnp.where(second, step - first_steps, step)
    block = jnp.where(second, meta_ref[1], meta_ref[0])
    diagonal = block // CHUNK_BLOCKS
    keys_len = CHUNK_BLOCKS * BLOCK
    factor = math.log2(math.e) / math.sqrt(DH)
    rows = tile_heads * BLOCK

    @pl.when(chunk == 0)
    def _():
        max_ref[...] = jnp.full_like(max_ref, -1e30)
        sum_ref[...] = jnp.zeros_like(sum_ref)
        acc_ref[...] = jnp.zeros_like(acc_ref)

    def update(masked):
        keys = k_ref[...].reshape(keys_len, DH)
        vals = v_ref[...].reshape(keys_len, DH)
        if masked:
            offset = (block - chunk * CHUNK_BLOCKS) * BLOCK
            row_token = lax.broadcasted_iota(jnp.int32, (BLOCK, keys_len), 0) + offset
            key_token = lax.broadcasted_iota(jnp.int32, (BLOCK, keys_len), 1)
            allowed = key_token <= row_token
        for part in range(heads // tile_heads):
            span = pl.ds(part * rows, rows)
            query = jnp.concatenate(
                [
                    q_ref[0, :, pl.ds((part * tile_heads + h) * DH, DH)]
                    for h in range(tile_heads)
                ],
                axis=0,
            )
            scores = lax.dot_general(
                query, keys, (((1,), (1,)), ((), ())), preferred_element_type=F32
            )
            if masked:
                scores = jnp.where(
                    allowed[None], scores.reshape(tile_heads, BLOCK, keys_len), -1e30
                ).reshape(rows, keys_len)
            old_max = max_ref[span, :]
            new_max = jnp.maximum(old_max, jnp.max(scores, axis=1, keepdims=True))
            decay = jnp.exp2((old_max - new_max) * factor)
            lane_sum = sum_ref[span, :] * decay
            weights = []
            for column in range(keys_len // DH):
                piece = jnp.exp2((scores[:, column * DH : (column + 1) * DH] - new_max) * factor)
                lane_sum = lane_sum + piece
                weights.append(piece.astype(BF16))
            sum_ref[span, :] = lane_sum
            max_ref[span, :] = new_max
            added = jnp.dot(jnp.concatenate(weights, axis=1), vals, preferred_element_type=F32)
            acc_ref[span, :] = acc_ref[span, :] * decay + added

    @pl.when(chunk == diagonal)
    def _():
        update(True)
        for head in range(heads):
            span = pl.ds(head * BLOCK, BLOCK)
            total = jnp.sum(sum_ref[span, :], axis=1, keepdims=True)
            out_ref[0, :, pl.ds(head * DH, DH)] = (acc_ref[span, :] / total).astype(BF16)

    @pl.when(chunk != diagonal)
    def _():
        update(False)


def attend(meta, q_pair, gathered, tile_heads=2):
    rows, width = q_pair.shape[1:]
    heads = width // DH
    steps = BLOCKS // CHUNK_BLOCKS + 1
    low = CHUNK_BLOCKS // 4

    def place(step, meta_ref):
        first_steps = meta_ref[2]
        second = (step >= first_steps).astype(jnp.int32)
        chunk = step - second * first_steps
        return second, chunk

    def pair_map(step, meta_ref):
        return place(step, meta_ref)[0], 0, 0

    def key_map(column):
        def index(step, meta_ref):
            chunk = place(step, meta_ref)[1]
            if low == 2:
                return chunk // 8, (chunk // 2) % 4, 0, chunk % 2, 0, column + meta_ref[3]
            zh, y, c, zl = chunk // 16, (chunk // 4) % 4, (chunk // 2) % 2, chunk % 2
            return zh * 2 + zl, y, 0, c, 0, column + meta_ref[3]

        return index

    block = (low, 1, 4, 1, BLOCK, DH)
    return pl.pallas_call(
        functools.partial(attend_kernel, heads=heads, tile_heads=tile_heads),
        grid_spec=pltpu.PrefetchScalarGridSpec(
            num_scalar_prefetch=1,
            grid=(steps,),
            in_specs=[
                pl.BlockSpec((1, rows, width), pair_map),
                pl.BlockSpec(block, key_map(0)),
                pl.BlockSpec(block, key_map(2)),
            ],
            out_specs=pl.BlockSpec((1, rows, width), pair_map),
            scratch_shapes=[pltpu.VMEM((heads * rows, DH), F32)] * 3,
        ),
        out_shape=jax.ShapeDtypeStruct((2, rows, width), BF16),
        compiler_params=params("arbitrary"),
        name="attend",
    )(meta, q_pair, gathered, gathered)


def slots_of(ids_ref):
    shape = (BLOCK, BLOCK)
    expert = lax.broadcasted_iota(jnp.int32, shape, 0)
    named = jnp.zeros(shape, F32)
    for k in range(TOP):
        named = named + jnp.where(ids_ref[k : k + 1, :] == expert, 1.0, 0.0)
    earlier = jnp.where(
        lax.broadcasted_iota(jnp.int32, shape, 0) < lax.broadcasted_iota(jnp.int32, shape, 1),
        1.0,
        0.0,
    )
    counts = jnp.dot(named.astype(BF16), earlier.astype(BF16), preferred_element_type=F32)
    return named, jnp.where(named > 0.0, counts, -1.0)


def project_kernel(
    core_ref, own_ref, got_ref, w_ref, hidden_ref, gain_ref, router_ref, ids_ref,
    h1_ref, slot_ref, route_ref, send_ref, over_ref, acc_ref,
):
    step = pl.program_id(0)
    depth = w_ref.shape[0]
    half_steps = pl.num_programs(0) // 2

    @pl.when(step == 0)
    def _():
        acc_ref[...] = jnp.zeros_like(acc_ref)

    column = pl.ds(pl.multiple_of(lax.rem(step, half_steps) * depth, depth), depth)

    @pl.when(step < half_steps)
    def _():
        acc_ref[...] += jnp.dot(own_ref[:, column], w_ref[...], preferred_element_type=F32)

    @pl.when(step >= half_steps)
    def _():
        acc_ref[...] += jnp.dot(got_ref[:, column], w_ref[...], preferred_element_type=F32)

    @pl.when(step == pl.num_programs(0) - 1)
    def _():
        h1 = (acc_ref[...] + hidden_ref[...].astype(F32)).astype(BF16)
        h1_ref[...] = h1
        h1_f = h1.astype(F32)
        mean = jnp.mean(h1_f * h1_f, axis=-1, keepdims=True)
        hn = (h1_f / jnp.sqrt(mean + 1e-06) * gain_ref[...]).astype(BF16)
        logits = jnp.dot(hn, router_ref[...], preferred_element_type=F32)
        named, slot = slots_of(ids_ref)
        slot_ref[...] = slot
        raised = jnp.where(named > 0.0, jnp.exp(jnp.transpose(logits)), 0.0)
        route_ref[...] = raised / jnp.sum(raised, axis=0, keepdims=True)
        wanted = lax.broadcasted_iota(jnp.int32, (BLOCK, MAIN, BLOCK), 1).astype(F32)
        pick = jnp.where(slot[:, None, :] == wanted, 1.0, 0.0).reshape(BLOCK * MAIN, BLOCK)
        send_ref[...] = jnp.dot(pick.astype(BF16), hn, preferred_element_type=F32).astype(BF16)
        last = jnp.where(slot == float(MAIN), 1.0, 0.0).astype(BF16)
        over_ref[...] = jnp.dot(last, hn, preferred_element_type=F32).astype(BF16)


def project(core, own, got, w_out, hidden, gain, w_router, ids_t):
    rows, half = own.shape
    width = hidden.shape[1]
    depth = 512
    half_steps = half // depth

    def w_map(step, core_ref):
        which = jnp.where(step < half_steps, core_ref[0], 1 - core_ref[0])
        return which * half_steps + lax.rem(step, half_steps), 0

    def full(shape):
        return pl.BlockSpec(shape, lambda step, core_ref: (0,) * len(shape))

    experts = w_router.shape[1]
    return pl.pallas_call(
        project_kernel,
        grid_spec=pltpu.PrefetchScalarGridSpec(
            num_scalar_prefetch=1,
            grid=(2 * half_steps,),
            in_specs=[
                full((rows, half)),
                full((rows, half)),
                pl.BlockSpec((depth, width), w_map),
                full((rows, width)),
                full((1, width)),
                full((width, experts)),
                full((TOP, rows)),
            ],
            out_specs=[
                full((rows, width)),
                full((experts, rows)),
                full((experts, rows)),
                full((experts * MAIN, width)),
                full((experts, width)),
            ],
            scratch_shapes=[pltpu.VMEM((rows, width), F32)],
        ),
        out_shape=[
            jax.ShapeDtypeStruct((rows, width), BF16),
            jax.ShapeDtypeStruct((experts, rows), F32),
            jax.ShapeDtypeStruct((experts, rows), F32),
            jax.ShapeDtypeStruct((experts * MAIN, width), BF16),
            jax.ShapeDtypeStruct((experts, width), BF16),
        ],
        compiler_params=params("arbitrary"),
        name="project",
    )(core, own, got, w_out, hidden, gain, w_router, ids_t)


def expert_kernel(
    main_ref, over_ref, gate_ref, up_ref, down_ref, y_main_ref, y_over_ref, act_ref, *, up_steps
):
    step = pl.program_id(0)
    tile = gate_ref.shape[1]
    main_rows = main_ref.shape[0]
    half = main_rows // 2
    spans = [(main_ref, y_main_ref, 0, half, 0), (main_ref, y_main_ref, half, half, half)]
    spans.append((over_ref, y_over_ref, 0, over_ref.shape[0], main_rows))

    for index in range(up_steps):

        @pl.when(step == index)
        def _(index=index):
            for source, _, start, size, place in spans:
                rows = source[start : start + size, :]
                gate = jnp.dot(rows, gate_ref[...], preferred_element_type=F32)
                up = jnp.dot(rows, up_ref[...], preferred_element_type=F32)
                act = gate / (1.0 + jnp.exp(-gate)) * up
                act_ref[place : place + size, index * tile : (index + 1) * tile] = act.astype(BF16)

    @pl.when(step >= up_steps)
    def _():
        for _, target, start, size, place in spans:
            target[start : start + size, :] = jnp.dot(
                act_ref[place : place + size, :], down_ref[...], preferred_element_type=F32
            ).astype(BF16)


def experts_of(main, over, w_gate, w_up, w_down):
    main_rows, width = main.shape
    over_rows = over.shape[0]
    hidden_units = w_gate.shape[1]
    tile = 256
    columns = 512
    up_steps = hidden_units // tile
    steps = up_steps + width // columns

    def up_map(step):
        return 0, jnp.minimum(step, up_steps - 1)

    def down_map(step):
        return 0, jnp.maximum(step - up_steps, 0)

    return pl.pallas_call(
        functools.partial(expert_kernel, up_steps=up_steps),
        grid=(steps,),
        in_specs=[
            pl.BlockSpec((main_rows, width), lambda step: (0, 0)),
            pl.BlockSpec((over_rows, width), lambda step: (0, 0)),
            pl.BlockSpec((width, tile), up_map),
            pl.BlockSpec((width, tile), up_map),
            pl.BlockSpec((hidden_units, columns), down_map),
        ],
        out_specs=[
            pl.BlockSpec((main_rows, columns), down_map),
            pl.BlockSpec((over_rows, columns), down_map),
        ],
        out_shape=[
            jax.ShapeDtypeStruct((main_rows, width), BF16),
            jax.ShapeDtypeStruct((over_rows, width), BF16),
        ],
        scratch_shapes=[pltpu.VMEM((main_rows + over_rows, hidden_units), BF16)],
        compiler_params=params("arbitrary"),
        name="experts_of",
    )(main, over, w_gate, w_up, w_down)


def combine_kernel(slot_ref, route_ref, main_ref, over_ref, h1_ref, out_ref, mix_ref, last_ref):
    @pl.when(pl.program_id(0) == 0)
    def _():
        slot = slot_ref[...]
        route = route_ref[...]
        wanted = lax.broadcasted_iota(jnp.int32, (BLOCK, MAIN, BLOCK), 1).astype(F32)
        mix = jnp.where(slot[:, None, :] == wanted, route[:, None, :], 0.0)
        mix_ref[...] = mix.reshape(BLOCK * MAIN, BLOCK).astype(BF16)
        last_ref[...] = jnp.where(slot == float(MAIN), route, 0.0).astype(BF16)

    def mixed(weights, rows):
        return lax.dot_general(
            weights, rows, (((0,), (0,)), ((), ())), preferred_element_type=F32
        )

    total = mixed(mix_ref[...], main_ref[...]) + mixed(last_ref[...], over_ref[...])
    out_ref[...] = (total + h1_ref[...].astype(F32)).astype(BF16)


def combine(slot, route, main, over, h1):
    rows, width = h1.shape
    columns = 512

    def whole(shape):
        return pl.BlockSpec(shape, lambda step: (0, 0))

    def tiled(count):
        return pl.BlockSpec((count, columns), lambda step: (0, step))

    return pl.pallas_call(
        combine_kernel,
        grid=(width // columns,),
        in_specs=[
            whole(slot.shape),
            whole(route.shape),
            tiled(main.shape[0]),
            tiled(over.shape[0]),
            tiled(rows),
        ],
        out_specs=tiled(rows),
        out_shape=jax.ShapeDtypeStruct((rows, width), BF16),
        scratch_shapes=[
            pltpu.VMEM((main.shape[0], rows), BF16),
            pltpu.VMEM((over.shape[0], rows), BF16),
        ],
        compiler_params=params("arbitrary"),
        name="combine",
    )(slot, route, main, over, h1)


def exchange(main, over):
    experts = over.shape[0]
    width = over.shape[1]
    swap = functools.partial(
        lax.all_to_all, axis_name=AXES, split_axis=0, concat_axis=0, tiled=True
    )
    main = swap(main.reshape(experts, MAIN, width)).reshape(experts * MAIN, width)
    over = swap(over.reshape(experts, width // DH, DH)).reshape(experts, width)
    return main, over


def local(
    hidden, queries, keys, values, w_out, norm_gain, w_router, expert_ids, w_gate, w_up, w_down
):
    rows = hidden.shape[0]
    device = lax.axis_index(AXES)
    core = lax.axis_index("c")
    positions = device * rows + jnp.arange(rows, dtype=jnp.int32)
    cos_t, sin_t = yarn_tables(positions, DH)
    core_arr = core.reshape(1).astype(jnp.int32)
    keep, give, kv = rotate_all(core_arr, queries, keys, values, cos_t, sin_t)
    gathered = lax.all_gather(kv, TORUS, axis=0, tiled=True)
    gathered = gathered.reshape(4, 4, 4, 2, BLOCK, 4 * DH)
    mirror = [(i, BLOCKS - 1 - i) for i in range(BLOCKS)]
    taken = lax.ppermute(give, AXES, mirror)
    other = BLOCKS - 1 - device
    meta = jnp.stack([other, device, other // CHUNK_BLOCKS + 1, core]).astype(jnp.int32)
    attn = attend(meta, jnp.stack([taken, keep]), gathered)
    got = lax.ppermute(attn[0], AXES, mirror)
    h1, slot, route, send, over = project(
        core_arr, attn[1], got, w_out, hidden, norm_gain[None, :], w_router, expert_ids.T
    )
    main, over = exchange(send, over)
    y_main, y_over = experts_of(main, over, w_gate[0], w_up[0], w_down[0])
    y_main, y_over = exchange(y_main, y_over)
    return combine(slot, route, y_main, y_over, h1)


def solution(mesh):
    torus = Mesh(mesh.devices.reshape(2, 4, 2, 2, 4), AXES)
    split = P(AXES, None)
    experts = P(AXES, None, None)
    in_specs = (
        split, split, split, split, P(), P(), P(), split, experts, experts, experts,
    )
    return jax.shard_map(
        local, mesh=torus, in_specs=in_specs, out_specs=split, check_vma=False
    )
```

time: 1340 us -> 345 us (0.26)
  waiting for transfers between devices: 667 us -> 182 us
  matrix products: 235 us -> 0 us
  local copies, waits for them, and re-layouts: 154 us -> 6.66 us
  other arithmetic: 147 us -> 3.55 us
  Pallas kernels: 0 us -> 73.9 us
  blocking collectives: 105 us -> 39.2 us
  starting transfers between devices: 7.93 us -> 23.8 us
    all_gather x2 -> x1, waiting for transfers between devices: 560 us -> 67.4 us  [local(): gathered = lax.all_gather(kv, TORUS, axis=0, tiled=True)]
    dot_general x38 -> x0, matrix products: 235 us -> none  [the longest x16 112 us: update(): jnp.einsum('thgp,phd->thgd', weights.astype(jnp.bfloat16), value_block, p...]
    reduce_sum x21 -> x0, other arithmetic: 95.1 us -> none  [the longest x16 71.3 us: update(): new_sum = run_sum * factor + jnp.sum(weights, axis=-1)]
    dynamic_slice x48 -> x0, local copies, waits for them, and re-layouts: 85 us -> none  [local(): lax.scan(update, initial, (key_blocks, value_blocks, offsets))]
    pallas_call x0 -> x5, Pallas kernels: none -> 73.9 us  [the longest x1 39.4 us: attend(): pl.pallas_call(functools.partial(attend_kernel, heads=heads, tile_heads=t...]
    all_to_all x1 -> x2, blocking collectives: 105 us -> 39.2 us  [exchange(): over = swap(over.reshape(experts, width // DH, DH)).reshape(experts, width)]
    reshape x3 -> x0, local copies, waits for them, and re-layouts: 33.5 us -> none  [the longest x1 12.5 us: local(): key_blocks = key_piece.reshape(count, block_len, kv_heads, DH)]
    reduce_or x1 -> x0, other arithmetic: 20.5 us -> none  [local(): filled = jnp.any(match, axis=(1, 2))]
  transfers between devices with their start and end apart: 3 -> 5, of which waited for: 3 -> 5; matrix products, arithmetic and copies ran while one was open for 5% -> 1% of each run, Pallas kernels for 0% -> 0%
where the time goes in v1:
time: 345 us; the launch traced here: 343 us
  waiting for transfers between devices  182 us (53%)
  Pallas kernels  73.9 us (21%)
  blocking collectives  39.2 us (11%)
  starting transfers between devices  23.8 us (7%)
  between operations  13.5 us (4%)
  local copies, waits for them, and re-layouts  6.66 us (2%)
  other arithmetic  3.55 us (1%)
    all_to_all x2, waiting for transfers between devices, exchange(): swap(main.reshape(experts, MAIN, width)).reshape(experts * MAIN, width)  100 us
    all_gather x1, waiting for transfers between devices, local(): gathered = lax.all_gather(kv, TORUS, axis=0, tiled=True)  67.4 us
    pallas_call x1, Pallas kernels, attend(): pl.pallas_call(functools.partial(attend_kernel, heads=heads, tile_heads=t...  39.4 us
    all_to_all x2, blocking collectives, exchange(): over = swap(over.reshape(experts, width // DH, DH)).reshape(experts, width)  39.2 us
    pallas_call x1, Pallas kernels, experts_of(): pl.pallas_call(functools.partial(expert_kernel, up_steps=up_steps), grid=...  17.6 us
    all_to_all x2, starting transfers between devices, exchange(): swap(main.reshape(experts, MAIN, width)).reshape(experts * MAIN, width)  12.5 us
    pallas_call x1, Pallas kernels, project(): pl.pallas_call(project_kernel, grid_spec=pltpu.PrefetchScalarGridSpec(num...  9.7 us
    ppermute x1, waiting for transfers between devices, local(): got = lax.ppermute(attn[0], AXES, mirror)  8.71 us
  transfers between devices with their start and end apart: 5, of which 5 were waited for; matrix products, arithmetic and copies ran while one was open for 1% of the time, Pallas kernels for 0%

profile of v1, /device:TPU:9, one launch (start us, length us, event | category | flops | bytes accessed | tf_op | source)
XLA Modules:
  0.0 342.7 jit_solution(1603180383547004982)
XLA Ops:
  6.5 0.0 all-gather.2.cloned.1.call-start
  6.6 0.3 fusion.2
  6.9 0.8 pad_maximum_fusion.1
  7.7 2.2 rotate_all.1
  9.9 0.0 all-gather.2.cloned.1.call-update
  9.9 7.6 %collective-permute-start = (bf16[128,1024]{1,0:T(8,128)(2,1)}, bf16[128,1024]{1,0:T(8,128)(2,1)S(1)}, u32[]{:S(2)}, u32[]{:S(2)}) collective-permute-start(bf16[128,1024]{1,0:T(8,128)(2,1)} %get-tuple-element.15), channel_id=1, source_target_pairs={{0,127},{1,126},{2,125},{3,124},{4,123},{5,122},{6,121},{7,120},{8... | collective-permute-start | bytes 786440 | tf_op jit(solution)/shard_map/ppermute | solution.py:472
  17.5 0.7 pad_add_fusion.meta_ref
  18.1 5.8 %collective-permute-done = bf16[128,1024]{1,0:T(8,128)(2,1)S(1)} collective-permute-done((bf16[128,1024]{1,0:T(8,128)(2,1)}, bf16[128,1024]{1,0:T(8,128)(2,1)S(1)}, u32[]{:S(2)}, u32[]{:S(2)}) %collective-permute-start) | collective-permute-done | bytes 262176 | tf_op jit(solution)/shard_map/ppermute | solution.py:472
  23.9 1.8 pad_maximum_fusion.q_ref
  25.7 67.4 %all-gather.2.cloned.1.call-done = bf16[16384,512]{1,0:T(8,128)(2,1)} async-done(((bf16[128,512]{1,0:T(8,128)(2,1)}), bf16[16384,512]{1,0:T(8,128)(2,1)}) %all-gather.2.cloned.1.call-update) | async-done | bytes 16777232 | tf_op jit(solution)/shard_map/all_gather | solution.py:469
  93.2 39.4 %attend.1 = bf16[2,128,1024]{2,1,0:T(8,128)(2,1)} custom-call(s32[4]{0:T(128)} %pad_add_fusion.meta_ref, bf16[2,128,1024]{2,1,0:T(8,128)(2,1)} %pad_maximum_fusion.q_ref, bf16[4,4,4,2,128,512]{5,4,3,2,1,0:T(8,128)(2,1)} %bitcast.32, bf16[4,4,4,2,128,512]{5,4,3,2,1,0:T(8,128)(2,1)} %bitcast.33), custom_call_target="tpu_custom_call" | custom-call | tf_op jit(solution)/shard_map/attend/pallas_call | solution.py:206
  132.6 1.8 slice_bitcast_fusion
  134.4 3.7 %collective-permute-start.1 = (bf16[128,1024]{1,0:T(8,128)(2,1)S(1)}, bf16[128,1024]{1,0:T(8,128)(2,1)S(1)}, u32[]{:S(2)}, u32[]{:S(2)}) collective-permute-start(bf16[128,1024]{1,0:T(8,128)(2,1)S(1)} %get-tuple-element.25), channel_id=1, source_target_pairs={{0,127},{1,126},{2,125},{3,124},{4,123},{5,122},{6,121},{7,120},{8... | collective-permute-start | bytes 786440 | tf_op jit(solution)/shard_map/ppermute | solution.py:476
  138.0 8.7 %collective-permute-done.1.got_ref = bf16[128,1024]{1,0:T(8,128)(2,1)S(1)} collective-permute-done((bf16[128,1024]{1,0:T(8,128)(2,1)S(1)}, bf16[128,1024]{1,0:T(8,128)(2,1)S(1)}, u32[]{:S(2)}, u32[]{:S(2)}) %collective-permute-start.1) | collective-permute-done | bytes 262176 | tf_op jit(solution)/shard_map/ppermute | solution.py:476
  146.8 0.0 copy-start
  146.8 0.7 copy-done
  147.5 9.7 %project.1 = (bf16[128,2048]{1,0:T(8,128)(2,1)}, f32[128,128]{1,0:T(8,128)}, f32[128,128]{1,0:T(8,128)}, bf16[1024,2048]{1,0:T(8,128)(2,1)}, bf16[128,2048]{1,0:T(8,128)(2,1)}) custom-call(s32[1]{0:T(128)} %bitcast.core_ref, bf16[128,1024]{1,0:T(8,128)(2,1)} %get-tuple-element.26.own_ref, bf16[128,1024]{1,0:T(8,128)(2,1)} %copy-done, ...), custom_call_target="tpu_custom_call" | custom-call | tf_op jit(solution)/shard_map/project/pallas_call | solution.py:295
  157.2 1.1 copy.12
  158.3 19.9 %all_to_all.20 = bf16[128,16,128]{2,1,0:T(8,128)(2,1)S(1)} all-to-all(bf16[128,16,128]{2,1,0:T(8,128)(2,1)S(1)} %bitcast.43), channel_id=1, replica_groups=mesh['zh'=2,'y'=4,'c'=2,'zl'=2,'x'=4] {'zh','y','c','zl','x'}, dimensions={0} | all-to-all | bytes 1048576 | tf_op jit(solution)/shard_map/all_to_all | solution.py:455
  178.2 6.2 %all-to-all-start = ((bf16[128,8,2048]{2,1,0:T(8,128)(2,1)}), bf16[128,8,2048]{2,1,0:T(8,128)(2,1)}, u32[]{:S(2)}, u32[]{:S(2)}) async-start(bf16[128,8,2048]{2,1,0:T(8,128)(2,1)} %bitcast.34), calls=%async_computation | async-start | bytes 8388608 | tf_op jit(solution)/shard_map/all_to_all | solution.py:454
  184.5 0.9 copy.19
  185.4 50.1 %all-to-all-done = bf16[128,8,2048]{2,1,0:T(8,128)(2,1)} async-done(((bf16[128,8,2048]{2,1,0:T(8,128)(2,1)}), bf16[128,8,2048]{2,1,0:T(8,128)(2,1)}, u32[]{:S(2)}, u32[]{:S(2)}) %all-to-all-start) | async-done | bytes 4194336 | tf_op jit(solution)/shard_map/all_to_all | solution.py:454
  235.5 17.6 %experts_of.1 = (bf16[1024,2048]{1,0:T(8,128)(2,1)}, bf16[128,2048]{1,0:T(8,128)(2,1)}) custom-call(bf16[1024,2048]{1,0:T(8,128)(2,1)} %bitcast.12.main_ref, bf16[128,2048]{1,0:T(8,128)(2,1)} %bitcast.39, bf16[2048,768]{1,0:T(8,128)(2,1)} %bitcast.36, bf16[2048,768]{1,0:T(8,128)(2,1)} %bitcast.37, bf16[768,2048]{1,0:T(8,128)(2,1)} %bitcast.38), custom_call_target="tpu_custom_call" | custom-call | tf_op jit(solution)/shard_map/experts_of/pallas_call | solution.py:374
  253.2 1.1 copy.14
  254.3 19.3 %all_to_all.21 = bf16[128,16,128]{2,1,0:T(8,128)(2,1)S(1)} all-to-all(bf16[128,16,128]{2,1,0:T(8,128)(2,1)S(1)} %bitcast.44), channel_id=1, replica_groups=mesh['zh'=2,'y'=4,'c'=2,'zl'=2,'x'=4] {'zh','y','c','zl','x'}, dimensions={0} | all-to-all | bytes 1048576 | tf_op jit(solution)/shard_map/all_to_all | solution.py:455
  273.6 6.2 %all-to-all-start.2 = ((bf16[128,8,2048]{2,1,0:T(8,128)(2,1)}), bf16[128,8,2048]{2,1,0:T(8,128)(2,1)}, u32[]{:S(2)}, u32[]{:S(2)}) async-start(bf16[128,8,2048]{2,1,0:T(8,128)(2,1)} %bitcast.35), calls=%async_computation.2 | async-start | bytes 8388608 | tf_op jit(solution)/shard_map/all_to_all | solution.py:454
  279.9 1.0 copy.18
  280.8 50.1 %all-to-all-done.2 = bf16[128,8,2048]{2,1,0:T(8,128)(2,1)} async-done(((bf16[128,8,2048]{2,1,0:T(8,128)(2,1)}), bf16[128,8,2048]{2,1,0:T(8,128)(2,1)}, u32[]{:S(2)}, u32[]{:S(2)}) %all-to-all-start.2) | async-done | bytes 4194336 | tf_op jit(solution)/shard_map/all_to_all | solution.py:454
  330.9 4.9 %combine.1 = bf16[128,2048]{1,0:T(8,128)(2,1)} custom-call(f32[128,128]{1,0:T(8,128)} %get-tuple-element.18.slot_ref, f32[128,128]{1,0:T(8,128)} %get-tuple-element.19.route_ref, bf16[1024,2048]{1,0:T(8,128)(2,1)} %bitcast.17.main_ref, bf16[128,2048]{1,0:T(8,128)(2,1)} %bitcast.40, bf16[128,2048]{1,0:T(8,128)(2,1)} %get-tuple-element.24.h1_ref), custom_call_target="tpu_custom_call" | custom-call | tf_op jit(solution)/shard_map/combine/pallas_call | solution.py:427
  (2 shorter events, 0.0 us)
Async XLA Ops:
  6.5 86.6 %all-gather.2.cloned.1.call-start = ((), (), s32[]{:S(2)}) async-start(), calls=%async_computation.4 | async-start | bytes 16908288 | tf_op jit(solution)/shard_map/all_gather | solution.py:469
  9.9 14.0 %collective-permute-start = (bf16[128,1024]{1,0:T(8,128)(2,1)}, bf16[128,1024]{1,0:T(8,128)(2,1)S(1)}, u32[]{:S(2)}, u32[]{:S(2)}) collective-permute-start(bf16[128,1024]{1,0:T(8,128)(2,1)} %get-tuple-element.15), channel_id=1, source_target_pairs={{0,127},{1,126},{2,125},{3,124},{4,123},{5,122},{6,121},{7,120},{8... | collective-permute-start | bytes 786440 | tf_op jit(solution)/shard_map/ppermute | solution.py:472
  134.4 12.4 %collective-permute-start.1 = (bf16[128,1024]{1,0:T(8,128)(2,1)S(1)}, bf16[128,1024]{1,0:T(8,128)(2,1)S(1)}, u32[]{:S(2)}, u32[]{:S(2)}) collective-permute-start(bf16[128,1024]{1,0:T(8,128)(2,1)S(1)} %get-tuple-element.25), channel_id=1, source_target_pairs={{0,127},{1,126},{2,125},{3,124},{4,123},{5,122},{6,121},{7,120},{8... | collective-permute-start | bytes 786440 | tf_op jit(solution)/shard_map/ppermute | solution.py:476
  146.8 0.7 copy-start
  178.2 57.3 %all-to-all-start = ((bf16[128,8,2048]{2,1,0:T(8,128)(2,1)}), bf16[128,8,2048]{2,1,0:T(8,128)(2,1)}, u32[]{:S(2)}, u32[]{:S(2)}) async-start(bf16[128,8,2048]{2,1,0:T(8,128)(2,1)} %bitcast.34), calls=%async_computation | async-start | bytes 8388608 | tf_op jit(solution)/shard_map/all_to_all | solution.py:454
  273.6 57.3 %all-to-all-start.2 = ((bf16[128,8,2048]{2,1,0:T(8,128)(2,1)}), bf16[128,8,2048]{2,1,0:T(8,128)(2,1)}, u32[]{:S(2)}, u32[]{:S(2)}) async-start(bf16[128,8,2048]{2,1,0:T(8,128)(2,1)} %bitcast.35), calls=%async_computation.2 | async-start | bytes 8388608 | tf_op jit(solution)/shard_map/all_to_all | solution.py:454
Sparse Core Ops, SparseCore 0:
  10.5 82.6 all-gather.1

commit v2 on v1

v2 whole, which is shorter than its diff:
```python
import functools
import math

import jax
import jax.numpy as jnp
from jax import lax
from jax.experimental import pallas as pl
from jax.experimental.pallas import tpu as pltpu
from jax.sharding import Mesh, PartitionSpec as P

DH = 128
TOP = 8
CAP = 9
MAIN = 8
BLOCK = 128
BLOCKS = 128
CHUNK_BLOCKS = 8
TILE_HEADS = 4
AXES = ("zh", "y", "c", "zl", "x")
TORUS = ("zh", "zl", "y", "x", "c")

rope_base = 1000000.0
yarn_factor = 4.0
orig_len = 32768.0
beta_fast = 32.0
beta_slow = 1.0
mscale_yarn = 0.1 * math.log(4.0) + 1.0

F32 = jnp.float32
BF16 = jnp.bfloat16
VMEM_LIMIT = 60 * 1024 * 1024


def params(*semantics):
    return pltpu.CompilerParams(
        dimension_semantics=semantics, vmem_limit_bytes=VMEM_LIMIT
    )


def yarn_tables(positions, head_size):
    half_size = head_size // 2
    index_f = jnp.arange(half_size, dtype=jnp.float32)
    pos_freq = rope_base ** (2.0 * index_f / head_size)
    inv_extra = 1.0 / pos_freq
    inv_inter = 1.0 / (yarn_factor * pos_freq)
    low_dim = max(
        math.floor(
            head_size
            * math.log(orig_len / (beta_fast * 2.0 * math.pi))
            / (2.0 * math.log(rope_base))
        ),
        0,
    )
    high_dim = min(
        math.ceil(
            head_size
            * math.log(orig_len / (beta_slow * 2.0 * math.pi))
            / (2.0 * math.log(rope_base))
        ),
        head_size - 1,
    )
    ramp_part = jnp.clip((index_f - low_dim) / max(high_dim - low_dim, 0.001), 0.0, 1.0)
    extra_part = 1.0 - ramp_part
    inverse = inv_inter * (1.0 - extra_part) + inv_extra * extra_part
    angles = positions.astype(jnp.float32)[:, None] * inverse[None, :]
    cos_half = jnp.cos(angles) * mscale_yarn
    sin_half = jnp.sin(angles) * mscale_yarn
    return (
        jnp.concatenate([cos_half, cos_half], axis=-1),
        jnp.concatenate([-sin_half, sin_half], axis=-1),
    )


def rotate_kernel(core_ref, q_ref, k_ref, v_ref, cos_ref, sin_ref, keep_ref, give_ref, kv_ref):
    core = core_ref[0]
    cos_t = cos_ref[...]
    sin_t = sin_ref[...]

    def rotated(part):
        value = part.astype(F32)
        return (value * cos_t + pltpu.roll(value, DH // 2, 1) * sin_t).astype(BF16)

    for head in range(2):
        columns = pl.ds(head * DH, DH)
        kv_ref[:, columns] = rotated(k_ref[:, columns])
    kv_ref[:, pl.ds(2 * DH, 2 * DH)] = v_ref[...]
    half = keep_ref.shape[1]
    for out_ref, which in ((keep_ref, core), (give_ref, 1 - core)):
        for head in range(half // DH):
            source = pl.ds(pl.multiple_of(which * half + head * DH, DH), DH)
            out_ref[:, pl.ds(head * DH, DH)] = rotated(q_ref[:, source])


def rotate_all(core, queries, keys, values, cos_t, sin_t):
    rows, width = queries.shape
    vmem = pl.BlockSpec(memory_space=pltpu.VMEM)
    return pl.pallas_call(
        rotate_kernel,
        in_specs=[pl.BlockSpec(memory_space=pltpu.SMEM)] + [vmem] * 5,
        out_specs=[vmem] * 3,
        out_shape=[
            jax.ShapeDtypeStruct((rows, width // 2), BF16),
            jax.ShapeDtypeStruct((rows, width // 2), BF16),
            jax.ShapeDtypeStruct((rows, 4 * DH), BF16),
        ],
        compiler_params=params(),
        name="rotate_all",
    )(core, queries, keys, values, cos_t, sin_t)


def attend_kernel(
    meta_ref, theirs_ref, own_ref, k_ref, v_ref, theirs_out_ref, own_out_ref,
    q_ref, max_ref, sum_ref, acc_ref, *, heads, tile_heads
):
    step = pl.program_id(0)
    second = step >= meta_ref[2]
    chunk = jnp.where(second, step - meta_ref[2], step)
    block = jnp.where(second, meta_ref[1], meta_ref[0])
    diagonal = block // CHUNK_BLOCKS
    keys_len = CHUNK_BLOCKS * BLOCK
    factor = math.log2(math.e) / math.sqrt(DH)
    rows = tile_heads * BLOCK
    parts = heads // tile_heads

    @pl.when(chunk == 0)
    def _():
        max_ref[...] = jnp.full_like(max_ref, -1e30)
        sum_ref[...] = jnp.zeros_like(sum_ref)
        acc_ref[...] = jnp.zeros_like(acc_ref)

    @pl.when(step == 0)
    def _():
        q_ref[...] = theirs_ref[...]

    @pl.when(step == meta_ref[2])
    def _():
        q_ref[...] = own_ref[...]

    def update(masked):
        keys = k_ref[...].reshape(keys_len, DH)
        vals = v_ref[...].reshape(keys_len, DH)
        if masked:
            offset = (block - chunk * CHUNK_BLOCKS) * BLOCK
            row_token = lax.broadcasted_iota(jnp.int32, (BLOCK, keys_len), 0) + offset
            key_token = lax.broadcasted_iota(jnp.int32, (BLOCK, keys_len), 1)
            allowed = key_token <= row_token

        def scores_of(part):
            query = jnp.concatenate(
                [q_ref[:, pl.ds((part * tile_heads + h) * DH, DH)] for h in range(tile_heads)],
                axis=0,
            )
            scores = lax.dot_general(
                query, keys, (((1,), (1,)), ((), ())), preferred_element_type=F32
            )
            if masked:
                scores = jnp.where(
                    allowed[None], scores.reshape(tile_heads, BLOCK, keys_len), -1e30
                ).reshape(rows, keys_len)
            return scores

        def absorb(part, scores):
            span = pl.ds(part * rows, rows)
            old_max = max_ref[span, :]
            new_max = jnp.maximum(old_max, jnp.max(scores, axis=1, keepdims=True))
            decay = jnp.exp2((old_max - new_max) * factor)
            lane_sum = sum_ref[span, :] * decay
            weights = []
            for column in range(keys_len // DH):
                piece = jnp.exp2((scores[:, column * DH : (column + 1) * DH] - new_max) * factor)
                lane_sum = lane_sum + piece
                weights.append(piece.astype(BF16))
            sum_ref[span, :] = lane_sum
            max_ref[span, :] = new_max
            added = jnp.dot(jnp.concatenate(weights, axis=1), vals, preferred_element_type=F32)
            acc_ref[span, :] = acc_ref[span, :] * decay + added

        scores = scores_of(0)
        for part in range(parts):
            later = scores_of(part + 1) if part + 1 < parts else None
            absorb(part, scores)
            scores = later

    @pl.when(chunk == diagonal)
    def _():
        update(True)

        def store(out_ref):
            for head in range(heads):
                span = pl.ds(head * BLOCK, BLOCK)
                total = jnp.sum(sum_ref[span, :], axis=1, keepdims=True)
                out_ref[:, pl.ds(head * DH, DH)] = (acc_ref[span, :] / total).astype(BF16)

        pl.when(second)(lambda: store(own_out_ref))
        pl.when(jnp.logical_not(second))(lambda: store(theirs_out_ref))

    @pl.when(chunk != diagonal)
    def _():
        update(False)


def attend(meta, theirs, own, gathered, tile_heads=TILE_HEADS):
    rows, width = own.shape
    heads = width // DH
    steps = BLOCKS // CHUNK_BLOCKS + 1

    def key_map(column):
        def index(step, meta_ref):
            chunk = jnp.where(step >= meta_ref[2], step - meta_ref[2], step)
            return chunk // 8, (chunk // 2) % 4, 0, chunk % 2, 0, 2 * column + meta_ref[3]

        return index

    def whole(step, meta_ref):
        return 0, 0

    piece = (2, 1, 4, 1, BLOCK, DH)
    return pl.pallas_call(
        functools.partial(attend_kernel, heads=heads, tile_heads=tile_heads),
        grid_spec=pltpu.PrefetchScalarGridSpec(
            num_scalar_prefetch=1,
            grid=(steps,),
            in_specs=[
                pl.BlockSpec((rows, width), whole),
                pl.BlockSpec((rows, width), whole),
                pl.BlockSpec(piece, key_map(0)),
                pl.BlockSpec(piece, key_map(1)),
            ],
            out_specs=[pl.BlockSpec((rows, width), whole)] * 2,
            scratch_shapes=[pltpu.VMEM((rows, width), BF16)]
            + [pltpu.VMEM((heads * rows, DH), F32)] * 3,
        ),
        out_shape=[jax.ShapeDtypeStruct((rows, width), BF16)] * 2,
        compiler_params=params("arbitrary"),
        name="attend",
    )(meta, theirs, own, gathered, gathered)


def slots_of(ids_ref):
    shape = (BLOCK, BLOCK)
    expert = lax.broadcasted_iota(jnp.int32, shape, 0)
    named = jnp.zeros(shape, F32)
    for k in range(TOP):
        named = named + jnp.where(ids_ref[k : k + 1, :] == expert, 1.0, 0.0)
    earlier = jnp.where(
        lax.broadcasted_iota(jnp.int32, shape, 0) < lax.broadcasted_iota(jnp.int32, shape, 1),
        1.0,
        0.0,
    )
    counts = jnp.dot(named.astype(BF16), earlier.astype(BF16), preferred_element_type=F32)
    return named, jnp.where(named > 0.0, counts, -1.0)


def own_kernel(core_ref, own_ref, w_ref, out_ref):
    @pl.when(pl.program_id(0) == 0)
    def _():
        out_ref[...] = jnp.zeros_like(out_ref)

    depth = w_ref.shape[0]
    column = pl.ds(pl.multiple_of(pl.program_id(0) * depth, depth), depth)
    out_ref[...] += jnp.dot(own_ref[:, column], w_ref[...], preferred_element_type=F32)


def project_own(core, own, w_out, depth=512):
    rows, half = own.shape
    width = w_out.shape[1]
    steps = half // depth
    return pl.pallas_call(
        own_kernel,
        grid_spec=pltpu.PrefetchScalarGridSpec(
            num_scalar_prefetch=1,
            grid=(steps,),
            in_specs=[
                pl.BlockSpec((rows, half), lambda step, core_ref: (0, 0)),
                pl.BlockSpec((depth, width), lambda step, core_ref: (core_ref[0] * steps + step, 0)),
            ],
            out_specs=pl.BlockSpec((rows, width), lambda step, core_ref: (0, 0)),
        ),
        out_shape=jax.ShapeDtypeStruct((rows, width), F32),
        compiler_params=params("arbitrary"),
        cost_estimate=pl.CostEstimate(
            flops=2 * rows * half * width, bytes_accessed=2 * half * width, transcendentals=0
        ),
        name="project_own",
    )(core, own, w_out)


def project_kernel(
    core_ref, part_ref, got_ref, w_ref, hidden_ref, gain_ref, router_ref, ids_ref,
    h1_ref, slot_ref, route_ref, send_ref, acc_ref, over_ref,
):
    step = pl.program_id(0)
    depth = w_ref.shape[0]

    @pl.when(step == 0)
    def _():
        acc_ref[...] = part_ref[...] + hidden_ref[...].astype(F32)

    column = pl.ds(pl.multiple_of(step * depth, depth), depth)
    acc_ref[...] += jnp.dot(got_ref[:, column], w_ref[...], preferred_element_type=F32)

    @pl.when(step == pl.num_programs(0) - 1)
    def _():
        h1 = acc_ref[...].astype(BF16)
        h1_ref[...] = h1
        h1_f = h1.astype(F32)
        mean = jnp.mean(h1_f * h1_f, axis=-1, keepdims=True)
        hn = (h1_f / jnp.sqrt(mean + 1e-06) * gain_ref[...]).astype(BF16)
        logits = jnp.dot(hn, router_ref[...], preferred_element_type=F32)
        named, slot = slots_of(ids_ref)
        slot_ref[...] = slot
        raised = jnp.where(named > 0.0, jnp.exp(jnp.transpose(logits)), 0.0)
        route_ref[...] = raised / jnp.sum(raised, axis=0, keepdims=True)
        wanted = lax.broadcasted_iota(jnp.int32, (BLOCK, MAIN, BLOCK), 1).astype(F32)
        pick = jnp.where(slot[:, None, :] == wanted, 1.0, 0.0).reshape(BLOCK * MAIN, BLOCK)
        pick = pick.astype(BF16)
        last = jnp.where(slot == float(MAIN), 1.0, 0.0).astype(BF16)
        tiles = hn.shape[1] // DH
        for tile in range(tiles):
            part = hn[:, tile * DH : (tile + 1) * DH]
            rows = jnp.dot(pick, part, preferred_element_type=F32)
            send_ref[:, tile * MAIN : (tile + 1) * MAIN, :] = rows.reshape(
                BLOCK, MAIN, DH
            ).astype(BF16)
            over_ref[:, tile, :] = jnp.dot(last, part, preferred_element_type=F32)
        send_ref[:, tiles * MAIN :, :] = over_ref[...].astype(BF16)


def project(core, part, got, w_out, hidden, gain, w_router, ids_t, depth=512):
    rows, half = got.shape
    width = hidden.shape[1]
    steps = half // depth

    def full(shape):
        return pl.BlockSpec(shape, lambda step, core_ref: (0,) * len(shape))

    experts = w_router.shape[1]
    packed = (experts, CAP * width // DH, DH)
    return pl.pallas_call(
        project_kernel,
        grid_spec=pltpu.PrefetchScalarGridSpec(
            num_scalar_prefetch=1,
            grid=(steps,),
            in_specs=[
                full((rows, width)),
                full((rows, half)),
                pl.BlockSpec(
                    (depth, width), lambda step, core_ref: ((1 - core_ref[0]) * steps + step, 0)
                ),
                full((rows, width)),
                full((1, width)),
                full((width, experts)),
                full((TOP, rows)),
            ],
            out_specs=[
                full((rows, width)),
                full((experts, rows)),
                full((experts, rows)),
                full(packed),
            ],
            scratch_shapes=[
                pltpu.VMEM((rows, width), F32),
                pltpu.VMEM((experts, width // DH, DH), F32),
            ],
        ),
        out_shape=[
            jax.ShapeDtypeStruct((rows, width), BF16),
            jax.ShapeDtypeStruct((experts, rows), F32),
            jax.ShapeDtypeStruct((experts, rows), F32),
            jax.ShapeDtypeStruct(packed, BF16),
        ],
        compiler_params=params("arbitrary"),
        name="project",
    )(core, part, got, w_out, hidden, gain, w_router, ids_t)


def expert_kernel(in_ref, gate_ref, up_ref, down_ref, out_ref, rows_ref, act_ref, over_ref, *, up_steps):
    step = pl.program_id(0)
    tile = gate_ref.shape[1]
    sources = in_ref.shape[0]
    main_rows = sources * MAIN
    width = gate_ref.shape[0]
    tiles = width // DH

    @pl.when(step == 0)
    def _():
        over_ref[...] = in_ref[:, tiles * MAIN :, :].astype(F32)
        for place in range(tiles):
            columns = pl.ds(place * DH, DH)
            rows_ref[:main_rows, columns] = in_ref[:, place * MAIN : (place + 1) * MAIN, :].reshape(
                main_rows, DH
            )
            rows_ref[main_rows:, columns] = over_ref[:, place, :].astype(BF16)

    half = main_rows // 2
    spans = [(0, half), (half, half), (main_rows, sources)]
    for index in range(up_steps):

        @pl.when(step == index)
        def _(index=index):
            for start, size in spans:
                rows = rows_ref[start : start + size, :]
                gate = jnp.dot(rows, gate_ref[...], preferred_element_type=F32)
                up = jnp.dot(rows, up_ref[...], preferred_element_type=F32)
                act = gate / (1.0 + jnp.exp(-gate)) * up
                act_ref[start : start + size, index * tile : (index + 1) * tile] = act.astype(BF16)

    columns = down_ref.shape[1]
    for index in range(width // columns):

        @pl.when(step == up_steps + index)
        def _(index=index):
            first = index * columns // DH
            for start, size in spans:
                rows = jnp.dot(
                    act_ref[start : start + size, :], down_ref[...], preferred_element_type=F32
                )
                for place in range(columns // DH):
                    piece = rows[:, place * DH : (place + 1) * DH]
                    if start < main_rows:
                        some = pl.ds(start // MAIN, size // MAIN)
                        out_ref[some, (first + place) * MAIN : (first + place + 1) * MAIN, :] = (
                            piece.reshape(size // MAIN, MAIN, DH).astype(BF16)
                        )
                    else:
                        over_ref[:, first + place, :] = piece
            if index == width // columns - 1:
                out_ref[:, tiles * MAIN :, :] = over_ref[...].astype(BF16)


def experts_of(packed, w_gate, w_up, w_down):
    sources = packed.shape[0]
    width, hidden_units = w_gate.shape
    tile = 256
    columns = 512
    up_steps = hidden_units // tile
    steps = up_steps + width // columns
    rows = sources * CAP

    def up_map(step):
        return 0, jnp.minimum(step, up_steps - 1)

    def down_map(step):
        return 0, jnp.maximum(step - up_steps, 0)

    def whole(step):
        return 0, 0, 0

    return pl.pallas_call(
        functools.partial(expert_kernel, up_steps=up_steps),
        grid=(steps,),
        in_specs=[
            pl.BlockSpec(packed.shape, whole),
            pl.BlockSpec((width, tile), up_map),
            pl.BlockSpec((width, tile), up_map),
            pl.BlockSpec((hidden_units, columns), down_map),
        ],
        out_specs=pl.BlockSpec(packed.shape, whole),
        out_shape=jax.ShapeDtypeStruct(packed.shape, BF16),
        scratch_shapes=[
            pltpu.VMEM((rows, width), BF16),
            pltpu.VMEM((rows, hidden_units), BF16),
            pltpu.VMEM((sources, width // DH, DH), F32),
        ],
        compiler_params=params("arbitrary"),
        name="experts_of",
    )(packed, w_gate, w_up, w_down)


def combine_kernel(slot_ref, route_ref, in_ref, h1_ref, out_ref, over_ref):
    slot = slot_ref[...]
    route = route_ref[...]
    wanted = lax.broadcasted_iota(jnp.int32, (BLOCK, MAIN, BLOCK), 1).astype(F32)
    mix = jnp.where(slot[:, None, :] == wanted, route[:, None, :], 0.0)
    mix = mix.reshape(BLOCK * MAIN, BLOCK).astype(BF16)
    last = jnp.where(slot == float(MAIN), route, 0.0).astype(BF16)
    tiles = h1_ref.shape[1] // DH
    over_ref[...] = in_ref[:, tiles * MAIN :, :].astype(F32)

    def mixed(weights, rows):
        return lax.dot_general(
            weights, rows, (((0,), (0,)), ((), ())), preferred_element_type=F32
        )

    per = 2
    for place in range(0, tiles, per):
        columns = pl.ds(place * DH, per * DH)
        spots = range(place, place + per)
        rows = jnp.concatenate(
            [
                in_ref[:, p * MAIN : (p + 1) * MAIN, :].reshape(BLOCK * MAIN, DH)
                for p in spots
            ],
            axis=1,
        )
        extra = jnp.concatenate([over_ref[:, p, :].astype(BF16) for p in spots], axis=1)
        total = mixed(mix, rows) + mixed(last, extra)
        out_ref[:, columns] = (total + h1_ref[:, columns].astype(F32)).astype(BF16)


def combine(slot, route, packed, h1):
    vmem = pl.BlockSpec(memory_space=pltpu.VMEM)
    return pl.pallas_call(
        combine_kernel,
        in_specs=[vmem] * 4,
        out_specs=vmem,
        out_shape=jax.ShapeDtypeStruct(h1.shape, BF16),
        scratch_shapes=[pltpu.VMEM((packed.shape[0], h1.shape[1] // DH, DH), F32)],
        compiler_params=params(),
        name="combine",
    )(slot, route, packed, h1)


def exchange(packed):
    return lax.all_to_all(packed, AXES, split_axis=0, concat_axis=0, tiled=True)


def local(
    hidden, queries, keys, values, w_out, norm_gain, w_router, expert_ids, w_gate, w_up, w_down
):
    rows = hidden.shape[0]
    device = lax.axis_index(AXES)
    core = lax.axis_index("c")
    positions = device * rows + jnp.arange(rows, dtype=jnp.int32)
    cos_t, sin_t = yarn_tables(positions, DH)
    core_arr = core.reshape(1).astype(jnp.int32)
    keep, give, kv = rotate_all(core_arr, queries, keys, values, cos_t, sin_t)
    gathered = lax.all_gather(kv, TORUS, axis=0, tiled=True)
    gathered = gathered.reshape(4, 4, 4, 2, BLOCK, 4 * DH)
    mirror = [(i, BLOCKS - 1 - i) for i in range(BLOCKS)]
    taken = lax.ppermute(give, AXES, mirror)
    other = BLOCKS - 1 - device
    meta = jnp.stack([other, device, other // CHUNK_BLOCKS + 1, core]).astype(jnp.int32)
    theirs, own = attend(meta, taken, keep, gathered)
    got = lax.ppermute(theirs, AXES, mirror)
    part = project_own(core_arr, own, w_out)
    h1, slot, route, send = project(
        core_arr, part, got, w_out, hidden, norm_gain[None, :], w_router, expert_ids.T
    )
    returned = exchange(experts_of(exchange(send), w_gate[0], w_up[0], w_down[0]))
    return combine(slot, route, returned, h1)


def solution(mesh):
    torus = Mesh(mesh.devices.reshape(2, 4, 2, 2, 4), AXES)
    split = P(AXES, None)
    experts = P(AXES, None, None)
    in_specs = (
        split, split, split, split, P(), P(), P(), split, experts, experts, experts,
    )
    return jax.shard_map(
        local, mesh=torus, in_specs=in_specs, out_specs=split, check_vma=False
    )
```

time: 345 us -> 307 us (0.89)
  waiting for transfers between devices: 182 us -> 80.2 us
  blocking collectives: 39.2 us -> 129 us
  starting transfers between devices: 23.8 us -> 11.2 us
  local copies, waits for them, and re-layouts: 6.66 us -> 0.71 us
  Pallas kernels: 73.9 us -> 69.2 us
    all_to_all x2 -> x0, waiting for transfers between devices: 100 us -> none  [exchange(): swap(main.reshape(experts, MAIN, width)).reshape(experts * MAIN, width)]
    all_to_all x2, blocking collectives: 39.2 us -> 129 us  [exchange(): return lax.all_to_all(packed, AXES, split_axis=0, concat_axis=0, tiled=True)]
    all_to_all x2 -> x0, starting transfers between devices: 12.5 us -> none  [exchange(): swap(main.reshape(experts, MAIN, width)).reshape(experts * MAIN, width)]
    pallas_call x1, Pallas kernels: 39.4 us -> 30.3 us  [attend(): pl.pallas_call(functools.partial(attend_kernel, heads=heads, tile_heads=t...]
    unnamed x6 -> x4, local copies, waits for them, and re-layouts: 4.89 us -> 0.71 us
    pallas_call x1 -> x2, Pallas kernels: 4.91 us -> 8.86 us  [the longest x1 5.11 us: combine(): pl.pallas_call(combine_kernel, in_specs=[vmem] * 4, out_specs=vmem, out_s...]
    ppermute x1, waiting for transfers between devices: 8.71 us -> 5.17 us  [local(): got = lax.ppermute(theirs, AXES, mirror)]
  transfers between devices with their start and end apart: 5 -> 3, of which waited for: 5 -> 3; matrix products, arithmetic and copies ran while one was open for 1% -> 0% of each run, Pallas kernels for 0% -> 1%
where the time goes in v2:
time: 307 us; the launch traced here: 306 us
  blocking collectives  129 us (42%)
  waiting for transfers between devices  80.2 us (26%)
  Pallas kernels  69.2 us (23%)
  between operations  13.4 us (4%)
  starting transfers between devices  11.2 us (4%)
    all_to_all x2, blocking collectives, exchange(): return lax.all_to_all(packed, AXES, split_axis=0, concat_axis=0, tiled=True)  129 us
    all_gather x1, waiting for transfers between devices, local(): gathered = lax.all_gather(kv, TORUS, axis=0, tiled=True)  69.3 us
    pallas_call x1, Pallas kernels, attend(): pl.pallas_call(functools.partial(attend_kernel, heads=heads, tile_heads=t...  30.3 us
    pallas_call x1, Pallas kernels, experts_of(): pl.pallas_call(functools.partial(expert_kernel, up_steps=up_steps), grid=...  20.1 us
    pallas_call x1, Pallas kernels, project(): pl.pallas_call(project_kernel, grid_spec=pltpu.PrefetchScalarGridSpec(num...  7.8 us
    ppermute x1, starting transfers between devices, local(): taken = lax.ppermute(give, AXES, mirror)  7.6 us
  transfers between devices with their start and end apart: 3, of which 3 were waited for; matrix products, arithmetic and copies ran while one was open for 0% of the time, Pallas kernels for 1%

profile of v2, /device:TPU:9, one launch (start us, length us, event | category | flops | bytes accessed | tf_op | source)
XLA Modules:
  0.0 305.8 jit_solution(14551859257921352550)
XLA Ops:
  6.5 0.0 all-gather.2.cloned.1.call-start
  6.6 0.3 fusion.2
  6.9 0.7 pad_maximum_fusion
  7.6 2.2 rotate_all.1
  9.8 0.0 all-gather.2.cloned.1.call-update
  9.8 7.6 %collective-permute-start = (bf16[128,1024]{1,0:T(8,128)(2,1)}, bf16[128,1024]{1,0:T(8,128)(2,1)S(1)}, u32[]{:S(2)}, u32[]{:S(2)}) collective-permute-start(bf16[128,1024]{1,0:T(8,128)(2,1)} %get-tuple-element.14), channel_id=1, source_target_pairs={{0,127},{1,126},{2,125},{3,124},{4,123},{5,122},{6,121},{7,120},{8... | collective-permute-start | bytes 786440 | tf_op jit(solution)/shard_map/ppermute | solution.py:531
  17.4 0.7 pad_add_fusion.meta_ref
  18.1 5.8 %collective-permute-done.theirs_ref = bf16[128,1024]{1,0:T(8,128)(2,1)S(1)} collective-permute-done((bf16[128,1024]{1,0:T(8,128)(2,1)}, bf16[128,1024]{1,0:T(8,128)(2,1)S(1)}, u32[]{:S(2)}, u32[]{:S(2)}) %collective-permute-start) | collective-permute-done | bytes 262176 | tf_op jit(solution)/shard_map/ppermute | solution.py:531
  23.9 0.0 copy-start
  23.9 69.3 %all-gather.2.cloned.1.call-done = bf16[16384,512]{1,0:T(8,128)(2,1)} async-done(((bf16[128,512]{1,0:T(8,128)(2,1)}), bf16[16384,512]{1,0:T(8,128)(2,1)}) %all-gather.2.cloned.1.call-update) | async-done | bytes 16777232 | tf_op jit(solution)/shard_map/all_gather | solution.py:528
  93.2 0.0 copy-done
  93.2 30.3 %attend.1 = (bf16[128,1024]{1,0:T(8,128)(2,1)}, bf16[128,1024]{1,0:T(8,128)(2,1)}) custom-call(s32[4]{0:T(128)} %pad_add_fusion.meta_ref, bf16[128,1024]{1,0:T(8,128)(2,1)} %copy-done, bf16[128,1024]{1,0:T(8,128)(2,1)} %get-tuple-element.15.own_ref, bf16[4,4,4,2,128,512]{5,4,3,2,1,0:T(8,128)(2,1)} %bitcast.10, bf16[4,4,4,2,128,512]{5,4,3,2,1,0:T(8,128)(2,1)} %bitcast.11), custom_call_target="tpu_custom_call" | custom-call | tf_op jit(solution)/shard_map/attend/pallas_call | solution.py:218
  123.5 3.6 %collective-permute-start.1 = (bf16[128,1024]{1,0:T(8,128)(2,1)}, bf16[128,1024]{1,0:T(8,128)(2,1)S(1)}, u32[]{:S(2)}, u32[]{:S(2)}) collective-permute-start(bf16[128,1024]{1,0:T(8,128)(2,1)} %get-tuple-element.18), channel_id=1, source_target_pairs={{0,127},{1,126},{2,125},{3,124},{4,123},{5,122},{6,121},{7,120},{8... | collective-permute-start | bytes 786440 | tf_op jit(solution)/shard_map/ppermute | solution.py:535
  127.1 3.8 %project_own.1.part_ref = f32[128,2048]{1,0:T(8,128)} custom-call(s32[1]{0:T(128)} %bitcast.core_ref, bf16[128,1024]{1,0:T(8,128)(2,1)} %get-tuple-element.17.own_ref, bf16[2048,2048]{1,0:T(8,128)(2,1)} %w_ref.3), custom_call_target="tpu_custom_call" | custom-call | flops 536870912 | bytes 4194304 | tf_op jit(solution)/shard_map/project_own/pallas_call | solution.py:268
  130.9 5.2 %collective-permute-done.1.got_ref = bf16[128,1024]{1,0:T(8,128)(2,1)S(1)} collective-permute-done((bf16[128,1024]{1,0:T(8,128)(2,1)}, bf16[128,1024]{1,0:T(8,128)(2,1)S(1)}, u32[]{:S(2)}, u32[]{:S(2)}) %collective-permute-start.1) | collective-permute-done | bytes 262176 | tf_op jit(solution)/shard_map/ppermute | solution.py:535
  136.0 0.0 copy-start.1
  136.0 0.7 copy-done.1
  136.7 7.8 %project.1 = (bf16[128,2048]{1,0:T(8,128)(2,1)}, f32[128,128]{1,0:T(8,128)}, f32[128,128]{1,0:T(8,128)}, bf16[128,144,128]{2,1,0:T(8,128)(2,1)}) custom-call(s32[1]{0:T(128)} %bitcast.core_ref, f32[128,2048]{1,0:T(8,128)} %project_own.1.part_ref, bf16[128,1024]{1,0:T(8,128)(2,1)} %copy-done.1, bf16[2048,2048]{1,0:T(8,128)(2,1)} %w_ref.3, ...), custom_call_target="tpu_custom_call" | custom-call | tf_op jit(solution)/shard_map/project/pallas_call | solution.py:339
  144.5 65.2 %all_to_all.10.in_ref = bf16[128,144,128]{2,1,0:T(8,128)(2,1)} all-to-all(bf16[128,144,128]{2,1,0:T(8,128)(2,1)} %get-tuple-element.21), channel_id=1, replica_groups=mesh['zh'=2,'y'=4,'c'=2,'zl'=2,'x'=4] {'zh','y','c','zl','x'}, dimensions={0} | all-to-all | bytes 9437184 | tf_op jit(solution)/shard_map/all_to_all | solution.py:515
  209.7 20.1 %experts_of.1 = bf16[128,144,128]{2,1,0:T(8,128)(2,1)} custom-call(bf16[128,144,128]{2,1,0:T(8,128)(2,1)} %all_to_all.10.in_ref, bf16[2048,768]{1,0:T(8,128)(2,1)} %bitcast.12, bf16[2048,768]{1,0:T(8,128)(2,1)} %bitcast.13, bf16[768,2048]{1,0:T(8,128)(2,1)} %bitcast.14), custom_call_target="tpu_custom_call" | custom-call | tf_op jit(solution)/shard_map/experts_of/pallas_call | solution.py:449
  229.8 64.0 %all_to_all.11.in_ref = bf16[128,144,128]{2,1,0:T(8,128)(2,1)} all-to-all(bf16[128,144,128]{2,1,0:T(8,128)(2,1)} %experts_of.1), channel_id=1, replica_groups=mesh['zh'=2,'y'=4,'c'=2,'zl'=2,'x'=4] {'zh','y','c','zl','x'}, dimensions={0} | all-to-all | bytes 9437184 | tf_op jit(solution)/shard_map/all_to_all | solution.py:515
  293.8 5.1 %combine.1 = bf16[128,2048]{1,0:T(8,128)(2,1)} custom-call(f32[128,128]{1,0:T(8,128)} %get-tuple-element.19.slot_ref, f32[128,128]{1,0:T(8,128)} %get-tuple-element.20.route_ref, bf16[128,144,128]{2,1,0:T(8,128)(2,1)} %all_to_all.11.in_ref, bf16[128,2048]{1,0:T(8,128)(2,1)} %get-tuple-element.22.h1_ref), custom_call_target="tpu_custom_call" | custom-call | tf_op jit(solution)/shard_map/combine/pallas_call | solution.py:503
  (2 shorter events, 0.0 us)
Async XLA Ops:
  6.5 86.6 %all-gather.2.cloned.1.call-start = ((), (), s32[]{:S(2)}) async-start(), calls=%async_computation.2 | async-start | bytes 16908288 | tf_op jit(solution)/shard_map/all_gather | solution.py:528
  9.8 14.0 %collective-permute-start = (bf16[128,1024]{1,0:T(8,128)(2,1)}, bf16[128,1024]{1,0:T(8,128)(2,1)S(1)}, u32[]{:S(2)}, u32[]{:S(2)}) collective-permute-start(bf16[128,1024]{1,0:T(8,128)(2,1)} %get-tuple-element.14), channel_id=1, source_target_pairs={{0,127},{1,126},{2,125},{3,124},{4,123},{5,122},{6,121},{7,120},{8... | collective-permute-start | bytes 786440 | tf_op jit(solution)/shard_map/ppermute | solution.py:531
  23.9 69.3 %copy-start = (bf16[128,1024]{1,0:T(8,128)(2,1)}, bf16[128,1024]{1,0:T(8,128)(2,1)S(1)}, u32[]{:S(2)}) copy-start(bf16[128,1024]{1,0:T(8,128)(2,1)S(1)} %collective-permute-done.theirs_ref) | copy-start | bytes 786436
  123.5 12.6 %collective-permute-start.1 = (bf16[128,1024]{1,0:T(8,128)(2,1)}, bf16[128,1024]{1,0:T(8,128)(2,1)S(1)}, u32[]{:S(2)}, u32[]{:S(2)}) collective-permute-start(bf16[128,1024]{1,0:T(8,128)(2,1)} %get-tuple-element.18), channel_id=1, source_target_pairs={{0,127},{1,126},{2,125},{3,124},{4,123},{5,122},{6,121},{7,120},{8... | collective-permute-start | bytes 786440 | tf_op jit(solution)/shard_map/ppermute | solution.py:535
  136.0 0.7 copy-start.1
Sparse Core Ops, SparseCore 0:
  10.5 82.6 all-gather.1

commit v3 on v2

--- a/solution.py
+++ b/solution.py
@@ -8,16 +8,20 @@
 from jax.experimental.pallas import tpu as pltpu
 from jax.sharding import Mesh, PartitionSpec as P
 
+
 DH = 128
 TOP = 8
 CAP = 9
 MAIN = 8
 BLOCK = 128
 BLOCKS = 128
-CHUNK_BLOCKS = 8
+UNIT = 4
+FAR = 1 << 20
 TILE_HEADS = 4
 AXES = ("zh", "y", "c", "zl", "x")
-TORUS = ("zh", "zl", "y", "x", "c")
+RING_Z = ("zh", "zl")
+RING_Y = ("y",)
+OFFSETS = (0, -1, 1, 2)
 
 rope_base = 1000000.0
 yarn_factor = 4.0
@@ -25,6 +29,7 @@
 beta_fast = 32.0
 beta_slow = 1.0
 mscale_yarn = 0.1 * math.log(4.0) + 1.0
+
 
 F32 = jnp.float32
 BF16 = jnp.bfloat16
@@ -71,7 +76,9 @@
     )
 
 
-def rotate_kernel(core_ref, q_ref, k_ref, v_ref, cos_ref, sin_ref, keep_ref, give_ref, kv_ref):
+def rotate_kernel(
+    core_ref, q_ref, k_ref, v_ref, cos_ref, sin_ref, keep_ref, give_ref, keep_kv_ref, give_kv_ref
+):
     core = core_ref[0]
     cos_t = cos_ref[...]
     sin_t = sin_ref[...]
@@ -80,15 +87,17 @@
         value = part.astype(F32)
         return (value * cos_t + pltpu.roll(value, DH // 2, 1) * sin_t).astype(BF16)
 
-    for head in range(2):
-        columns = pl.ds(head * DH, DH)
-        kv_ref[:, columns] = rotated(k_ref[:, columns])
-    kv_ref[:, pl.ds(2 * DH, 2 * DH)] = v_ref[...]
     half = keep_ref.shape[1]
-    for out_ref, which in ((keep_ref, core), (give_ref, 1 - core)):
+    for q_out, kv_out, which in (
+        (keep_ref, keep_kv_ref, core),
+        (give_ref, give_kv_ref, 1 - core),
+    ):
+        head_span = pl.ds(pl.multiple_of(which * DH, DH), DH)
+        kv_out[:, :DH] = rotated(k_ref[:, head_span])
+        kv_out[:, DH:] = v_ref[:, head_span]
         for head in range(half // DH):
             source = pl.ds(pl.multiple_of(which * half + head * DH, DH), DH)
-            out_ref[:, pl.ds(head * DH, DH)] = rotated(q_ref[:, source])
+            q_out[:, pl.ds(head * DH, DH)] = rotated(q_ref[:, source])
 
 
 def rotate_all(core, queries, keys, values, cos_t, sin_t):
@@ -97,143 +106,192 @@
     return pl.pallas_call(
         rotate_kernel,
         in_specs=[pl.BlockSpec(memory_space=pltpu.SMEM)] + [vmem] * 5,
-        out_specs=[vmem] * 3,
-        out_shape=[
-            jax.ShapeDtypeStruct((rows, width // 2), BF16),
-            jax.ShapeDtypeStruct((rows, width // 2), BF16),
-            jax.ShapeDtypeStruct((rows, 4 * DH), BF16),
-        ],
+        out_specs=[vmem] * 4,
+        out_shape=[jax.ShapeDtypeStruct((rows, width // 2), BF16)] * 2
+        + [jax.ShapeDtypeStruct((rows, 2 * DH), BF16)] * 2,
         compiler_params=params(),
         name="rotate_all",
     )(core, queries, keys, values, cos_t, sin_t)
 
 
-def attend_kernel(
-    meta_ref, theirs_ref, own_ref, k_ref, v_ref, theirs_out_ref, own_out_ref,
-    q_ref, max_ref, sum_ref, acc_ref, *, heads, tile_heads
-):
-    step = pl.program_id(0)
-    second = step >= meta_ref[2]
-    chunk = jnp.where(second, step - meta_ref[2], step)
-    block = jnp.where(second, meta_ref[1], meta_ref[0])
-    diagonal = block // CHUNK_BLOCKS
-    keys_len = CHUNK_BLOCKS * BLOCK
+def first_block(z, y, c):
+    return z // 2 * 64 + y * 16 + c * 8 + z % 2 * 4
+
+
+def attend_kernel(meta_ref, theirs_ref, own_ref, *refs, units, pieces, heads, tile_heads, first, last):
+    piece_refs, refs = refs[:pieces], refs[pieces:]
+    if not first:
+        state_in, refs = refs[:3], refs[3:]
+    if last:
+        out_refs, refs = refs[:2], refs[2:]
+    state, refs = refs[:3], refs[3:]
+    kv_ref, q_ref, base_ref, list_ref, sem_ref = refs
+    unit_rows = UNIT * BLOCK
+    copies = []
+    place = 0
+    for index, piece in enumerate(piece_refs):
+        size = piece.shape[0]
+        copies.append(
+            pltpu.make_async_copy(piece, kv_ref.at[pl.ds(place, size), :], sem_ref.at[index])
+        )
+        copies[-1].start()
+        place += size
+    max_ref, sum_ref, acc_ref = state
+    if first:
+        max_ref[...] = jnp.full_like(max_ref, -1e30)
+        sum_ref[...] = jnp.zeros_like(sum_ref)
+        acc_ref[...] = jnp.zeros_like(acc_ref)
+    else:
+        for source, target in zip(state_in, state):
+            target[...] = source[...]
+    q_ref[0] = theirs_ref[...]
+    q_ref[1] = own_ref[...]
+    for index, (z_off, y_off, c) in enumerate(units):
+        base_ref[index] = first_block((meta_ref[2] + z_off) % 4, (meta_ref[3] + y_off) % 4, c)
+    for copy in copies:
+        copy.wait()
+
     factor = math.log2(math.e) / math.sqrt(DH)
     rows = tile_heads * BLOCK
     parts = heads // tile_heads
-
-    @pl.when(chunk == 0)
-    def _():
-        max_ref[...] = jnp.full_like(max_ref, -1e30)
-        sum_ref[...] = jnp.zeros_like(sum_ref)
-        acc_ref[...] = jnp.zeros_like(acc_ref)
-
-    @pl.when(step == 0)
-    def _():
-        q_ref[...] = theirs_ref[...]
-
-    @pl.when(step == meta_ref[2])
-    def _():
-        q_ref[...] = own_ref[...]
-
-    def update(masked):
-        keys = k_ref[...].reshape(keys_len, DH)
-        vals = v_ref[...].reshape(keys_len, DH)
-        if masked:
-            offset = (block - chunk * CHUNK_BLOCKS) * BLOCK
-            row_token = lax.broadcasted_iota(jnp.int32, (BLOCK, keys_len), 0) + offset
-            key_token = lax.broadcasted_iota(jnp.int32, (BLOCK, keys_len), 1)
-            allowed = key_token <= row_token
-
-        def scores_of(part):
-            query = jnp.concatenate(
-                [q_ref[:, pl.ds((part * tile_heads + h) * DH, DH)] for h in range(tile_heads)],
-                axis=0,
+    keys_len = 2 * unit_rows
+
+    @pl.loop(0, 2)
+    def _(which):
+        block = meta_ref[which]
+
+        def update(u0, u1, masked):
+            starts = [pl.multiple_of(jnp.maximum(u, 0) * unit_rows, unit_rows) for u in (u0, u1)]
+            keys = jnp.concatenate([kv_ref[pl.ds(s, unit_rows), :DH] for s in starts], axis=0)
+            vals = jnp.concatenate([kv_ref[pl.ds(s, unit_rows), DH:] for s in starts], axis=0)
+            if masked:
+                bases = [jnp.where(u < 0, FAR, base_ref[jnp.maximum(u, 0)]) for u in (u0, u1)]
+                shape = (BLOCK, unit_rows)
+                row_token = lax.broadcasted_iota(jnp.int32, shape, 0)
+                key_token = lax.broadcasted_iota(jnp.int32, shape, 1)
+                allowed = jnp.concatenate(
+                    [
+                        jnp.where(key_token + (base - block) * BLOCK <= row_token, 1, 0)
+                        for base in bases
+                    ],
+                    axis=1,
+                )
+
+            def scores_of(part):
+                query = jnp.concatenate(
+                    [
+                        q_ref[which, :, pl.ds((part * tile_heads + h) * DH, DH)]
+                        for h in range(tile_heads)
+                    ],
+                    axis=0,
+                )
+                scores = lax.dot_general(
+                    query, keys, (((1,), (1,)), ((), ())), preferred_element_type=F32
+                )
+                if masked:
+                    scores = jnp.where(
+                        allowed[None] > 0, scores.reshape(tile_heads, BLOCK, keys_len), -1e30
+                    ).reshape(rows, keys_len)
+                return scores
+
+            def absorb(part, scores):
+                start = pl.multiple_of((which * heads + part * tile_heads) * BLOCK, BLOCK)
+                span = pl.ds(start, rows)
+                old_max = max_ref[span, :]
+                new_max = jnp.maximum(old_max, jnp.max(scores, axis=1, keepdims=True))
+                decay = jnp.exp2((old_max - new_max) * factor)
+                lane_sum = sum_ref[span, :] * decay
+                weights = []
+                for column in range(keys_len // DH):
+                    some = scores[:, column * DH : (column + 1) * DH]
+                    piece = jnp.exp2((some - new_max) * factor)
+                    lane_sum = lane_sum + piece
+                    weights.append(piece.astype(BF16))
+                sum_ref[span, :] = lane_sum
+                max_ref[span, :] = new_max
+                added = jnp.dot(jnp.concatenate(weights, axis=1), vals, preferred_element_type=F32)
+                acc_ref[span, :] = acc_ref[span, :] * decay + added
+
+            scores = scores_of(0)
+            for part in range(parts):
+                later = scores_of(part + 1) if part + 1 < parts else None
+                absorb(part, scores)
+                scores = later
+
+        count = jnp.int32(0)
+        diagonal = jnp.int32(-1)
+        for unit in range(len(units)):
+            base = base_ref[unit]
+            list_ref[count] = unit
+            count = count + jnp.where(base + UNIT <= block, 1, 0)
+            diagonal = jnp.where(
+                jnp.logical_and(base <= block, block < base + UNIT), unit, diagonal
             )
-            scores = lax.dot_general(
-                query, keys, (((1,), (1,)), ((), ())), preferred_element_type=F32
-            )
-            if masked:
-                scores = jnp.where(
-                    allowed[None], scores.reshape(tile_heads, BLOCK, keys_len), -1e30
-                ).reshape(rows, keys_len)
-            return scores
-
-        def absorb(part, scores):
-            span = pl.ds(part * rows, rows)
-            old_max = max_ref[span, :]
-            new_max = jnp.maximum(old_max, jnp.max(scores, axis=1, keepdims=True))
-            decay = jnp.exp2((old_max - new_max) * factor)
-            lane_sum = sum_ref[span, :] * decay
-            weights = []
-            for column in range(keys_len // DH):
-                piece = jnp.exp2((scores[:, column * DH : (column + 1) * DH] - new_max) * factor)
-                lane_sum = lane_sum + piece
-                weights.append(piece.astype(BF16))
-            sum_ref[span, :] = lane_sum
-            max_ref[span, :] = new_max
-            added = jnp.dot(jnp.concatenate(weights, axis=1), vals, preferred_element_type=F32)
-            acc_ref[span, :] = acc_ref[span, :] * decay + added
-
-        scores = scores_of(0)
-        for part in range(parts):
-            later = scores_of(part + 1) if part + 1 < parts else None
-            absorb(part, scores)
-            scores = later
-
-    @pl.when(chunk == diagonal)
-    def _():
-        update(True)
-
-        def store(out_ref):
-            for head in range(heads):
-                span = pl.ds(head * BLOCK, BLOCK)
-                total = jnp.sum(sum_ref[span, :], axis=1, keepdims=True)
-                out_ref[:, pl.ds(head * DH, DH)] = (acc_ref[span, :] / total).astype(BF16)
-
-        pl.when(second)(lambda: store(own_out_ref))
-        pl.when(jnp.logical_not(second))(lambda: store(theirs_out_ref))
-
-    @pl.when(chunk != diagonal)
-    def _():
-        update(False)
-
-
-def attend(meta, theirs, own, gathered, tile_heads=TILE_HEADS):
+        whole = count // 2
+
+        @pl.loop(0, whole)
+        def _(step):
+            update(list_ref[2 * step], list_ref[2 * step + 1], False)
+
+        odd = jnp.where(count > 2 * whole, list_ref[jnp.maximum(count - 1, 0)], -1)
+
+        @pl.when(jnp.logical_or(odd >= 0, diagonal >= 0))
+        def _():
+            update(odd, diagonal, True)
+
+    if last:
+        for head in range(2 * heads):
+            span = pl.ds(head * BLOCK, BLOCK)
+            total = jnp.sum(sum_ref[span, :], axis=1, keepdims=True)
+            out_refs[head // heads][:, pl.ds(head % heads * DH, DH)] = (
+                acc_ref[span, :] / total
+            ).astype(BF16)
+
+
+def attend(meta, units, theirs, own, pieces, state=None, last=False, tile_heads=TILE_HEADS):
     rows, width = own.shape
     heads = width // DH
-    steps = BLOCKS // CHUNK_BLOCKS + 1
-
-    def key_map(column):
-        def index(step, meta_ref):
-            chunk = jnp.where(step >= meta_ref[2], step - meta_ref[2], step)
-            return chunk // 8, (chunk // 2) % 4, 0, chunk % 2, 0, 2 * column + meta_ref[3]
-
-        return index
-
-    def whole(step, meta_ref):
-        return 0, 0
-
-    piece = (2, 1, 4, 1, BLOCK, DH)
+    vmem = pl.BlockSpec(memory_space=pltpu.VMEM)
+    states = [(2 * heads * rows, DH)] * 3
+    scratch = [
+        pltpu.VMEM((len(units) * UNIT * BLOCK, 2 * DH), BF16),
+        pltpu.VMEM((2, rows, width), BF16),
+        pltpu.SMEM((len(units),), jnp.int32),
+        pltpu.SMEM((len(units) + 1,), jnp.int32),
+        pltpu.SemaphoreType.DMA((len(pieces),)),
+    ]
+    if last:
+        scratch = [pltpu.VMEM(shape, F32) for shape in states] + scratch
+        out_shape = [jax.ShapeDtypeStruct((rows, width), BF16)] * 2
+    else:
+        out_shape = [jax.ShapeDtypeStruct(shape, F32) for shape in states]
+    state = [] if state is None else list(state)
+    kernel = functools.partial(
+        attend_kernel,
+        units=units,
+        pieces=len(pieces),
+        heads=heads,
+        tile_heads=tile_heads,
+        first=not state,
+        last=last,
+    )
+    keys_seen = len(units) * UNIT * BLOCK
     return pl.pallas_call(
-        functools.partial(attend_kernel, heads=heads, tile_heads=tile_heads),
-        grid_spec=pltpu.PrefetchScalarGridSpec(
-            num_scalar_prefetch=1,
-            grid=(steps,),
-            in_specs=[
-                pl.BlockSpec((rows, width), whole),
-                pl.BlockSpec((rows, width), whole),
-                pl.BlockSpec(piece, key_map(0)),
-                pl.BlockSpec(piece, key_map(1)),
-            ],
-            out_specs=[pl.BlockSpec((rows, width), whole)] * 2,
-            scratch_shapes=[pltpu.VMEM((rows, width), BF16)]
-            + [pltpu.VMEM((heads * rows, DH), F32)] * 3,
+        kernel,
+        in_specs=[pl.BlockSpec(memory_space=pltpu.SMEM), vmem, vmem]
+        + [pl.BlockSpec(memory_space=pl.ANY)] * len(pieces)
+        + [vmem] * len(state),
+        out_specs=[vmem] * len(out_shape),
+        out_shape=out_shape,
+        scratch_shapes=scratch,
+        compiler_params=params(),
+        cost_estimate=pl.CostEstimate(
+            flops=4 * keys_seen * heads * rows * DH,
+            bytes_accessed=keys_seen * 4 * DH,
+            transcendentals=keys_seen * heads * rows,
         ),
-        out_shape=[jax.ShapeDtypeStruct((rows, width), BF16)] * 2,
-        compiler_params=params("arbitrary"),
-        name="attend",
-    )(meta, theirs, own, gathered, gathered)
+        name="attend_last" if last else "attend_more" if state else "attend_first",
+    )(meta, theirs, own, *pieces, *state)
 
 
 def slots_of(ids_ref):
@@ -515,6 +573,24 @@
     return lax.all_to_all(packed, AXES, split_axis=0, concat_axis=0, tiled=True)
 
 
+def ring_near(piece, axes):
+    left = lax.ppermute(piece, axes, [(i, (i + 1) % 4) for i in range(4)])
+    right = lax.ppermute(piece, axes, [(i, (i + 3) % 4) for i in range(4)])
+    return left, right
+
+
+def ring_far(left, right, axes):
+    half = left.shape[0] // 2
+    low = lax.ppermute(left[:half], axes, [(i, (i + 1) % 4) for i in range(4)])
+    high = lax.ppermute(right[half:], axes, [(i, (i + 3) % 4) for i in range(4)])
+    return low, high
+
+
+def ring_gather(piece, axes):
+    left, right = ring_near(piece, axes)
+    return jnp.concatenate([piece, left, right, *ring_far(left, right, axes)], axis=0)
+
+
 def local(
     hidden, queries, keys, values, w_out, norm_gain, w_router, expert_ids, w_gate, w_up, w_down
 ):
@@ -524,14 +600,37 @@
     positions = device * rows + jnp.arange(rows, dtype=jnp.int32)
     cos_t, sin_t = yarn_tables(positions, DH)
     core_arr = core.reshape(1).astype(jnp.int32)
-    keep, give, kv = rotate_all(core_arr, queries, keys, values, cos_t, sin_t)
-    gathered = lax.all_gather(kv, TORUS, axis=0, tiled=True)
-    gathered = gathered.reshape(4, 4, 4, 2, BLOCK, 4 * DH)
+    keep, give, keep_kv, give_kv = rotate_all(core_arr, queries, keys, values, cos_t, sin_t)
     mirror = [(i, BLOCKS - 1 - i) for i in range(BLOCKS)]
     taken = lax.ppermute(give, AXES, mirror)
-    other = BLOCKS - 1 - device
-    meta = jnp.stack([other, device, other // CHUNK_BLOCKS + 1, core]).astype(jnp.int32)
-    theirs, own = attend(meta, taken, keep, gathered)
+    other_kv = lax.ppermute(give_kv, ("c",), [(0, 1), (1, 0)])
+    is_low = core == 0
+    chip = jnp.concatenate(
+        [jnp.where(is_low, keep_kv, other_kv), jnp.where(is_low, other_kv, keep_kv)], axis=0
+    )
+    row = lax.all_gather(chip, ("x",), axis=0)
+    low = row[:, :rows].reshape(UNIT * rows, 2 * DH)
+    high = row[:, rows:].reshape(UNIT * rows, 2 * DH)
+    low = ring_gather(low, RING_Y)
+    high = ring_gather(high, RING_Z)
+    low_near = ring_near(low, RING_Z)
+    high_near = ring_near(high, RING_Y)
+    low_far = ring_far(*low_near, RING_Z)
+    high_far = ring_far(*high_near, RING_Y)
+
+    def units(order):
+        return [(outer, inner, 0) for outer in order for inner in OFFSETS] + [
+            (inner, outer, 1) for outer in order for inner in OFFSETS
+        ]
+
+    meta = jnp.stack(
+        [BLOCKS - 1 - device, device, lax.axis_index(RING_Z), lax.axis_index(RING_Y)]
+    ).astype(jnp.int32)
+    state = attend(meta, units((0,)), taken, keep, [low, high])
+    state = attend(meta, units((-1, 1)), taken, keep, [*low_near, *high_near], state=state)
+    theirs, own = attend(
+        meta, units((2,)), taken, keep, [*low_far, *high_far], state=state, last=True
+    )
     got = lax.ppermute(theirs, AXES, mirror)
     part = project_own(core_arr, own, w_out)
     h1, slot, route, send = project(
@@ -548,6 +647,4 @@
     in_specs = (
         split, split, split, split, P(), P(), P(), split, experts, experts, experts,
     )
-    return jax.shard_map(
-        local, mesh=torus, in_specs=in_specs, out_specs=split, check_vma=False
-    )
+    return jax.shard_map(local, mesh=torus, in_specs=in_specs, out_specs=split, check_vma=False)

time: 307 us -> 294 us (0.958)
  waiting for transfers between devices: 80.2 us -> 15.3 us
  starting transfers between devices: 11.2 us -> 39.6 us
  blocking collectives: 129 us -> 143 us
  between operations: 13.4 us -> 0.22 us
  Pallas kernels: 69.2 us -> 80.8 us
  local copies, waits for them, and re-layouts: 0.71 us -> 10.8 us
    all_gather x1 -> x0, waiting for transfers between devices: 69.3 us -> none  [local(): gathered = lax.all_gather(kv, TORUS, axis=0, tiled=True)]
    ppermute x0 -> x17, starting transfers between devices: none -> 21.4 us  [the longest x4 7.38 us: ring_far(): lax.ppermute(right[half:], axes, [(i, (i + 3) % 4) for i in range(4)])]
    ppermute x0 -> x17, waiting for transfers between devices: none -> 13.9 us  [the longest x4 12.8 us: ring_near(): left = lax.ppermute(piece, axes, [(i, (i + 1) % 4) for i in range(4)])]
    pallas_call x1 -> x3, Pallas kernels: 30.3 us -> 41.9 us  [attend(): pl.pallas_call(kernel, in_specs=[pl.BlockSpec(memory_space=pltpu.SMEM), v...]
    all_gather x0 -> x1, blocking collectives: none -> 11.2 us  [local(): row = lax.all_gather(chip, ('x',), axis=0)]
    unnamed x4 -> x18, local copies, waits for them, and re-layouts: 0.71 us -> 7.16 us
    ppermute x1, waiting for transfers between devices: 5.76 us -> 0.01 us  [local(): taken = lax.ppermute(give, AXES, mirror)]
    ppermute x1, starting transfers between devices: 3.64 us -> 9.37 us  [local(): got = lax.ppermute(theirs, AXES, mirror)]
  transfers between devices with their start and end apart: 3 -> 19, of which waited for: 3 -> 5; matrix products, arithmetic and copies ran while one was open for 0% -> 3% of each run, Pallas kernels for 1% -> 12%
where the time goes in v3:
time: 294 us; the launch traced here: 292 us
  blocking collectives  143 us (49%)
  Pallas kernels  80.8 us (27%)
  starting transfers between devices  39.6 us (13%)
  waiting for transfers between devices  15.3 us (5%)
  local copies, waits for them, and re-layouts  10.8 us (4%)
    all_to_all x2, blocking collectives, exchange(): return lax.all_to_all(packed, AXES, split_axis=0, concat_axis=0, tiled=True)  132 us
    pallas_call x3, Pallas kernels, attend(): pl.pallas_call(kernel, in_specs=[pl.BlockSpec(memory_space=pltpu.SMEM), v...  41.9 us
    pallas_call x1, Pallas kernels, experts_of(): pl.pallas_call(functools.partial(expert_kernel, up_steps=up_steps), grid=...  20.1 us
    ppermute x4, waiting for transfers between devices, ring_near(): left = lax.ppermute(piece, axes, [(i, (i + 1) % 4) for i in range(4)])  12.8 us
    all_gather x1, blocking collectives, local(): row = lax.all_gather(chip, ('x',), axis=0)  11.2 us
    ppermute x1, starting transfers between devices, local(): got = lax.ppermute(theirs, AXES, mirror)  9.37 us
    ppermute x1, starting transfers between devices, local(): taken = lax.ppermute(give, AXES, mirror)  8.85 us
    pallas_call x1, Pallas kernels, project(): pl.pallas_call(project_kernel, grid_spec=pltpu.PrefetchScalarGridSpec(num...  7.82 us
  transfers between devices with their start and end apart: 19, of which 5 were waited for; matrix products, arithmetic and copies ran while one was open for 3% of the time, Pallas kernels for 12%

profile of v3, /device:TPU:9, one launch (start us, length us, event | category | flops | bytes accessed | tf_op | source)
XLA Modules:
  0.0 292.1 jit_solution(12801716902041206201)
XLA Ops:
  0.1 0.3 fusion.2
  0.4 0.8 pad_maximum_fusion.1
  1.1 2.2 rotate_all.1
  3.3 0.7 collective-permute-start.1
  4.0 1.1 collective-permute-done.1
  5.1 0.9 broadcast_select_fusion.1
  6.0 11.2 %all-gather = bf16[1024,256]{1,0:T(8,128)(2,1)S(1)} all-gather(bf16[256,256]{1,0:T(8,128)(2,1)S(1)} %pad_maximum_fusion), channel_id=2, replica_groups=mesh['zh'=2,'y'=4,'c'=2,'zl'=2,'x'=4] {'x'}, dimensions={0}, use_global_device_ids=true | all-gather | bytes 655360 | tf_op jit(solution)/shard_map/all_gather | solution.py:611
  17.2 1.7 collective-permute-start.10
  18.9 2.2 collective-permute-start.11
  21.1 1.3 collective-permute-start.2
  22.6 0.7 constant_dynamic-update-slice_fusion.9
  23.3 0.7 constant_dynamic-update-slice_fusion.4
  24.1 1.4 collective-permute-done.10
  25.6 2.7 collective-permute-start.13
  28.4 1.4 collective-permute-start.4
  29.7 0.2 collective-permute-start.5
  30.0 0.7 constant_dynamic-update-slice_fusion.8
  30.7 0.7 constant_dynamic-update-slice_fusion.7
  31.4 0.7 constant_dynamic-update-slice_fusion.3
  32.2 0.7 constant_dynamic-update-slice_fusion.2
  32.9 0.7 constant_dynamic-update-slice_fusion.6
  33.6 0.7 constant_dynamic-update-slice_fusion.5.refs_1_
  34.2 1.3 collective-permute-start.14
  35.7 0.7 constant_dynamic-update-slice_fusion.1
  36.4 0.7 constant_dynamic-update-slice_fusion.refs_0_
  37.0 2.7 collective-permute-start.8
  39.7 8.9 %collective-permute-start = (bf16[128,1024]{1,0:T(8,128)(2,1)S(1)}, bf16[128,1024]{1,0:T(8,128)(2,1)}, u32[]{:S(2)}, u32[]{:S(2)}) collective-permute-start(bf16[128,1024]{1,0:T(8,128)(2,1)S(1)} %copy-done.4), channel_id=1, source_target_pairs={{0,127},{1,126},{2,125},{3,124},{4,123},{5,122},{6,121},{7,120},{8... | collective-permute-start | bytes 786440 | tf_op jit(solution)/shard_map/ppermute | solution.py:605
  48.6 0.6 pad_add_fusion.meta_ref
  49.2 10.9 %collective-permute-done.14.refs_2_ = bf16[2048,256]{1,0:T(8,128)(2,1)S(1)} collective-permute-done((bf16[2048,256]{1,0:T(8,128)(2,1)}, bf16[2048,256]{1,0:T(8,128)(2,1)S(1)}, u32[]{:S(2)}, u32[]{:S(2)}) %collective-permute-start.14) | collective-permute-done | bytes 1048608 | tf_op jit(solution)/shard_map/ppermute | solution.py:577
  60.1 2.3 collective-permute-start.15
  62.4 1.5 collective-permute-start.17
  63.9 0.5 collective-permute-done.6.refs_0_
  64.4 1.1 slice.43
  65.6 1.1 slice.44
  66.6 2.9 collective-permute-start.9
  69.6 13.3 %attend_first.1 = (f32[2048,128]{1,0:T(8,128)}, f32[2048,128]{1,0:T(8,128)}, f32[2048,128]{1,0:T(8,128)}) custom-call(s32[4]{0:T(128)} %pad_add_fusion.meta_ref, bf16[128,1024]{1,0:T(8,128)(2,1)} %collective-permute-done.theirs_ref, bf16[128,1024]{1,0:T(8,128)(2,1)} %get-tuple-element.22.own_ref, ...), custom_call_target="tpu_custom_call" | custom-call | flops 2147483648 | bytes 2097152 | tf_op jit(solution)/shard_map/attend_first/pallas_call | solution.py:279
  82.9 19.3 %attend_more.1 = (f32[2048,128]{1,0:T(8,128)}, f32[2048,128]{1,0:T(8,128)}, f32[2048,128]{1,0:T(8,128)}) custom-call(s32[4]{0:T(128)} %pad_add_fusion.meta_ref, bf16[128,1024]{1,0:T(8,128)(2,1)} %collective-permute-done.theirs_ref, bf16[128,1024]{1,0:T(8,128)(2,1)} %get-tuple-element.22.own_ref, bf16[2048,256]{1,0:T(8,128)(2,1)} %collective-permute-done.6.refs_0_, ...), custom_call_target="tpu_custom_call" | custom-call | flops 4294967296 | bytes 4194304 | tf_op jit(solution)/shard_map/attend_more/pallas_call | solution.py:279
  102.2 0.8 copy-done.3
  103.0 9.3 %attend_last.1 = (bf16[128,1024]{1,0:T(8,128)(2,1)}, bf16[128,1024]{1,0:T(8,128)(2,1)}) custom-call(s32[4]{0:T(128)} %pad_add_fusion.meta_ref, bf16[128,1024]{1,0:T(8,128)(2,1)} %collective-permute-done.theirs_ref, bf16[128,1024]{1,0:T(8,128)(2,1)} %get-tuple-element.22.own_ref, bf16[1024,256]{1,0:T(8,128)(2,1)} %collective-permute-done.7.refs_0_, ...), custom_call_target="tpu_custom_call" | custom-call | flops 2147483648 | bytes 2097152 | tf_op jit(solution)/shard_map/attend_last/pallas_call | solution.py:279
  112.3 9.4 %collective-permute-start.18 = (bf16[128,1024]{1,0:T(8,128)(2,1)}, bf16[128,1024]{1,0:T(8,128)(2,1)S(1)}, u32[]{:S(2)}, u32[]{:S(2)}) collective-permute-start(bf16[128,1024]{1,0:T(8,128)(2,1)} %get-tuple-element.32), channel_id=1, source_target_pairs={{0,127},{1,126},{2,125},{3,124},{4,123},{5,122},{6,121},{7,120},{8... | collective-permute-start | bytes 786440 | tf_op jit(solution)/shard_map/ppermute | solution.py:634
  121.6 3.8 %project_own.1.part_ref = f32[128,2048]{1,0:T(8,128)} custom-call(s32[1]{0:T(128)} %bitcast.core_ref, bf16[128,1024]{1,0:T(8,128)(2,1)} %get-tuple-element.31.own_ref, bf16[2048,2048]{1,0:T(8,128)(2,1)} %w_ref.3), custom_call_target="tpu_custom_call" | custom-call | flops 536870912 | bytes 4194304 | tf_op jit(solution)/shard_map/project_own/pallas_call | solution.py:326
  125.4 1.4 collective-permute-done.18.got_ref
  126.8 0.7 copy-done
  127.5 7.8 %project.1 = (bf16[128,2048]{1,0:T(8,128)(2,1)}, f32[128,128]{1,0:T(8,128)}, f32[128,128]{1,0:T(8,128)}, bf16[128,144,128]{2,1,0:T(8,128)(2,1)}) custom-call(s32[1]{0:T(128)} %bitcast.core_ref, f32[128,2048]{1,0:T(8,128)} %project_own.1.part_ref, bf16[128,1024]{1,0:T(8,128)(2,1)} %copy-done, bf16[2048,2048]{1,0:T(8,128)(2,1)} %w_ref.3, ...), custom_call_target="tpu_custom_call" | custom-call | tf_op jit(solution)/shard_map/project/pallas_call | solution.py:397
  135.3 67.6 %all_to_all.10.in_ref = bf16[128,144,128]{2,1,0:T(8,128)(2,1)} all-to-all(bf16[128,144,128]{2,1,0:T(8,128)(2,1)} %get-tuple-element.35), channel_id=1, replica_groups=mesh['zh'=2,'y'=4,'c'=2,'zl'=2,'x'=4] {'zh','y','c','zl','x'}, dimensions={0} | all-to-all | bytes 9437184 | tf_op jit(solution)/shard_map/all_to_all | solution.py:573
  202.9 20.1 %experts_of.1 = bf16[128,144,128]{2,1,0:T(8,128)(2,1)} custom-call(bf16[128,144,128]{2,1,0:T(8,128)(2,1)} %all_to_all.10.in_ref, bf16[2048,768]{1,0:T(8,128)(2,1)} %bitcast.13, bf16[2048,768]{1,0:T(8,128)(2,1)} %bitcast.14, bf16[768,2048]{1,0:T(8,128)(2,1)} %bitcast.15), custom_call_target="tpu_custom_call" | custom-call | tf_op jit(solution)/shard_map/experts_of/pallas_call | solution.py:507
  223.0 64.0 %all_to_all.11.in_ref = bf16[128,144,128]{2,1,0:T(8,128)(2,1)} all-to-all(bf16[128,144,128]{2,1,0:T(8,128)(2,1)} %experts_of.1), channel_id=1, replica_groups=mesh['zh'=2,'y'=4,'c'=2,'zl'=2,'x'=4] {'zh','y','c','zl','x'}, dimensions={0} | all-to-all | bytes 9437184 | tf_op jit(solution)/shard_map/all_to_all | solution.py:573
  287.0 5.1 %combine.1 = bf16[128,2048]{1,0:T(8,128)(2,1)} custom-call(f32[128,128]{1,0:T(8,128)} %get-tuple-element.33.slot_ref, f32[128,128]{1,0:T(8,128)} %get-tuple-element.34.route_ref, bf16[128,144,128]{2,1,0:T(8,128)(2,1)} %all_to_all.11.in_ref, bf16[128,2048]{1,0:T(8,128)(2,1)} %get-tuple-element.36.h1_ref), custom_call_target="tpu_custom_call" | custom-call | tf_op jit(solution)/shard_map/combine/pallas_call | solution.py:561
  (37 shorter events, 0.7 us)
Async XLA Ops:
  3.3 36.4 %copy-start.4 = (bf16[128,1024]{1,0:T(8,128)(2,1)S(1)}, bf16[128,1024]{1,0:T(8,128)(2,1)}, u32[]{:S(2)}) copy-start(bf16[128,1024]{1,0:T(8,128)(2,1)} %get-tuple-element.21) | copy-start | bytes 786436
  3.3 1.8 collective-permute-start.1
  17.2 8.3 %collective-permute-start.10 = (bf16[512,256]{1,0:T(8,128)(2,1)S(1)}, bf16[512,256]{1,0:T(8,128)(2,1)S(1)}, u32[]{:S(2)}, u32[]{:S(2)}) collective-permute-start(bf16[512,256]{1,0:T(8,128)(2,1)S(1)} %bitcast.20), channel_id=1, source_target_pairs={{0,4},{4,64},{64,68},{68,0},{1,5},{5,65},{65,69},{69,1},{2,6},{6,6... | collective-permute-start | bytes 786440 | tf_op jit(solution)/shard_map/ppermute | solution.py:577
  18.9 6.6 %collective-permute-start.11 = (bf16[512,256]{1,0:T(8,128)(2,1)S(1)}, bf16[512,256]{1,0:T(8,128)(2,1)S(1)}, u32[]{:S(2)}, u32[]{:S(2)}) collective-permute-start(bf16[512,256]{1,0:T(8,128)(2,1)S(1)} %bitcast.21), channel_id=1, source_target_pairs={{0,68},{4,0},{64,4},{68,64},{1,69},{5,1},{65,5},{69,65},{2,70},{6,... | collective-permute-start | bytes 786440 | tf_op jit(solution)/shard_map/ppermute | solution.py:578
  21.1 7.2 %collective-permute-start.2 = (bf16[512,256]{1,0:T(8,128)(2,1)S(1)}, bf16[512,256]{1,0:T(8,128)(2,1)S(1)}, u32[]{:S(2)}, u32[]{:S(2)}) collective-permute-start(bf16[512,256]{1,0:T(8,128)(2,1)S(1)} %bitcast.17), channel_id=1, source_target_pairs={{0,16},{16,32},{32,48},{48,0},{1,17},{17,33},{33,49},{49,1},{2,18}... | collective-permute-start | bytes 786440 | tf_op jit(solution)/shard_map/ppermute | solution.py:577
  22.4 7.3 %collective-permute-start.3 = (bf16[512,256]{1,0:T(8,128)(2,1)S(1)}, bf16[512,256]{1,0:T(8,128)(2,1)S(1)}, u32[]{:S(2)}, u32[]{:S(2)}) collective-permute-start(bf16[512,256]{1,0:T(8,128)(2,1)S(1)} %bitcast.18), channel_id=1, source_target_pairs={{0,48},{16,0},{32,16},{48,32},{1,49},{17,1},{33,17},{49,33},{2,50}... | collective-permute-start | bytes 786440 | tf_op jit(solution)/shard_map/ppermute | solution.py:578
  25.5 7.4 %collective-permute-start.12 = (bf16[256,256]{1,0:T(8,128)(2,1)S(1)}, bf16[256,256]{1,0:T(8,128)(2,1)S(1)}, u32[]{:S(2)}, u32[]{:S(2)}) collective-permute-start(bf16[256,256]{1,0:T(8,128)(2,1)S(1)} %slice.46), channel_id=1, source_target_pairs={{0,4},{4,64},{64,68},{68,0},{1,5},{5,65},{65,69},{69,1},{2,6},{6,6... | collective-permute-start | bytes 393224 | tf_op jit(solution)/shard_map/ppermute | solution.py:584
  25.6 7.9 %collective-permute-start.13 = (bf16[256,256]{1,0:T(8,128)(2,1)S(1)}, bf16[256,256]{1,0:T(8,128)(2,1)S(1)}, u32[]{:S(2)}, u32[]{:S(2)}) collective-permute-start(bf16[256,256]{1,0:T(8,128)(2,1)S(1)} %slice.47), channel_id=1, source_target_pairs={{0,68},{4,0},{64,4},{68,64},{1,69},{5,1},{65,5},{69,65},{2,70},{6,... | collective-permute-start | bytes 393224 | tf_op jit(solution)/shard_map/ppermute | solution.py:585
  28.4 7.3 %collective-permute-start.4 = (bf16[256,256]{1,0:T(8,128)(2,1)S(1)}, bf16[256,256]{1,0:T(8,128)(2,1)S(1)}, u32[]{:S(2)}, u32[]{:S(2)}) collective-permute-start(bf16[256,256]{1,0:T(8,128)(2,1)S(1)} %slice.41), channel_id=1, source_target_pairs={{0,16},{16,32},{32,48},{48,0},{1,17},{17,33},{33,49},{49,1},{2,18}... | collective-permute-start | bytes 393224 | tf_op jit(solution)/shard_map/ppermute | solution.py:584
  29.7 6.6 %collective-permute-start.5 = (bf16[256,256]{1,0:T(8,128)(2,1)S(1)}, bf16[256,256]{1,0:T(8,128)(2,1)S(1)}, u32[]{:S(2)}, u32[]{:S(2)}) collective-permute-start(bf16[256,256]{1,0:T(8,128)(2,1)S(1)} %slice.42), channel_id=1, source_target_pairs={{0,48},{16,0},{32,16},{48,32},{1,49},{17,1},{33,17},{49,33},{2,50}... | collective-permute-start | bytes 393224 | tf_op jit(solution)/shard_map/ppermute | solution.py:585
  34.2 25.8 %collective-permute-start.14 = (bf16[2048,256]{1,0:T(8,128)(2,1)}, bf16[2048,256]{1,0:T(8,128)(2,1)S(1)}, u32[]{:S(2)}, u32[]{:S(2)}) collective-permute-start(bf16[2048,256]{1,0:T(8,128)(2,1)} %constant_dynamic-update-slice_fusion.5.refs_1_), channel_id=1, source_target_pairs={{0,16},{16,32},{32,48},{48,0},{1,17},{17,33},{33,49},{49,1},{2,18}... | collective-permute-start | bytes 3145736 | tf_op jit(solution)/shard_map/ppermute | solution.py:577
  35.5 26.8 %collective-permute-start.16 = (bf16[2048,256]{1,0:T(8,128)(2,1)}, bf16[2048,256]{1,0:T(8,128)(2,1)S(1)}, u32[]{:S(2)}, u32[]{:S(2)}) collective-permute-start(bf16[2048,256]{1,0:T(8,128)(2,1)} %constant_dynamic-update-slice_fusion.5.refs_1_), channel_id=1, source_target_pairs={{0,48},{16,0},{32,16},{48,32},{1,49},{17,1},{33,17},{49,33},{2,50}... | collective-permute-start | bytes 3145736 | tf_op jit(solution)/shard_map/ppermute | solution.py:578
  37.0 27.3 %collective-permute-start.6 = (bf16[2048,256]{1,0:T(8,128)(2,1)}, bf16[2048,256]{1,0:T(8,128)(2,1)}, u32[]{:S(2)}, u32[]{:S(2)}) collective-permute-start(bf16[2048,256]{1,0:T(8,128)(2,1)} %constant_dynamic-update-slice_fusion.refs_0_), channel_id=1, source_target_pairs={{0,4},{4,64},{64,68},{68,0},{1,5},{5,65},{65,69},{69,1},{2,6},{6,6... | collective-permute-start | bytes 3145736 | tf_op jit(solution)/shard_map/ppermute | solution.py:577
  37.0 28.5 %collective-permute-start.8 = (bf16[2048,256]{1,0:T(8,128)(2,1)}, bf16[2048,256]{1,0:T(8,128)(2,1)}, u32[]{:S(2)}, u32[]{:S(2)}) collective-permute-start(bf16[2048,256]{1,0:T(8,128)(2,1)} %constant_dynamic-update-slice_fusion.refs_0_), channel_id=1, source_target_pairs={{0,68},{4,0},{64,4},{68,64},{1,69},{5,1},{65,5},{69,65},{2,70},{6,... | collective-permute-start | bytes 3145736 | tf_op jit(solution)/shard_map/ppermute | solution.py:578
  39.7 29.8 %collective-permute-start = (bf16[128,1024]{1,0:T(8,128)(2,1)S(1)}, bf16[128,1024]{1,0:T(8,128)(2,1)}, u32[]{:S(2)}, u32[]{:S(2)}) collective-permute-start(bf16[128,1024]{1,0:T(8,128)(2,1)S(1)} %copy-done.4), channel_id=1, source_target_pairs={{0,127},{1,126},{2,125},{3,124},{4,123},{5,122},{6,121},{7,120},{8... | collective-permute-start | bytes 786440 | tf_op jit(solution)/shard_map/ppermute | solution.py:605
  60.0 22.8 %copy-start.1 = (bf16[2048,256]{1,0:T(8,128)(2,1)}, bf16[2048,256]{1,0:T(8,128)(2,1)S(1)}, u32[]{:S(2)}) copy-start(bf16[2048,256]{1,0:T(8,128)(2,1)S(1)} %collective-permute-done.14.refs_2_) | copy-start | bytes 3145732
  60.1 42.1 %collective-permute-start.15 = (bf16[1024,256]{1,0:T(8,128)(2,1)S(1)}, bf16[1024,256]{1,0:T(8,128)(2,1)S(1)}, u32[]{:S(2)}, u32[]{:S(2)}) collective-permute-start(bf16[1024,256]{1,0:T(8,128)(2,1)S(1)} %slice.48), channel_id=1, source_target_pairs={{0,16},{16,32},{32,48},{48,0},{1,17},{17,33},{33,49},{49,1},{2,18}... | collective-permute-start | bytes 1572872 | tf_op jit(solution)/shard_map/ppermute | solution.py:584
  62.3 1.6 copy-start.2
  62.4 39.8 %collective-permute-start.17 = (bf16[1024,256]{1,0:T(8,128)(2,1)S(1)}, bf16[1024,256]{1,0:T(8,128)(2,1)}, u32[]{:S(2)}, u32[]{:S(2)}) collective-permute-start(bf16[1024,256]{1,0:T(8,128)(2,1)S(1)} %slice.49), channel_id=1, source_target_pairs={{0,48},{16,0},{32,16},{48,32},{1,49},{17,1},{33,17},{49,33},{2,50}... | collective-permute-start | bytes 1572872 | tf_op jit(solution)/shard_map/ppermute | solution.py:585
  65.5 36.7 %collective-permute-start.7 = (bf16[1024,256]{1,0:T(8,128)(2,1)S(1)}, bf16[1024,256]{1,0:T(8,128)(2,1)}, u32[]{:S(2)}, u32[]{:S(2)}) collective-permute-start(bf16[1024,256]{1,0:T(8,128)(2,1)S(1)} %slice.43), channel_id=1, source_target_pairs={{0,4},{4,64},{64,68},{68,0},{1,5},{5,65},{65,69},{69,1},{2,6},{6,6... | collective-permute-start | bytes 1572872 | tf_op jit(solution)/shard_map/ppermute | solution.py:584
  66.6 35.6 %collective-permute-start.9 = (bf16[1024,256]{1,0:T(8,128)(2,1)S(1)}, bf16[1024,256]{1,0:T(8,128)(2,1)}, u32[]{:S(2)}, u32[]{:S(2)}) collective-permute-start(bf16[1024,256]{1,0:T(8,128)(2,1)S(1)} %slice.44), channel_id=1, source_target_pairs={{0,68},{4,0},{64,4},{68,64},{1,69},{5,1},{65,5},{69,65},{2,70},{6,... | collective-permute-start | bytes 1572872 | tf_op jit(solution)/shard_map/ppermute | solution.py:585
  102.2 0.8 copy-start.3
  112.3 14.5 %collective-permute-start.18 = (bf16[128,1024]{1,0:T(8,128)(2,1)}, bf16[128,1024]{1,0:T(8,128)(2,1)S(1)}, u32[]{:S(2)}, u32[]{:S(2)}) collective-permute-start(bf16[128,1024]{1,0:T(8,128)(2,1)} %get-tuple-element.32), channel_id=1, source_target_pairs={{0,127},{1,126},{2,125},{3,124},{4,123},{5,122},{6,121},{7,120},{8... | collective-permute-start | bytes 786440 | tf_op jit(solution)/shard_map/ppermute | solution.py:634
  126.8 0.7 copy-start

commit v4 on v3

--- a/solution.py
+++ b/solution.py
@@ -13,6 +13,7 @@
 TOP = 8
 CAP = 9
 MAIN = 8
+STRIPE = 48
 BLOCK = 128
 BLOCKS = 128
 UNIT = 4
@@ -345,25 +346,29 @@
 
 def project_kernel(
     core_ref, part_ref, got_ref, w_ref, hidden_ref, gain_ref, router_ref, ids_ref,
-    h1_ref, slot_ref, route_ref, send_ref, acc_ref, over_ref,
+    h1_ref, slot_ref, route_ref, send_ref, acc_ref, hn_ref, pick_ref, over_ref, *, steps,
 ):
     step = pl.program_id(0)
     depth = w_ref.shape[0]
+    tiles = hn_ref.shape[1] // DH
 
     @pl.when(step == 0)
     def _():
         acc_ref[...] = part_ref[...] + hidden_ref[...].astype(F32)
 
-    column = pl.ds(pl.multiple_of(step * depth, depth), depth)
-    acc_ref[...] += jnp.dot(got_ref[:, column], w_ref[...], preferred_element_type=F32)
-
-    @pl.when(step == pl.num_programs(0) - 1)
+    @pl.when(step < steps)
+    def _():
+        column = pl.ds(pl.multiple_of(step * depth, depth), depth)
+        acc_ref[...] += jnp.dot(got_ref[:, column], w_ref[...], preferred_element_type=F32)
+
+    @pl.when(step == steps - 1)
     def _():
         h1 = acc_ref[...].astype(BF16)
         h1_ref[...] = h1
         h1_f = h1.astype(F32)
         mean = jnp.mean(h1_f * h1_f, axis=-1, keepdims=True)
         hn = (h1_f / jnp.sqrt(mean + 1e-06) * gain_ref[...]).astype(BF16)
+        hn_ref[...] = hn
         logits = jnp.dot(hn, router_ref[...], preferred_element_type=F32)
         named, slot = slots_of(ids_ref)
         slot_ref[...] = slot
@@ -371,40 +376,59 @@
         route_ref[...] = raised / jnp.sum(raised, axis=0, keepdims=True)
         wanted = lax.broadcasted_iota(jnp.int32, (BLOCK, MAIN, BLOCK), 1).astype(F32)
         pick = jnp.where(slot[:, None, :] == wanted, 1.0, 0.0).reshape(BLOCK * MAIN, BLOCK)
-        pick = pick.astype(BF16)
+        pick_ref[...] = pick.astype(BF16)
         last = jnp.where(slot == float(MAIN), 1.0, 0.0).astype(BF16)
-        tiles = hn.shape[1] // DH
         for tile in range(tiles):
             part = hn[:, tile * DH : (tile + 1) * DH]
-            rows = jnp.dot(pick, part, preferred_element_type=F32)
-            send_ref[:, tile * MAIN : (tile + 1) * MAIN, :] = rows.reshape(
-                BLOCK, MAIN, DH
-            ).astype(BF16)
             over_ref[:, tile, :] = jnp.dot(last, part, preferred_element_type=F32)
-        send_ref[:, tiles * MAIN :, :] = over_ref[...].astype(BF16)
+
+    stripe = send_ref.shape[1] // MAIN
+    for index in range(pl.cdiv(tiles, stripe)):
+
+        @pl.when(step == steps + index)
+        def _(index=index):
+            first = index * stripe
+            held = min(stripe, tiles - first)
+            columns = hn_ref[:, first * DH : (first + held) * DH]
+            rows = jnp.dot(pick_ref[...], columns, preferred_element_type=F32)
+            send_ref[:, : held * MAIN, :] = tiled_rows(rows)
+            if held < stripe:
+                send_ref[:, held * MAIN :, :] = over_ref[...].astype(BF16)
+
+
+def tiled_rows(rows):
+    sources = rows.shape[0] // MAIN
+    pieces = [
+        rows[:, tile * DH : (tile + 1) * DH].reshape(sources, MAIN, DH)
+        for tile in range(rows.shape[1] // DH)
+    ]
+    return jnp.concatenate(pieces, axis=1).astype(BF16)
 
 
 def project(core, part, got, w_out, hidden, gain, w_router, ids_t, depth=512):
     rows, half = got.shape
     width = hidden.shape[1]
     steps = half // depth
+    experts = w_router.shape[1]
+    tiles = width // DH
+    packed = (experts, tiles * CAP, DH)
+    over = (experts, tiles, DH)
 
     def full(shape):
         return pl.BlockSpec(shape, lambda step, core_ref: (0,) * len(shape))
 
-    experts = w_router.shape[1]
-    packed = (experts, CAP * width // DH, DH)
+    def w_map(step, core_ref):
+        return (1 - core_ref[0]) * steps + jnp.minimum(step, steps - 1), 0
+
     return pl.pallas_call(
-        project_kernel,
+        functools.partial(project_kernel, steps=steps),
         grid_spec=pltpu.PrefetchScalarGridSpec(
             num_scalar_prefetch=1,
-            grid=(steps,),
+            grid=(steps + packed[1] // STRIPE,),
             in_specs=[
                 full((rows, width)),
                 full((rows, half)),
-                pl.BlockSpec(
-                    (depth, width), lambda step, core_ref: ((1 - core_ref[0]) * steps + step, 0)
-                ),
+                pl.BlockSpec((depth, width), w_map),
                 full((rows, width)),
                 full((1, width)),
                 full((width, experts)),
@@ -414,11 +438,16 @@
                 full((rows, width)),
                 full((experts, rows)),
                 full((experts, rows)),
-                full(packed),
+                pl.BlockSpec(
+                    (experts, STRIPE, DH),
+                    lambda step, core_ref: (0, jnp.maximum(step - steps, 0), 0),
+                ),
             ],
             scratch_shapes=[
                 pltpu.VMEM((rows, width), F32),
-                pltpu.VMEM((experts, width // DH, DH), F32),
+                pltpu.VMEM((rows, width), BF16),
+                pltpu.VMEM((experts * MAIN, rows), BF16),
+                pltpu.VMEM(over, F32),
             ],
         ),
         out_shape=[
@@ -432,88 +461,92 @@
     )(core, part, got, w_out, hidden, gain, w_router, ids_t)
 
 
-def expert_kernel(in_ref, gate_ref, up_ref, down_ref, out_ref, rows_ref, act_ref, over_ref, *, up_steps):
+def expert_kernel(
+    in_ref, gate_ref, up_ref, down_ref, out_ref, rows_ref, act_ref, over_ref, *, steps, up_steps
+):
     step = pl.program_id(0)
     tile = gate_ref.shape[1]
     sources = in_ref.shape[0]
     main_rows = sources * MAIN
-    width = gate_ref.shape[0]
-    tiles = width // DH
-
-    @pl.when(step == 0)
-    def _():
-        over_ref[...] = in_ref[:, tiles * MAIN :, :].astype(F32)
-        for place in range(tiles):
-            columns = pl.ds(place * DH, DH)
-            rows_ref[:main_rows, columns] = in_ref[:, place * MAIN : (place + 1) * MAIN, :].reshape(
-                main_rows, DH
-            )
-            rows_ref[main_rows:, columns] = over_ref[:, place, :].astype(BF16)
-
-    half = main_rows // 2
-    spans = [(0, half), (half, half), (main_rows, sources)]
-    for index in range(up_steps):
+    tiles = gate_ref.shape[0] // DH
+    stripe = in_ref.shape[1] // MAIN
+    third = sources * CAP // 3
+
+    for index in range(steps):
 
         @pl.when(step == index)
         def _(index=index):
-            for start, size in spans:
-                rows = rows_ref[start : start + size, :]
+            first = index * stripe
+            held = min(stripe, tiles - first)
+            for place in range(held):
+                columns = pl.ds((first + place) * DH, DH)
+                rows_ref[:main_rows, columns] = in_ref[
+                    :, place * MAIN : (place + 1) * MAIN, :
+                ].reshape(main_rows, DH)
+            if held < stripe:
+                over_ref[...] = in_ref[:, held * MAIN :, :].astype(F32)
+                for place in range(tiles):
+                    columns = pl.ds(place * DH, DH)
+                    rows_ref[main_rows:, columns] = over_ref[:, place, :].astype(BF16)
+
+    for index in range(up_steps):
+
+        @pl.when(step == steps + index)
+        def _(index=index):
+            for start in range(0, 3 * third, third):
+                rows = rows_ref[start : start + third, :]
                 gate = jnp.dot(rows, gate_ref[...], preferred_element_type=F32)
                 up = jnp.dot(rows, up_ref[...], preferred_element_type=F32)
                 act = gate / (1.0 + jnp.exp(-gate)) * up
-                act_ref[start : start + size, index * tile : (index + 1) * tile] = act.astype(BF16)
-
-    columns = down_ref.shape[1]
-    for index in range(width // columns):
-
-        @pl.when(step == up_steps + index)
+                act_ref[start : start + third, index * tile : (index + 1) * tile] = act.astype(BF16)
+
+    for index in range(steps):
+
+        @pl.when(step == steps + up_steps + index)
         def _(index=index):
-            first = index * columns // DH
-            for start, size in spans:
+            first = index * stripe
+            held = min(stripe, tiles - first)
+            for start in range(0, 3 * third, third):
                 rows = jnp.dot(
-                    act_ref[start : start + size, :], down_ref[...], preferred_element_type=F32
+                    act_ref[start : start + third, :],
+                    down_ref[:, : held * DH],
+                    preferred_element_type=F32,
                 )
-                for place in range(columns // DH):
-                    piece = rows[:, place * DH : (place + 1) * DH]
-                    if start < main_rows:
-                        some = pl.ds(start // MAIN, size // MAIN)
-                        out_ref[some, (first + place) * MAIN : (first + place + 1) * MAIN, :] = (
-                            piece.reshape(size // MAIN, MAIN, DH).astype(BF16)
-                        )
-                    else:
-                        over_ref[:, first + place, :] = piece
-            if index == width // columns - 1:
-                out_ref[:, tiles * MAIN :, :] = over_ref[...].astype(BF16)
+                some = min(third, main_rows - start)
+                out_ref[start // MAIN : (start + some) // MAIN, : held * MAIN, :] = tiled_rows(
+                    rows[:some]
+                )
+                if some < third:
+                    for place in range(held):
+                        over_ref[:, first + place, :] = rows[some:, place * DH : (place + 1) * DH]
+            if held < stripe:
+                out_ref[:, held * MAIN :, :] = over_ref[...].astype(BF16)
 
 
 def experts_of(packed, w_gate, w_up, w_down):
     sources = packed.shape[0]
     width, hidden_units = w_gate.shape
     tile = 256
-    columns = 512
+    steps = packed.shape[1] // STRIPE
     up_steps = hidden_units // tile
-    steps = up_steps + width // columns
     rows = sources * CAP
 
+    def out_step(step):
+        return jnp.maximum(step - steps - up_steps, 0)
+
     def up_map(step):
-        return 0, jnp.minimum(step, up_steps - 1)
-
-    def down_map(step):
-        return 0, jnp.maximum(step - up_steps, 0)
-
-    def whole(step):
-        return 0, 0, 0
+        return 0, jnp.clip(step - steps, 0, up_steps - 1)
 
     return pl.pallas_call(
-        functools.partial(expert_kernel, up_steps=up_steps),
-        grid=(steps,),
+        functools.partial(expert_kernel, steps=steps, up_steps=up_steps),
+        grid=(2 * steps + up_steps,),
         in_specs=[
-            pl.BlockSpec(packed.shape, whole),
+            pl.BlockSpec((sources, STRIPE, DH), lambda step: (0, jnp.minimum(step, steps - 1), 0)),
             pl.BlockSpec((width, tile), up_map),
             pl.BlockSpec((width, tile), up_map),
-            pl.BlockSpec((hidden_units, columns), down_map),
+            pl.BlockSpec((hidden_units, STRIPE // MAIN * DH), lambda step: (0, out_step(step))),
         ],
-        out_specs=pl.BlockSpec(packed.shape, whole),
+        out_specs=pl.BlockSpec((sources, STRIPE, DH), lambda step: (0, out_step(step), 0)),
         out_shape=jax.ShapeDtypeStruct(packed.shape, BF16),
         scratch_shapes=[
             pltpu.VMEM((rows, width), BF16),
@@ -525,48 +558,72 @@
     )(packed, w_gate, w_up, w_down)
 
 
-def combine_kernel(slot_ref, route_ref, in_ref, h1_ref, out_ref, over_ref):
-    slot = slot_ref[...]
-    route = route_ref[...]
-    wanted = lax.broadcasted_iota(jnp.int32, (BLOCK, MAIN, BLOCK), 1).astype(F32)
-    mix = jnp.where(slot[:, None, :] == wanted, route[:, None, :], 0.0)
-    mix = mix.reshape(BLOCK * MAIN, BLOCK).astype(BF16)
-    last = jnp.where(slot == float(MAIN), route, 0.0).astype(BF16)
-    tiles = h1_ref.shape[1] // DH
-    over_ref[...] = in_ref[:, tiles * MAIN :, :].astype(F32)
-
-    def mixed(weights, rows):
-        return lax.dot_general(
-            weights, rows, (((0,), (0,)), ((), ())), preferred_element_type=F32
-        )
-
-    per = 2
-    for place in range(0, tiles, per):
-        columns = pl.ds(place * DH, per * DH)
-        spots = range(place, place + per)
-        rows = jnp.concatenate(
-            [
-                in_ref[:, p * MAIN : (p + 1) * MAIN, :].reshape(BLOCK * MAIN, DH)
-                for p in spots
-            ],
-            axis=1,
-        )
-        extra = jnp.concatenate([over_ref[:, p, :].astype(BF16) for p in spots], axis=1)
-        total = mixed(mix, rows) + mixed(last, extra)
-        out_ref[:, columns] = (total + h1_ref[:, columns].astype(F32)).astype(BF16)
+def combine_kernel(
+    slot_ref, route_ref, in_ref, in_over_ref, h1_ref, out_ref, mix_ref, last_ref, over_ref, *, tiles
+):
+    step = pl.program_id(0)
+    stripe = in_ref.shape[1] // MAIN
+
+    @pl.when(step == 0)
+    def _():
+        slot = slot_ref[...]
+        route = route_ref[...]
+        wanted = lax.broadcasted_iota(jnp.int32, (BLOCK, MAIN, BLOCK), 1).astype(F32)
+        mix = jnp.where(slot[:, None, :] == wanted, route[:, None, :], 0.0)
+        mix_ref[...] = jnp.transpose(mix.reshape(BLOCK * MAIN, BLOCK).astype(BF16))
+        last_ref[...] = jnp.transpose(jnp.where(slot == float(MAIN), route, 0.0)).astype(BF16)
+        over_ref[...] = in_over_ref[...].astype(F32)
+
+    for index in range(pl.cdiv(tiles, stripe)):
+
+        @pl.when(step == index)
+        def _(index=index):
+            first = index * stripe
+            held = min(stripe, tiles - first)
+            rows = jnp.concatenate(
+                [
+                    in_ref[:, p * MAIN : (p + 1) * MAIN, :].reshape(BLOCK * MAIN, DH)
+                    for p in range(held)
+                ],
+                axis=1,
+            )
+            extra = jnp.concatenate(
+                [over_ref[:, first + p, :].astype(BF16) for p in range(held)], axis=1
+            )
+            total = jnp.dot(mix_ref[...], rows, preferred_element_type=F32)
+            total = total + jnp.dot(last_ref[...], extra, preferred_element_type=F32)
+            columns = slice(first * DH, (first + held) * DH)
+            out_ref[:, columns] = (total + h1_ref[:, columns].astype(F32)).astype(BF16)
 
 
 def combine(slot, route, packed, h1):
-    vmem = pl.BlockSpec(memory_space=pltpu.VMEM)
+    rows, width = h1.shape
+    experts = packed.shape[0]
+    tiles = width // DH
+
+    def whole(shape):
+        return pl.BlockSpec(shape, lambda step: (0,) * len(shape))
+
     return pl.pallas_call(
-        combine_kernel,
-        in_specs=[vmem] * 4,
-        out_specs=vmem,
-        out_shape=jax.ShapeDtypeStruct(h1.shape, BF16),
-        scratch_shapes=[pltpu.VMEM((packed.shape[0], h1.shape[1] // DH, DH), F32)],
-        compiler_params=params(),
+        functools.partial(combine_kernel, tiles=tiles),
+        grid=(packed.shape[1] // STRIPE,),
+        in_specs=[
+            whole(slot.shape),
+            whole(route.shape),
+            pl.BlockSpec((experts, STRIPE, DH), lambda step: (0, step, 0)),
+            pl.BlockSpec((experts, tiles, DH), lambda step: (0, MAIN, 0)),
+            whole(h1.shape),
+        ],
+        out_specs=whole(h1.shape),
+        out_shape=jax.ShapeDtypeStruct((rows, width), BF16),
+        scratch_shapes=[
+            pltpu.VMEM((rows, experts * MAIN), BF16),
+            pltpu.VMEM((rows, experts), BF16),
+            pltpu.VMEM((experts, tiles, DH), F32),
+        ],
+        compiler_params=params("arbitrary"),
         name="combine",
-    )(slot, route, packed, h1)
+    )(slot, route, packed, packed, h1)
 
 
 def exchange(packed):
@@ -588,7 +645,8 @@
 
 def ring_gather(piece, axes):
     left, right = ring_near(piece, axes)
-    return jnp.concatenate([piece, left, right, *ring_far(left, right, axes)], axis=0)
+    far = lax.ppermute(piece, axes, [(i, (i + 2) % 4) for i in range(4)])
+    return jnp.concatenate([piece, left, right, far], axis=0)
 
 
 def local(
@@ -633,10 +691,10 @@
     )
     got = lax.ppermute(theirs, AXES, mirror)
     part = project_own(core_arr, own, w_out)
-    h1, slot, route, send = project(
+    h1, slot, route, packed = project(
         core_arr, part, got, w_out, hidden, norm_gain[None, :], w_router, expert_ids.T
     )
-    returned = exchange(experts_of(exchange(send), w_gate[0], w_up[0], w_down[0]))
+    returned = exchange(experts_of(exchange(packed), w_gate[0], w_up[0], w_down[0]))
     return combine(slot, route, returned, h1)
 
 

time: 294 us -> 298 us (1.014)
  waiting for transfers between devices: 15.3 us -> 30.6 us
  local copies, waits for them, and re-layouts: 10.8 us -> 4.79 us
  starting transfers between devices: 39.6 us -> 34.3 us
    ppermute x4, waiting for transfers between devices: 0.01 us -> 7.74 us  [ring_near(): right = lax.ppermute(piece, axes, [(i, (i + 3) % 4) for i in range(4)])]
    unnamed x18 -> x12, local copies, waits for them, and re-layouts: 7.16 us -> 1.48 us
    ppermute x4, waiting for transfers between devices: 12.8 us -> 18.4 us  [ring_near(): left = lax.ppermute(piece, axes, [(i, (i + 1) % 4) for i in range(4)])]
    ppermute x4 -> x2, starting transfers between devices: 7.38 us -> 3.1 us  [ring_far(): lax.ppermute(right[half:], axes, [(i, (i + 3) % 4) for i in range(4)])]
    ppermute x1, starting transfers between devices: 9.37 us -> 5.46 us  [local(): got = lax.ppermute(theirs, AXES, mirror)]
  transfers between devices with their start and end apart: 19 -> 17, of which waited for: 5 -> 6; matrix products, arithmetic and copies ran while one was open for 3% -> 1% of each run, Pallas kernels for 12% -> 12%
where the time goes in v4:
time: 298 us; the launch traced here: 296 us
  blocking collectives  141 us (47%)
  Pallas kernels  81.8 us (27%)
  starting transfers between devices  34.3 us (12%)
  waiting for transfers between devices  30.6 us (10%)
  local copies, waits for them, and re-layouts  4.79 us (2%)
    all_to_all x2, blocking collectives, exchange(): return lax.all_to_all(packed, AXES, split_axis=0, concat_axis=0, tiled=True)  130 us
    pallas_call x3, Pallas kernels, attend(): pl.pallas_call(kernel, in_specs=[pl.BlockSpec(memory_space=pltpu.SMEM), v...  41.8 us
    pallas_call x1, Pallas kernels, experts_of(): pl.pallas_call(functools.partial(expert_kernel, steps=steps, up_steps=up_...  20.2 us
    ppermute x4, waiting for transfers between devices, ring_near(): left = lax.ppermute(piece, axes, [(i, (i + 1) % 4) for i in range(4)])  18.4 us
    all_gather x1, blocking collectives, local(): row = lax.all_gather(chip, ('x',), axis=0)  11.2 us
    ppermute x1, starting transfers between devices, local(): taken = lax.ppermute(give, AXES, mirror)  9.13 us
    pallas_call x1, Pallas kernels, project(): pl.pallas_call(functools.partial(project_kernel, steps=steps), grid_spec=...  8.32 us
    ppermute x4, starting transfers between devices, ring_near(): right = lax.ppermute(piece, axes, [(i, (i + 3) % 4) for i in range(4)])  8 us
  transfers between devices with their start and end apart: 17, of which 6 were waited for; matrix products, arithmetic and copies ran while one was open for 1% of the time, Pallas kernels for 12%

profile of v4, /device:TPU:9, one launch (start us, length us, event | category | flops | bytes accessed | tf_op | source)
XLA Modules:
  0.0 295.6 jit_solution(8294794268925975740)
XLA Ops:
  0.1 0.3 fusion.2
  0.4 0.8 pad_maximum_fusion.3
  1.1 2.2 rotate_all.1
  3.3 0.7 collective-permute-start.1
  4.0 1.1 collective-permute-done.1
  5.1 0.9 broadcast_select_fusion.1
  6.0 11.2 %all-gather = bf16[1024,256]{1,0:T(8,128)(2,1)S(1)} all-gather(bf16[256,256]{1,0:T(8,128)(2,1)S(1)} %pad_maximum_fusion.2), channel_id=2, replica_groups=mesh['zh'=2,'y'=4,'c'=2,'zl'=2,'x'=4] {'x'}, dimensions={0}, use_global_device_ids=true | all-gather | bytes 655360 | tf_op jit(solution)/shard_map/all_gather | solution.py:669
  17.2 3.8 %collective-permute-start.10 = (bf16[512,256]{1,0:T(8,128)(2,1)S(1)}, bf16[512,256]{1,0:T(8,128)(2,1)S(1)}, u32[]{:S(2)}, u32[]{:S(2)}) collective-permute-start(bf16[512,256]{1,0:T(8,128)(2,1)S(1)} %bitcast.21), channel_id=1, source_target_pairs={{0,68},{4,0},{64,4},{68,64},{1,69},{5,1},{65,5},{69,65},{2,70},{6,... | collective-permute-start | bytes 786440 | tf_op jit(solution)/shard_map/ppermute | solution.py:635
  21.1 0.7 collective-permute-start.9
  21.8 1.3 collective-permute-start.2
  23.1 0.2 collective-permute-start.3
  23.2 7.7 %collective-permute-done.10 = bf16[512,256]{1,0:T(8,128)(2,1)S(1)} collective-permute-done((bf16[512,256]{1,0:T(8,128)(2,1)S(1)}, bf16[512,256]{1,0:T(8,128)(2,1)S(1)}, u32[]{:S(2)}, u32[]{:S(2)}) %collective-permute-start.10) | collective-permute-done | bytes 262176 | tf_op jit(solution)/shard_map/ppermute | solution.py:635
  31.0 2.0 collective-permute-start.4
  33.0 0.0 collective-permute-done.11
  33.0 2.8 collective-permute-done.9
  35.8 0.1 pad_maximum_fusion.1.refs_1_
  35.9 1.4 collective-permute-start.12
  37.3 0.2 collective-permute-start.14
  37.5 0.6 collective-permute-done.4
  38.1 0.1 pad_maximum_fusion.refs_0_
  38.2 0.1 collective-permute-start.5
  38.3 3.8 %collective-permute-start.7 = (bf16[2048,256]{1,0:T(8,128)(2,1)S(1)}, bf16[2048,256]{1,0:T(8,128)(2,1)}, u32[]{:S(2)}, u32[]{:S(2)}) collective-permute-start(bf16[2048,256]{1,0:T(8,128)(2,1)S(1)} %pad_maximum_fusion.refs_0_), channel_id=1, source_target_pairs={{0,68},{4,0},{64,4},{68,64},{1,69},{5,1},{65,5},{69,65},{2,70},{6,... | collective-permute-start | bytes 3145736 | tf_op jit(solution)/shard_map/ppermute | solution.py:635
  42.1 9.1 %collective-permute-start = (bf16[128,1024]{1,0:T(8,128)(2,1)S(1)}, bf16[128,1024]{1,0:T(8,128)(2,1)}, u32[]{:S(2)}, u32[]{:S(2)}) collective-permute-start(bf16[128,1024]{1,0:T(8,128)(2,1)S(1)} %copy-done.5), channel_id=1, source_target_pairs={{0,127},{1,126},{2,125},{3,124},{4,123},{5,122},{6,121},{7,120},{8... | collective-permute-start | bytes 786440 | tf_op jit(solution)/shard_map/ppermute | solution.py:663
  51.2 0.6 pad_add_fusion.meta_ref
  51.8 15.6 %collective-permute-done.12.refs_2_ = bf16[2048,256]{1,0:T(8,128)(2,1)S(1)} collective-permute-done((bf16[2048,256]{1,0:T(8,128)(2,1)S(1)}, bf16[2048,256]{1,0:T(8,128)(2,1)S(1)}, u32[]{:S(2)}, u32[]{:S(2)}) %collective-permute-start.12) | collective-permute-done | bytes 1048608 | tf_op jit(solution)/shard_map/ppermute | solution.py:634
  67.4 2.4 collective-permute-start.13
  69.8 1.1 slice.29
  70.9 0.1 collective-permute-start.15
  71.0 0.0 collective-permute-done.5.refs_0_
  71.0 1.1 slice.25
  72.1 0.1 collective-permute-start.6
  72.2 0.0 collective-permute-done.7.refs_1_
  72.2 1.1 slice.26
  73.3 3.0 %collective-permute-start.8 = (bf16[1024,256]{1,0:T(8,128)(2,1)S(1)}, bf16[1024,256]{1,0:T(8,128)(2,1)}, u32[]{:S(2)}, u32[]{:S(2)}) collective-permute-start(bf16[1024,256]{1,0:T(8,128)(2,1)S(1)} %slice.26), channel_id=1, source_target_pairs={{0,68},{4,0},{64,4},{68,64},{1,69},{5,1},{65,5},{69,65},{2,70},{6,... | collective-permute-start | bytes 1572872 | tf_op jit(solution)/shard_map/ppermute | solution.py:642
  76.3 13.3 %attend_first.1 = (f32[2048,128]{1,0:T(8,128)}, f32[2048,128]{1,0:T(8,128)}, f32[2048,128]{1,0:T(8,128)}) custom-call(s32[4]{0:T(128)} %pad_add_fusion.meta_ref, bf16[128,1024]{1,0:T(8,128)(2,1)} %collective-permute-done.theirs_ref, bf16[128,1024]{1,0:T(8,128)(2,1)} %get-tuple-element.22.own_ref, bf16[2048,256]{1,0:T(8,128)(2,1)} %copy-done.1, ...), custom_call_target="tpu_custom_call" | custom-call | flops 2147483648 | bytes 2097152 | tf_op jit(solution)/shard_map/attend_first/pallas_call | solution.py:280
  89.6 19.2 %attend_more.1 = (f32[2048,128]{1,0:T(8,128)}, f32[2048,128]{1,0:T(8,128)}, f32[2048,128]{1,0:T(8,128)}) custom-call(s32[4]{0:T(128)} %pad_add_fusion.meta_ref, bf16[128,1024]{1,0:T(8,128)(2,1)} %collective-permute-done.theirs_ref, bf16[128,1024]{1,0:T(8,128)(2,1)} %get-tuple-element.22.own_ref, bf16[2048,256]{1,0:T(8,128)(2,1)} %collective-permute-done.5.refs_0_, ...), custom_call_target="tpu_custom_call" | custom-call | flops 4294967296 | bytes 4194304 | tf_op jit(solution)/shard_map/attend_more/pallas_call | solution.py:280
  108.9 0.0 copy-start.4
  108.9 0.8 copy-done.4
  109.7 9.3 %attend_last.1 = (bf16[128,1024]{1,0:T(8,128)(2,1)}, bf16[128,1024]{1,0:T(8,128)(2,1)}) custom-call(s32[4]{0:T(128)} %pad_add_fusion.meta_ref, bf16[128,1024]{1,0:T(8,128)(2,1)} %collective-permute-done.theirs_ref, bf16[128,1024]{1,0:T(8,128)(2,1)} %get-tuple-element.22.own_ref, bf16[1024,256]{1,0:T(8,128)(2,1)} %collective-permute-done.6.refs_0_, ...), custom_call_target="tpu_custom_call" | custom-call | flops 2147483648 | bytes 2097152 | tf_op jit(solution)/shard_map/attend_last/pallas_call | solution.py:280
  119.0 5.5 %collective-permute-start.16 = (bf16[128,1024]{1,0:T(8,128)(2,1)}, bf16[128,1024]{1,0:T(8,128)(2,1)S(1)}, u32[]{:S(2)}, u32[]{:S(2)}) collective-permute-start(bf16[128,1024]{1,0:T(8,128)(2,1)} %get-tuple-element.32), channel_id=1, source_target_pairs={{0,127},{1,126},{2,125},{3,124},{4,123},{5,122},{6,121},{7,120},{8... | collective-permute-start | bytes 786440 | tf_op jit(solution)/shard_map/ppermute | solution.py:692
  124.5 3.8 %project_own.1.part_ref = f32[128,2048]{1,0:T(8,128)} custom-call(s32[1]{0:T(128)} %bitcast.core_ref, bf16[128,1024]{1,0:T(8,128)(2,1)} %get-tuple-element.31.own_ref, bf16[2048,2048]{1,0:T(8,128)(2,1)} %w_ref.3), custom_call_target="tpu_custom_call" | custom-call | flops 536870912 | bytes 4194304 | tf_op jit(solution)/shard_map/project_own/pallas_call | solution.py:327
  128.2 2.7 collective-permute-done.16.got_ref
  130.9 0.7 copy-done.2
  131.6 8.3 %project.1 = (bf16[128,2048]{1,0:T(8,128)(2,1)}, f32[128,128]{1,0:T(8,128)}, f32[128,128]{1,0:T(8,128)}, bf16[128,144,128]{2,1,0:T(8,128)(2,1)}) custom-call(s32[1]{0:T(128)} %bitcast.core_ref, f32[128,2048]{1,0:T(8,128)} %project_own.1.part_ref, bf16[128,1024]{1,0:T(8,128)(2,1)} %copy-done.2, bf16[2048,2048]{1,0:T(8,128)(2,1)} %w_ref.3, ...), custom_call_target="tpu_custom_call" | custom-call | tf_op jit(solution)/shard_map/project/pallas_call | solution.py:423
  139.9 66.0 %all_to_all.10.in_ref = bf16[128,144,128]{2,1,0:T(8,128)(2,1)} all-to-all(bf16[128,144,128]{2,1,0:T(8,128)(2,1)} %get-tuple-element.35), channel_id=1, replica_groups=mesh['zh'=2,'y'=4,'c'=2,'zl'=2,'x'=4] {'zh','y','c','zl','x'}, dimensions={0} | all-to-all | bytes 9437184 | tf_op jit(solution)/shard_map/all_to_all | solution.py:630
  205.9 20.2 %experts_of.1 = bf16[128,144,128]{2,1,0:T(8,128)(2,1)} custom-call(bf16[128,144,128]{2,1,0:T(8,128)(2,1)} %all_to_all.10.in_ref, bf16[2048,768]{1,0:T(8,128)(2,1)} %bitcast.13, bf16[2048,768]{1,0:T(8,128)(2,1)} %bitcast.14, bf16[768,2048]{1,0:T(8,128)(2,1)} %bitcast.15), custom_call_target="tpu_custom_call" | custom-call | tf_op jit(solution)/shard_map/experts_of/pallas_call | solution.py:540
  226.0 64.0 %all_to_all.11.in_ref.in_over_ref = bf16[128,144,128]{2,1,0:T(8,128)(2,1)} all-to-all(bf16[128,144,128]{2,1,0:T(8,128)(2,1)} %experts_of.1), channel_id=1, replica_groups=mesh['zh'=2,'y'=4,'c'=2,'zl'=2,'x'=4] {'zh','y','c','zl','x'}, dimensions={0} | all-to-all | bytes 9437184 | tf_op jit(solution)/shard_map/all_to_all | solution.py:630
  290.0 5.5 %combine.1 = bf16[128,2048]{1,0:T(8,128)(2,1)} custom-call(f32[128,128]{1,0:T(8,128)} %get-tuple-element.33.slot_ref, f32[128,128]{1,0:T(8,128)} %get-tuple-element.34.route_ref, bf16[128,144,128]{2,1,0:T(8,128)(2,1)} %all_to_all.11.in_ref.in_over_ref, bf16[128,144,128]{2,1,0:T(8,128)(2,1)} %all_to_all.11.in_ref.in_over_ref, ...), custom_call_target="tpu_custom_call" | custom-call | tf_op jit(solution)/shard_map/combine/pallas_call | solution.py:607
  (23 shorter events, 0.1 us)
Async XLA Ops:
  3.3 1.8 collective-permute-start.1
  17.2 13.7 %collective-permute-start.10 = (bf16[512,256]{1,0:T(8,128)(2,1)S(1)}, bf16[512,256]{1,0:T(8,128)(2,1)S(1)}, u32[]{:S(2)}, u32[]{:S(2)}) collective-permute-start(bf16[512,256]{1,0:T(8,128)(2,1)S(1)} %bitcast.21), channel_id=1, source_target_pairs={{0,68},{4,0},{64,4},{68,64},{1,69},{5,1},{65,5},{69,65},{2,70},{6,... | collective-permute-start | bytes 786440 | tf_op jit(solution)/shard_map/ppermute | solution.py:635
  21.1 11.9 %collective-permute-start.11 = (bf16[512,256]{1,0:T(8,128)(2,1)S(1)}, bf16[512,256]{1,0:T(8,128)(2,1)S(1)}, u32[]{:S(2)}, u32[]{:S(2)}) collective-permute-start(bf16[512,256]{1,0:T(8,128)(2,1)S(1)} %bitcast.22), channel_id=1, source_target_pairs={{0,64},{4,68},{64,0},{68,4},{1,65},{5,69},{65,1},{69,5},{2,66},{6,... | collective-permute-start | bytes 786440 | tf_op jit(solution)/shard_map/ppermute | solution.py:648
  21.1 14.8 %collective-permute-start.9 = (bf16[512,256]{1,0:T(8,128)(2,1)S(1)}, bf16[512,256]{1,0:T(8,128)(2,1)S(1)}, u32[]{:S(2)}, u32[]{:S(2)}) collective-permute-start(bf16[512,256]{1,0:T(8,128)(2,1)S(1)} %bitcast.23), channel_id=1, source_target_pairs={{0,4},{4,64},{64,68},{68,0},{1,5},{5,65},{65,69},{69,1},{2,6},{6,6... | collective-permute-start | bytes 786440 | tf_op jit(solution)/shard_map/ppermute | solution.py:634
  21.8 20.3 %copy-start.5 = (bf16[128,1024]{1,0:T(8,128)(2,1)S(1)}, bf16[128,1024]{1,0:T(8,128)(2,1)}, u32[]{:S(2)}) copy-start(bf16[128,1024]{1,0:T(8,128)(2,1)} %get-tuple-element.21) | copy-start | bytes 786436
  21.8 15.7 %collective-permute-start.2 = (bf16[512,256]{1,0:T(8,128)(2,1)S(1)}, bf16[512,256]{1,0:T(8,128)(2,1)S(1)}, u32[]{:S(2)}, u32[]{:S(2)}) collective-permute-start(bf16[512,256]{1,0:T(8,128)(2,1)S(1)} %bitcast.17), channel_id=1, source_target_pairs={{0,16},{16,32},{32,48},{48,0},{1,17},{17,33},{33,49},{49,1},{2,18}... | collective-permute-start | bytes 786440 | tf_op jit(solution)/shard_map/ppermute | solution.py:634
  23.1 14.4 %collective-permute-start.3 = (bf16[512,256]{1,0:T(8,128)(2,1)S(1)}, bf16[512,256]{1,0:T(8,128)(2,1)S(1)}, u32[]{:S(2)}, u32[]{:S(2)}) collective-permute-start(bf16[512,256]{1,0:T(8,128)(2,1)S(1)} %bitcast.18), channel_id=1, source_target_pairs={{0,48},{16,0},{32,16},{48,32},{1,49},{17,1},{33,17},{49,33},{2,50}... | collective-permute-start | bytes 786440 | tf_op jit(solution)/shard_map/ppermute | solution.py:635
  31.0 7.1 %collective-permute-start.4 = (bf16[512,256]{1,0:T(8,128)(2,1)S(1)}, bf16[512,256]{1,0:T(8,128)(2,1)S(1)}, u32[]{:S(2)}, u32[]{:S(2)}) collective-permute-start(bf16[512,256]{1,0:T(8,128)(2,1)S(1)} %bitcast.19), channel_id=1, source_target_pairs={{0,32},{16,48},{32,0},{48,16},{1,33},{17,49},{33,1},{49,17},{2,34}... | collective-permute-start | bytes 786440 | tf_op jit(solution)/shard_map/ppermute | solution.py:648
  35.9 35.0 %copy-start = (bf16[2048,256]{1,0:T(8,128)(2,1)}, bf16[2048,256]{1,0:T(8,128)(2,1)S(1)}, u32[]{:S(2)}) copy-start(bf16[2048,256]{1,0:T(8,128)(2,1)S(1)} %pad_maximum_fusion.1.refs_1_) | copy-start | bytes 3145732
  35.9 31.5 %collective-permute-start.12 = (bf16[2048,256]{1,0:T(8,128)(2,1)S(1)}, bf16[2048,256]{1,0:T(8,128)(2,1)S(1)}, u32[]{:S(2)}, u32[]{:S(2)}) collective-permute-start(bf16[2048,256]{1,0:T(8,128)(2,1)S(1)} %pad_maximum_fusion.1.refs_1_), channel_id=1, source_target_pairs={{0,16},{16,32},{32,48},{48,0},{1,17},{17,33},{33,49},{49,1},{2,18}... | collective-permute-start | bytes 3145736 | tf_op jit(solution)/shard_map/ppermute | solution.py:634
  37.3 32.5 %collective-permute-start.14 = (bf16[2048,256]{1,0:T(8,128)(2,1)S(1)}, bf16[2048,256]{1,0:T(8,128)(2,1)}, u32[]{:S(2)}, u32[]{:S(2)}) collective-permute-start(bf16[2048,256]{1,0:T(8,128)(2,1)S(1)} %pad_maximum_fusion.1.refs_1_), channel_id=1, source_target_pairs={{0,48},{16,0},{32,16},{48,32},{1,49},{17,1},{33,17},{49,33},{2,50}... | collective-permute-start | bytes 3145736 | tf_op jit(solution)/shard_map/ppermute | solution.py:635
  38.2 35.1 %copy-start.1 = (bf16[2048,256]{1,0:T(8,128)(2,1)}, bf16[2048,256]{1,0:T(8,128)(2,1)S(1)}, u32[]{:S(2)}) copy-start(bf16[2048,256]{1,0:T(8,128)(2,1)S(1)} %pad_maximum_fusion.refs_0_) | copy-start | bytes 3145732
  38.2 32.8 %collective-permute-start.5 = (bf16[2048,256]{1,0:T(8,128)(2,1)S(1)}, bf16[2048,256]{1,0:T(8,128)(2,1)}, u32[]{:S(2)}, u32[]{:S(2)}) collective-permute-start(bf16[2048,256]{1,0:T(8,128)(2,1)S(1)} %pad_maximum_fusion.refs_0_), channel_id=1, source_target_pairs={{0,4},{4,64},{64,68},{68,0},{1,5},{5,65},{65,69},{69,1},{2,6},{6,6... | collective-permute-start | bytes 3145736 | tf_op jit(solution)/shard_map/ppermute | solution.py:634
  38.3 33.9 %collective-permute-start.7 = (bf16[2048,256]{1,0:T(8,128)(2,1)S(1)}, bf16[2048,256]{1,0:T(8,128)(2,1)}, u32[]{:S(2)}, u32[]{:S(2)}) collective-permute-start(bf16[2048,256]{1,0:T(8,128)(2,1)S(1)} %pad_maximum_fusion.refs_0_), channel_id=1, source_target_pairs={{0,68},{4,0},{64,4},{68,64},{1,69},{5,1},{65,5},{69,65},{2,70},{6,... | collective-permute-start | bytes 3145736 | tf_op jit(solution)/shard_map/ppermute | solution.py:635
  42.1 34.2 %collective-permute-start = (bf16[128,1024]{1,0:T(8,128)(2,1)S(1)}, bf16[128,1024]{1,0:T(8,128)(2,1)}, u32[]{:S(2)}, u32[]{:S(2)}) collective-permute-start(bf16[128,1024]{1,0:T(8,128)(2,1)S(1)} %copy-done.5), channel_id=1, source_target_pairs={{0,127},{1,126},{2,125},{3,124},{4,123},{5,122},{6,121},{7,120},{8... | collective-permute-start | bytes 786440 | tf_op jit(solution)/shard_map/ppermute | solution.py:663
  67.4 2.4 copy-start.3
  67.4 41.4 %collective-permute-start.13 = (bf16[1024,256]{1,0:T(8,128)(2,1)S(1)}, bf16[1024,256]{1,0:T(8,128)(2,1)}, u32[]{:S(2)}, u32[]{:S(2)}) collective-permute-start(bf16[1024,256]{1,0:T(8,128)(2,1)S(1)} %slice.28), channel_id=1, source_target_pairs={{0,16},{16,32},{32,48},{48,0},{1,17},{17,33},{33,49},{49,1},{2,18}... | collective-permute-start | bytes 1572872 | tf_op jit(solution)/shard_map/ppermute | solution.py:641
  70.9 38.0 %collective-permute-start.15 = (bf16[1024,256]{1,0:T(8,128)(2,1)S(1)}, bf16[1024,256]{1,0:T(8,128)(2,1)S(1)}, u32[]{:S(2)}, u32[]{:S(2)}) collective-permute-start(bf16[1024,256]{1,0:T(8,128)(2,1)S(1)} %slice.29), channel_id=1, source_target_pairs={{0,48},{16,0},{32,16},{48,32},{1,49},{17,1},{33,17},{49,33},{2,50}... | collective-permute-start | bytes 1572872 | tf_op jit(solution)/shard_map/ppermute | solution.py:642
  72.1 36.8 %collective-permute-start.6 = (bf16[1024,256]{1,0:T(8,128)(2,1)S(1)}, bf16[1024,256]{1,0:T(8,128)(2,1)}, u32[]{:S(2)}, u32[]{:S(2)}) collective-permute-start(bf16[1024,256]{1,0:T(8,128)(2,1)S(1)} %slice.25), channel_id=1, source_target_pairs={{0,4},{4,64},{64,68},{68,0},{1,5},{5,65},{65,69},{69,1},{2,6},{6,6... | collective-permute-start | bytes 1572872 | tf_op jit(solution)/shard_map/ppermute | solution.py:641
  73.3 35.6 %collective-permute-start.8 = (bf16[1024,256]{1,0:T(8,128)(2,1)S(1)}, bf16[1024,256]{1,0:T(8,128)(2,1)}, u32[]{:S(2)}, u32[]{:S(2)}) collective-permute-start(bf16[1024,256]{1,0:T(8,128)(2,1)S(1)} %slice.26), channel_id=1, source_target_pairs={{0,68},{4,0},{64,4},{68,64},{1,69},{5,1},{65,5},{69,65},{2,70},{6,... | collective-permute-start | bytes 1572872 | tf_op jit(solution)/shard_map/ppermute | solution.py:642
  108.9 0.8 copy-start.4
  119.0 11.9 %collective-permute-start.16 = (bf16[128,1024]{1,0:T(8,128)(2,1)}, bf16[128,1024]{1,0:T(8,128)(2,1)S(1)}, u32[]{:S(2)}, u32[]{:S(2)}) collective-permute-start(bf16[128,1024]{1,0:T(8,128)(2,1)} %get-tuple-element.32), channel_id=1, source_target_pairs={{0,127},{1,126},{2,125},{3,124},{4,123},{5,122},{6,121},{7,120},{8... | collective-permute-start | bytes 786440 | tf_op jit(solution)/shard_map/ppermute | solution.py:692
  130.9 0.7 copy-start.2

commit v5 on v4

--- a/solution.py
+++ b/solution.py
@@ -20,6 +20,7 @@
 FAR = 1 << 20
 TILE_HEADS = 4
 AXES = ("zh", "y", "c", "zl", "x")
+TORUS = ("zh", "zl", "y", "x", "c")
 RING_Z = ("zh", "zl")
 RING_Y = ("y",)
 OFFSETS = (0, -1, 1, 2)
@@ -344,9 +345,73 @@
     )(core, own, w_out)
 
 
+def torus_place(expert):
+    zh, y, c = expert // 64, expert // 16 % 4, expert // 8 % 2
+    zl, x = expert // 4 % 2, expert % 4
+    return zh * 64 + zl * 32 + y * 8 + x * 2 + c
+
+
+def plan_kernel(ids_ref, slot_ref, pick_ref, last_ref):
+    slot = slots_of(ids_ref)[1]
+    slot_ref[...] = slot
+    wanted = lax.broadcasted_iota(jnp.int32, (BLOCK, MAIN, BLOCK), 1).astype(F32)
+    pick = jnp.where(slot[:, None, :] == wanted, 1.0, 0.0).reshape(BLOCK * MAIN, BLOCK)
+    pick_ref[...] = pick.astype(BF16)
+    last_ref[...] = jnp.where(slot == float(MAIN), 1.0, 0.0).astype(BF16)
+
+
+def plan(places_t):
+    rows = places_t.shape[1]
+    vmem = pl.BlockSpec(memory_space=pltpu.VMEM)
+    return pl.pallas_call(
+        plan_kernel,
+        in_specs=[vmem],
+        out_specs=[vmem] * 3,
+        out_shape=[
+            jax.ShapeDtypeStruct((BLOCKS, rows), F32),
+            jax.ShapeDtypeStruct((BLOCKS * MAIN, rows), BF16),
+            jax.ShapeDtypeStruct((BLOCKS, rows), BF16),
+        ],
+        compiler_params=params(),
+        name="plan",
+    )(places_t)
+
+
+def routes_kernel(hn_ref, router_ref, ids_ref, slot_ref, mix_ref, last_ref):
+    logits = jnp.dot(hn_ref[...], router_ref[...], preferred_element_type=F32)
+    named = slots_of(ids_ref)[0]
+    raised = jnp.where(named > 0.0, jnp.exp(jnp.transpose(logits)), 0.0)
+    by_expert = (raised / jnp.sum(raised, axis=0, keepdims=True)).astype(BF16)
+    shape = (BLOCK, BLOCK)
+    place = torus_place(lax.broadcasted_iota(jnp.int32, shape, 1))
+    order = jnp.where(place == lax.broadcasted_iota(jnp.int32, shape, 0), 1.0, 0.0)
+    route = jnp.dot(order.astype(BF16), by_expert, preferred_element_type=F32)
+    slot = slot_ref[...]
+    wanted = lax.broadcasted_iota(jnp.int32, (BLOCK, MAIN, BLOCK), 1).astype(F32)
+    mix = jnp.where(slot[:, None, :] == wanted, route[:, None, :], 0.0)
+    mix_ref[...] = jnp.transpose(mix.reshape(BLOCK * MAIN, BLOCK).astype(BF16))
+    last_ref[...] = jnp.transpose(jnp.where(slot == float(MAIN), route, 0.0)).astype(BF16)
+
+
+def routes(hn, w_router, ids_t, slot):
+    rows = hn.shape[0]
+    vmem = pl.BlockSpec(memory_space=pltpu.VMEM)
+    return pl.pallas_call(
+        routes_kernel,
+        in_specs=[vmem] * 4,
+        out_specs=[vmem] * 2,
+        out_shape=[
+            jax.ShapeDtypeStruct((rows, BLOCKS * MAIN), BF16),
+            jax.ShapeDtypeStruct((rows, BLOCKS), BF16),
+        ],
+        compiler_params=params(),
+        name="routes",
+    )(hn, w_router, ids_t, slot)
+
+
 def project_kernel(
-    core_ref, part_ref, got_ref, w_ref, hidden_ref, gain_ref, router_ref, ids_ref,
-    h1_ref, slot_ref, route_ref, send_ref, acc_ref, hn_ref, pick_ref, over_ref, *, steps,
+    core_ref, part_ref, got_ref, w_ref, hidden_ref, gain_ref, pick_ref, last_ref,
+    h1_ref, hn_ref, send_ref, acc_ref, over_ref, *, steps,
 ):
     step = pl.program_id(0)
     depth = w_ref.shape[0]
@@ -369,18 +434,9 @@
         mean = jnp.mean(h1_f * h1_f, axis=-1, keepdims=True)
         hn = (h1_f / jnp.sqrt(mean + 1e-06) * gain_ref[...]).astype(BF16)
         hn_ref[...] = hn
-        logits = jnp.dot(hn, router_ref[...], preferred_element_type=F32)
-        named, slot = slots_of(ids_ref)
-        slot_ref[...] = slot
-        raised = jnp.where(named > 0.0, jnp.exp(jnp.transpose(logits)), 0.0)
-        route_ref[...] = raised / jnp.sum(raised, axis=0, keepdims=True)
-        wanted = lax.broadcasted_iota(jnp.int32, (BLOCK, MAIN, BLOCK), 1).astype(F32)
-        pick = jnp.where(slot[:, None, :] == wanted, 1.0, 0.0).reshape(BLOCK * MAIN, BLOCK)
-        pick_ref[...] = pick.astype(BF16)
-        last = jnp.where(slot == float(MAIN), 1.0, 0.0).astype(BF16)
         for tile in range(tiles):
             part = hn[:, tile * DH : (tile + 1) * DH]
-            over_ref[:, tile, :] = jnp.dot(last, part, preferred_element_type=F32)
+            over_ref[:, tile, :] = jnp.dot(last_ref[...], part, preferred_element_type=F32)
 
     stripe = send_ref.shape[1] // MAIN
     for index in range(pl.cdiv(tiles, stripe)):
@@ -405,14 +461,13 @@
     return jnp.concatenate(pieces, axis=1).astype(BF16)
 
 
-def project(core, part, got, w_out, hidden, gain, w_router, ids_t, depth=512):
+def project(core, part, got, w_out, hidden, gain, pick, last, depth=512):
     rows, half = got.shape
     width = hidden.shape[1]
     steps = half // depth
-    experts = w_router.shape[1]
+    experts = last.shape[0]
     tiles = width // DH
     packed = (experts, tiles * CAP, DH)
-    over = (experts, tiles, DH)
 
     def full(shape):
         return pl.BlockSpec(shape, lambda step, core_ref: (0,) * len(shape))
@@ -431,13 +486,12 @@
                 pl.BlockSpec((depth, width), w_map),
                 full((rows, width)),
                 full((1, width)),
-                full((width, experts)),
-                full((TOP, rows)),
+                full(pick.shape),
+                full(last.shape),
             ],
             out_specs=[
                 full((rows, width)),
-                full((experts, rows)),
-                full((experts, rows)),
+                full((rows, width)),
                 pl.BlockSpec(
                     (experts, STRIPE, DH),
                     lambda step, core_ref: (0, jnp.maximum(step - steps, 0), 0),
@@ -445,20 +499,17 @@
             ],
             scratch_shapes=[
                 pltpu.VMEM((rows, width), F32),
-                pltpu.VMEM((rows, width), BF16),
-                pltpu.VMEM((experts * MAIN, rows), BF16),
-                pltpu.VMEM(over, F32),
+                pltpu.VMEM((experts, tiles, DH), F32),
             ],
         ),
         out_shape=[
             jax.ShapeDtypeStruct((rows, width), BF16),
-            jax.ShapeDtypeStruct((experts, rows), F32),
-            jax.ShapeDtypeStruct((experts, rows), F32),
+            jax.ShapeDtypeStruct((rows, width), BF16),
             jax.ShapeDtypeStruct(packed, BF16),
         ],
         compiler_params=params("arbitrary"),
         name="project",
-    )(core, part, got, w_out, hidden, gain, w_router, ids_t)
+    )(core, part, got, w_out, hidden, gain, pick, last)
 
 
 def expert_kernel(
@@ -559,19 +610,13 @@
 
 
 def combine_kernel(
-    slot_ref, route_ref, in_ref, in_over_ref, h1_ref, out_ref, mix_ref, last_ref, over_ref, *, tiles
+    mix_ref, last_ref, in_ref, in_over_ref, h1_ref, out_ref, over_ref, *, tiles
 ):
     step = pl.program_id(0)
     stripe = in_ref.shape[1] // MAIN
 
     @pl.when(step == 0)
     def _():
-        slot = slot_ref[...]
-        route = route_ref[...]
-        wanted = lax.broadcasted_iota(jnp.int32, (BLOCK, MAIN, BLOCK), 1).astype(F32)
-        mix = jnp.where(slot[:, None, :] == wanted, route[:, None, :], 0.0)
-        mix_ref[...] = jnp.transpose(mix.reshape(BLOCK * MAIN, BLOCK).astype(BF16))
-        last_ref[...] = jnp.transpose(jnp.where(slot == float(MAIN), route, 0.0)).astype(BF16)
         over_ref[...] = in_over_ref[...].astype(F32)
 
     for index in range(pl.cdiv(tiles, stripe)):
@@ -596,7 +641,7 @@
             out_ref[:, columns] = (total + h1_ref[:, columns].astype(F32)).astype(BF16)
 
 
-def combine(slot, route, packed, h1):
+def combine(mix, last, packed, h1):
     rows, width = h1.shape
     experts = packed.shape[0]
     tiles = width // DH
@@ -608,26 +653,22 @@
         functools.partial(combine_kernel, tiles=tiles),
         grid=(packed.shape[1] // STRIPE,),
         in_specs=[
-            whole(slot.shape),
-            whole(route.shape),
+            whole(mix.shape),
+            whole(last.shape),
             pl.BlockSpec((experts, STRIPE, DH), lambda step: (0, step, 0)),
             pl.BlockSpec((experts, tiles, DH), lambda step: (0, MAIN, 0)),
             whole(h1.shape),
         ],
         out_specs=whole(h1.shape),
         out_shape=jax.ShapeDtypeStruct((rows, width), BF16),
-        scratch_shapes=[
-            pltpu.VMEM((rows, experts * MAIN), BF16),
-            pltpu.VMEM((rows, experts), BF16),
-            pltpu.VMEM((experts, tiles, DH), F32),
-        ],
+        scratch_shapes=[pltpu.VMEM((experts, tiles, DH), F32)],
         compiler_params=params("arbitrary"),
         name="combine",
-    )(slot, route, packed, packed, h1)
+    )(mix, last, packed, packed, h1)
 
 
 def exchange(packed):
-    return lax.all_to_all(packed, AXES, split_axis=0, concat_axis=0, tiled=True)
+    return lax.all_to_all(packed, TORUS, split_axis=0, concat_axis=0, tiled=True)
 
 
 def ring_near(piece, axes):
@@ -691,11 +732,14 @@
     )
     got = lax.ppermute(theirs, AXES, mirror)
     part = project_own(core_arr, own, w_out)
-    h1, slot, route, packed = project(
-        core_arr, part, got, w_out, hidden, norm_gain[None, :], w_router, expert_ids.T
-    )
-    returned = exchange(experts_of(exchange(packed), w_gate[0], w_up[0], w_down[0]))
-    return combine(slot, route, returned, h1)
+    slot, pick, last = plan(torus_place(expert_ids.T))
+    h1, hn, packed = project(
+        core_arr, part, got, w_out, hidden, norm_gain[None, :], pick, last
+    )
+    arrived = exchange(packed)
+    mix, last = routes(hn, w_router, expert_ids.T, slot)
+    returned = exchange(experts_of(arrived, w_gate[0], w_up[0], w_down[0]))
+    return combine(mix, last, returned, h1)
 
 
 def solution(mesh):

time: 298 us -> 298 us (level)
  blocking collectives: 141 us -> 76.7 us
  waiting for transfers between devices: 30.6 us -> 81.5 us
  starting transfers between devices: 34.3 us -> 41.6 us
  Pallas kernels: 81.8 us -> 85.6 us
    all_to_all x2 -> x1, blocking collectives: 130 us -> 65.5 us  [exchange(): lax.all_to_all(packed, TORUS, split_axis=0, concat_axis=0, tiled=True)]
    all_to_all x0 -> x1, waiting for transfers between devices: none -> 53.2 us  [exchange(): lax.all_to_all(packed, TORUS, split_axis=0, concat_axis=0, tiled=True)]
    all_to_all x0 -> x1, starting transfers between devices: none -> 7.08 us  [exchange(): lax.all_to_all(packed, TORUS, split_axis=0, concat_axis=0, tiled=True)]
    pallas_call x0 -> x2, Pallas kernels: none -> 4.28 us  [the longest x1 2.61 us: routes(): pl.pallas_call(routes_kernel, in_specs=[vmem] * 4, out_specs=[vmem] * 2,...]
  transfers between devices with their start and end apart: 17 -> 18, of which waited for: 6 -> 7; matrix products, arithmetic and copies ran while one was open for 1% -> 2% of each run, Pallas kernels for 12% -> 14%
where the time goes in v5:
time: 298 us; the launch traced here: 294 us
  Pallas kernels  85.6 us (29%)
  waiting for transfers between devices  81.5 us (27%)
  blocking collectives  76.7 us (26%)
  starting transfers between devices  41.6 us (14%)
  local copies, waits for them, and re-layouts  4.81 us (2%)
  other arithmetic  3.35 us (1%)
    all_to_all x1, blocking collectives, exchange(): lax.all_to_all(packed, TORUS, split_axis=0, concat_axis=0, tiled=True)  65.5 us
    all_to_all x1, waiting for transfers between devices, exchange(): lax.all_to_all(packed, TORUS, split_axis=0, concat_axis=0, tiled=True)  53.2 us
    pallas_call x3, Pallas kernels, attend(): pl.pallas_call(kernel, in_specs=[pl.BlockSpec(memory_space=pltpu.SMEM), v...  41.9 us
    pallas_call x1, Pallas kernels, experts_of(): pl.pallas_call(functools.partial(expert_kernel, steps=steps, up_steps=up_...  20.1 us
    ppermute x4, waiting for transfers between devices, ring_near(): left = lax.ppermute(piece, axes, [(i, (i + 1) % 4) for i in range(4)])  18.4 us
    all_gather x1, blocking collectives, local(): row = lax.all_gather(chip, ('x',), axis=0)  11.2 us
    ppermute x1, starting transfers between devices, local(): taken = lax.ppermute(give, AXES, mirror)  9.13 us
    pallas_call x1, Pallas kernels, project(): pl.pallas_call(functools.partial(project_kernel, steps=steps), grid_spec=...  8.04 us
  transfers between devices with their start and end apart: 18, of which 7 were waited for; matrix products, arithmetic and copies ran while one was open for 2% of the time, Pallas kernels for 14%

profile of v5, /device:TPU:9, one launch (start us, length us, event | category | flops | bytes accessed | tf_op | source)
XLA Modules:
  0.0 293.8 jit_solution(10993536071976146814)
XLA Ops:
  0.1 0.3 fusion.2
  0.4 0.8 pad_maximum_fusion.3
  1.1 2.2 rotate_all.1
  3.3 0.7 collective-permute-start.1
  4.0 1.1 collective-permute-done.1
  5.1 0.9 broadcast_select_fusion.1
  6.0 11.2 %all-gather = bf16[1024,256]{1,0:T(8,128)(2,1)S(1)} all-gather(bf16[256,256]{1,0:T(8,128)(2,1)S(1)} %pad_maximum_fusion.2), channel_id=2, replica_groups=mesh['zh'=2,'y'=4,'c'=2,'zl'=2,'x'=4] {'x'}, dimensions={0}, use_global_device_ids=true | all-gather | bytes 655360 | tf_op jit(solution)/shard_map/all_gather | solution.py:710
  17.2 3.8 %collective-permute-start.10 = (bf16[512,256]{1,0:T(8,128)(2,1)S(1)}, bf16[512,256]{1,0:T(8,128)(2,1)S(1)}, u32[]{:S(2)}, u32[]{:S(2)}) collective-permute-start(bf16[512,256]{1,0:T(8,128)(2,1)S(1)} %bitcast.22), channel_id=1, source_target_pairs={{0,68},{4,0},{64,4},{68,64},{1,69},{5,1},{65,5},{69,65},{2,70},{6,... | collective-permute-start | bytes 786440 | tf_op jit(solution)/shard_map/ppermute | solution.py:676
  21.1 0.7 collective-permute-start.9
  21.8 1.3 collective-permute-start.2
  23.1 0.2 collective-permute-start.3
  23.2 7.7 %collective-permute-done.10 = bf16[512,256]{1,0:T(8,128)(2,1)S(1)} collective-permute-done((bf16[512,256]{1,0:T(8,128)(2,1)S(1)}, bf16[512,256]{1,0:T(8,128)(2,1)S(1)}, u32[]{:S(2)}, u32[]{:S(2)}) %collective-permute-start.10) | collective-permute-done | bytes 262176 | tf_op jit(solution)/shard_map/ppermute | solution.py:676
  31.0 2.0 collective-permute-start.4
  33.0 2.8 collective-permute-done.9
  35.8 0.1 pad_maximum_fusion.1.refs_1_
  35.9 1.4 collective-permute-start.12
  37.3 0.2 collective-permute-start.14
  37.5 0.6 collective-permute-done.4
  38.1 0.1 pad_maximum_fusion.refs_0_
  38.2 0.1 collective-permute-start.5
  38.3 3.8 %collective-permute-start.7 = (bf16[2048,256]{1,0:T(8,128)(2,1)S(1)}, bf16[2048,256]{1,0:T(8,128)(2,1)}, u32[]{:S(2)}, u32[]{:S(2)}) collective-permute-start(bf16[2048,256]{1,0:T(8,128)(2,1)S(1)} %pad_maximum_fusion.refs_0_), channel_id=1, source_target_pairs={{0,68},{4,0},{64,4},{68,64},{1,69},{5,1},{65,5},{69,65},{2,70},{6,... | collective-permute-start | bytes 3145736 | tf_op jit(solution)/shard_map/ppermute | solution.py:676
  42.1 9.1 %collective-permute-start = (bf16[128,1024]{1,0:T(8,128)(2,1)S(1)}, bf16[128,1024]{1,0:T(8,128)(2,1)}, u32[]{:S(2)}, u32[]{:S(2)}) collective-permute-start(bf16[128,1024]{1,0:T(8,128)(2,1)S(1)} %copy-done.6), channel_id=1, source_target_pairs={{0,127},{1,126},{2,125},{3,124},{4,123},{5,122},{6,121},{7,120},{8... | collective-permute-start | bytes 786440 | tf_op jit(solution)/shard_map/ppermute | solution.py:704
  51.2 0.6 pad_add_fusion.meta_ref
  51.9 15.5 %collective-permute-done.12.refs_2_ = bf16[2048,256]{1,0:T(8,128)(2,1)S(1)} collective-permute-done((bf16[2048,256]{1,0:T(8,128)(2,1)S(1)}, bf16[2048,256]{1,0:T(8,128)(2,1)S(1)}, u32[]{:S(2)}, u32[]{:S(2)}) %collective-permute-start.12) | collective-permute-done | bytes 1048608 | tf_op jit(solution)/shard_map/ppermute | solution.py:675
  67.5 2.4 collective-permute-start.13
  69.8 1.1 slice.29
  70.9 0.1 collective-permute-start.15
  71.0 1.1 slice.25
  72.1 0.1 collective-permute-start.6
  72.2 1.1 slice.26
  73.3 3.0 %collective-permute-start.8 = (bf16[1024,256]{1,0:T(8,128)(2,1)S(1)}, bf16[1024,256]{1,0:T(8,128)(2,1)}, u32[]{:S(2)}, u32[]{:S(2)}) collective-permute-start(bf16[1024,256]{1,0:T(8,128)(2,1)S(1)} %slice.26), channel_id=1, source_target_pairs={{0,68},{4,0},{64,4},{68,64},{1,69},{5,1},{65,5},{69,65},{2,70},{6,... | collective-permute-start | bytes 1572872 | tf_op jit(solution)/shard_map/ppermute | solution.py:683
  76.3 13.3 %attend_first.1 = (f32[2048,128]{1,0:T(8,128)}, f32[2048,128]{1,0:T(8,128)}, f32[2048,128]{1,0:T(8,128)}) custom-call(s32[4]{0:T(128)} %pad_add_fusion.meta_ref, bf16[128,1024]{1,0:T(8,128)(2,1)} %collective-permute-done.theirs_ref, bf16[128,1024]{1,0:T(8,128)(2,1)} %get-tuple-element.26.own_ref, bf16[2048,256]{1,0:T(8,128)(2,1)} %copy-done.1, ...), custom_call_target="tpu_custom_call" | custom-call | flops 2147483648 | bytes 2097152 | tf_op jit(solution)/shard_map/attend_first/pallas_call | solution.py:281
  89.6 19.2 %attend_more.1 = (f32[2048,128]{1,0:T(8,128)}, f32[2048,128]{1,0:T(8,128)}, f32[2048,128]{1,0:T(8,128)}) custom-call(s32[4]{0:T(128)} %pad_add_fusion.meta_ref, bf16[128,1024]{1,0:T(8,128)(2,1)} %collective-permute-done.theirs_ref, bf16[128,1024]{1,0:T(8,128)(2,1)} %get-tuple-element.26.own_ref, bf16[2048,256]{1,0:T(8,128)(2,1)} %collective-permute-done.5.refs_0_, ...), custom_call_target="tpu_custom_call" | custom-call | flops 4294967296 | bytes 4194304 | tf_op jit(solution)/shard_map/attend_more/pallas_call | solution.py:281
  108.9 0.8 copy-done.5
  109.7 9.3 %attend_last.1 = (bf16[128,1024]{1,0:T(8,128)(2,1)}, bf16[128,1024]{1,0:T(8,128)(2,1)}) custom-call(s32[4]{0:T(128)} %pad_add_fusion.meta_ref, bf16[128,1024]{1,0:T(8,128)(2,1)} %collective-permute-done.theirs_ref, bf16[128,1024]{1,0:T(8,128)(2,1)} %get-tuple-element.26.own_ref, bf16[1024,256]{1,0:T(8,128)(2,1)} %collective-permute-done.6.refs_0_, ...), custom_call_target="tpu_custom_call" | custom-call | flops 2147483648 | bytes 2097152 | tf_op jit(solution)/shard_map/attend_last/pallas_call | solution.py:281
  119.0 5.7 %collective-permute-start.16 = (bf16[128,1024]{1,0:T(8,128)(2,1)}, bf16[128,1024]{1,0:T(8,128)(2,1)S(1)}, u32[]{:S(2)}, u32[]{:S(2)}) collective-permute-start(bf16[128,1024]{1,0:T(8,128)(2,1)} %get-tuple-element.36), channel_id=1, source_target_pairs={{0,127},{1,126},{2,125},{3,124},{4,123},{5,122},{6,121},{7,120},{8... | collective-permute-start | bytes 786440 | tf_op jit(solution)/shard_map/ppermute | solution.py:733
  124.7 0.6 fusion.8.ids_ref
  125.3 1.7 plan.1
  127.0 3.8 %project_own.1.part_ref = f32[128,2048]{1,0:T(8,128)} custom-call(s32[1]{0:T(128)} %bitcast.core_ref, bf16[128,1024]{1,0:T(8,128)(2,1)} %get-tuple-element.35.own_ref, bf16[2048,2048]{1,0:T(8,128)(2,1)} %w_ref.3), custom_call_target="tpu_custom_call" | custom-call | flops 536870912 | bytes 4194304 | tf_op jit(solution)/shard_map/project_own/pallas_call | solution.py:328
  130.7 0.4 collective-permute-done.16.got_ref
  131.2 0.7 copy-done.2
  131.9 8.0 %project.1 = (bf16[128,2048]{1,0:T(8,128)(2,1)}, bf16[128,2048]{1,0:T(8,128)(2,1)}, bf16[128,144,128]{2,1,0:T(8,128)(2,1)}) custom-call(s32[1]{0:T(128)} %bitcast.core_ref, f32[128,2048]{1,0:T(8,128)} %project_own.1.part_ref, bf16[128,1024]{1,0:T(8,128)(2,1)} %copy-done.2, bf16[2048,2048]{1,0:T(8,128)(2,1)} %w_ref.3, bf16[128,2048]{1,0:T(8,128)(2,1)} %hidden_ref.1, ...), custom_call_target="tpu_custom_call" | custom-call | tf_op jit(solution)/shard_map/project/pallas_call | solution.py:478
  139.9 65.5 %all_to_all.10.in_ref = bf16[128,144,128]{2,1,0:T(8,128)(2,1)} all-to-all(bf16[128,144,128]{2,1,0:T(8,128)(2,1)} %get-tuple-element.43), channel_id=1, replica_groups=mesh['zh'=2,'y'=4,'c'=2,'zl'=2,'x'=4] {'zh','zl','y','x','c'}, dimensions={0} | all-to-all | bytes 9437184 | tf_op jit(solution)/shard_map/all_to_all | solution.py:671
  205.4 20.1 %experts_of.1 = bf16[128,144,128]{2,1,0:T(8,128)(2,1)} custom-call(bf16[128,144,128]{2,1,0:T(8,128)(2,1)} %all_to_all.10.in_ref, bf16[2048,768]{1,0:T(8,128)(2,1)} %bitcast.14, bf16[2048,768]{1,0:T(8,128)(2,1)} %bitcast.15, bf16[768,2048]{1,0:T(8,128)(2,1)} %bitcast.16), custom_call_target="tpu_custom_call" | custom-call | tf_op jit(solution)/shard_map/experts_of/pallas_call | solution.py:591
  225.4 7.1 %all-to-all-start.1 = ((bf16[128,144,128]{2,1,0:T(8,128)(2,1)}), bf16[128,144,128]{2,1,0:T(8,128)(2,1)}, u32[]{:S(2)}, u32[]{:S(2)}) async-start(bf16[128,144,128]{2,1,0:T(8,128)(2,1)} %experts_of.1), calls=%async_computation.1 | async-start | bytes 9437184 | tf_op jit(solution)/shard_map/all_to_all | solution.py:671
  232.5 2.6 routes.1
  235.1 53.2 %all-to-all-done.1.in_ref.in_over_ref = bf16[128,144,128]{2,1,0:T(8,128)(2,1)} async-done(((bf16[128,144,128]{2,1,0:T(8,128)(2,1)}), bf16[128,144,128]{2,1,0:T(8,128)(2,1)}, u32[]{:S(2)}, u32[]{:S(2)}) %all-to-all-start.1) | async-done | bytes 4718624 | tf_op jit(solution)/shard_map/all_to_all | solution.py:671
  288.4 5.5 %combine.1 = bf16[128,2048]{1,0:T(8,128)(2,1)} custom-call(bf16[128,1024]{1,0:T(8,128)(2,1)} %get-tuple-element.41.mix_ref, bf16[128,128]{1,0:T(8,128)(2,1)} %get-tuple-element.42.last_ref, bf16[128,144,128]{2,1,0:T(8,128)(2,1)} %all-to-all-done.1.in_ref.in_over_ref, bf16[128,144,128]{2,1,0:T(8,128)(2,1)} %all-to-all-done.1.in_ref.in_over_ref, ...), custom_call_target="tpu_custom_call" | custom-call | tf_op jit(solution)/shard_map/combine/pallas_call | solution.py:652
  (29 shorter events, 0.2 us)
Async XLA Ops:
  3.3 1.8 collective-permute-start.1
  17.2 13.7 %collective-permute-start.10 = (bf16[512,256]{1,0:T(8,128)(2,1)S(1)}, bf16[512,256]{1,0:T(8,128)(2,1)S(1)}, u32[]{:S(2)}, u32[]{:S(2)}) collective-permute-start(bf16[512,256]{1,0:T(8,128)(2,1)S(1)} %bitcast.22), channel_id=1, source_target_pairs={{0,68},{4,0},{64,4},{68,64},{1,69},{5,1},{65,5},{69,65},{2,70},{6,... | collective-permute-start | bytes 786440 | tf_op jit(solution)/shard_map/ppermute | solution.py:676
  21.1 11.9 %collective-permute-start.11 = (bf16[512,256]{1,0:T(8,128)(2,1)S(1)}, bf16[512,256]{1,0:T(8,128)(2,1)S(1)}, u32[]{:S(2)}, u32[]{:S(2)}) collective-permute-start(bf16[512,256]{1,0:T(8,128)(2,1)S(1)} %bitcast.23), channel_id=1, source_target_pairs={{0,64},{4,68},{64,0},{68,4},{1,65},{5,69},{65,1},{69,5},{2,66},{6,... | collective-permute-start | bytes 786440 | tf_op jit(solution)/shard_map/ppermute | solution.py:689
  21.1 14.8 %collective-permute-start.9 = (bf16[512,256]{1,0:T(8,128)(2,1)S(1)}, bf16[512,256]{1,0:T(8,128)(2,1)S(1)}, u32[]{:S(2)}, u32[]{:S(2)}) collective-permute-start(bf16[512,256]{1,0:T(8,128)(2,1)S(1)} %bitcast.24), channel_id=1, source_target_pairs={{0,4},{4,64},{64,68},{68,0},{1,5},{5,65},{65,69},{69,1},{2,6},{6,6... | collective-permute-start | bytes 786440 | tf_op jit(solution)/shard_map/ppermute | solution.py:675
  21.8 20.3 %copy-start.6 = (bf16[128,1024]{1,0:T(8,128)(2,1)S(1)}, bf16[128,1024]{1,0:T(8,128)(2,1)}, u32[]{:S(2)}) copy-start(bf16[128,1024]{1,0:T(8,128)(2,1)} %get-tuple-element.25) | copy-start | bytes 786436
  21.8 15.7 %collective-permute-start.2 = (bf16[512,256]{1,0:T(8,128)(2,1)S(1)}, bf16[512,256]{1,0:T(8,128)(2,1)S(1)}, u32[]{:S(2)}, u32[]{:S(2)}) collective-permute-start(bf16[512,256]{1,0:T(8,128)(2,1)S(1)} %bitcast.18), channel_id=1, source_target_pairs={{0,16},{16,32},{32,48},{48,0},{1,17},{17,33},{33,49},{49,1},{2,18}... | collective-permute-start | bytes 786440 | tf_op jit(solution)/shard_map/ppermute | solution.py:675
  23.1 14.4 %collective-permute-start.3 = (bf16[512,256]{1,0:T(8,128)(2,1)S(1)}, bf16[512,256]{1,0:T(8,128)(2,1)S(1)}, u32[]{:S(2)}, u32[]{:S(2)}) collective-permute-start(bf16[512,256]{1,0:T(8,128)(2,1)S(1)} %bitcast.19), channel_id=1, source_target_pairs={{0,48},{16,0},{32,16},{48,32},{1,49},{17,1},{33,17},{49,33},{2,50}... | collective-permute-start | bytes 786440 | tf_op jit(solution)/shard_map/ppermute | solution.py:676
  31.0 7.1 %collective-permute-start.4 = (bf16[512,256]{1,0:T(8,128)(2,1)S(1)}, bf16[512,256]{1,0:T(8,128)(2,1)S(1)}, u32[]{:S(2)}, u32[]{:S(2)}) collective-permute-start(bf16[512,256]{1,0:T(8,128)(2,1)S(1)} %bitcast.20), channel_id=1, source_target_pairs={{0,32},{16,48},{32,0},{48,16},{1,33},{17,49},{33,1},{49,17},{2,34}... | collective-permute-start | bytes 786440 | tf_op jit(solution)/shard_map/ppermute | solution.py:689
  35.9 35.0 %copy-start = (bf16[2048,256]{1,0:T(8,128)(2,1)}, bf16[2048,256]{1,0:T(8,128)(2,1)S(1)}, u32[]{:S(2)}) copy-start(bf16[2048,256]{1,0:T(8,128)(2,1)S(1)} %pad_maximum_fusion.1.refs_1_) | copy-start | bytes 3145732
  35.9 31.5 %collective-permute-start.12 = (bf16[2048,256]{1,0:T(8,128)(2,1)S(1)}, bf16[2048,256]{1,0:T(8,128)(2,1)S(1)}, u32[]{:S(2)}, u32[]{:S(2)}) collective-permute-start(bf16[2048,256]{1,0:T(8,128)(2,1)S(1)} %pad_maximum_fusion.1.refs_1_), channel_id=1, source_target_pairs={{0,16},{16,32},{32,48},{48,0},{1,17},{17,33},{33,49},{49,1},{2,18}... | collective-permute-start | bytes 3145736 | tf_op jit(solution)/shard_map/ppermute | solution.py:675
  37.3 32.5 %collective-permute-start.14 = (bf16[2048,256]{1,0:T(8,128)(2,1)S(1)}, bf16[2048,256]{1,0:T(8,128)(2,1)}, u32[]{:S(2)}, u32[]{:S(2)}) collective-permute-start(bf16[2048,256]{1,0:T(8,128)(2,1)S(1)} %pad_maximum_fusion.1.refs_1_), channel_id=1, source_target_pairs={{0,48},{16,0},{32,16},{48,32},{1,49},{17,1},{33,17},{49,33},{2,50}... | collective-permute-start | bytes 3145736 | tf_op jit(solution)/shard_map/ppermute | solution.py:676
  38.2 35.1 %copy-start.1 = (bf16[2048,256]{1,0:T(8,128)(2,1)}, bf16[2048,256]{1,0:T(8,128)(2,1)S(1)}, u32[]{:S(2)}) copy-start(bf16[2048,256]{1,0:T(8,128)(2,1)S(1)} %pad_maximum_fusion.refs_0_) | copy-start | bytes 3145732
  38.2 32.8 %collective-permute-start.5 = (bf16[2048,256]{1,0:T(8,128)(2,1)S(1)}, bf16[2048,256]{1,0:T(8,128)(2,1)}, u32[]{:S(2)}, u32[]{:S(2)}) collective-permute-start(bf16[2048,256]{1,0:T(8,128)(2,1)S(1)} %pad_maximum_fusion.refs_0_), channel_id=1, source_target_pairs={{0,4},{4,64},{64,68},{68,0},{1,5},{5,65},{65,69},{69,1},{2,6},{6,6... | collective-permute-start | bytes 3145736 | tf_op jit(solution)/shard_map/ppermute | solution.py:675
  38.3 33.9 %collective-permute-start.7 = (bf16[2048,256]{1,0:T(8,128)(2,1)S(1)}, bf16[2048,256]{1,0:T(8,128)(2,1)}, u32[]{:S(2)}, u32[]{:S(2)}) collective-permute-start(bf16[2048,256]{1,0:T(8,128)(2,1)S(1)} %pad_maximum_fusion.refs_0_), channel_id=1, source_target_pairs={{0,68},{4,0},{64,4},{68,64},{1,69},{5,1},{65,5},{69,65},{2,70},{6,... | collective-permute-start | bytes 3145736 | tf_op jit(solution)/shard_map/ppermute | solution.py:676
  42.1 34.2 %collective-permute-start = (bf16[128,1024]{1,0:T(8,128)(2,1)S(1)}, bf16[128,1024]{1,0:T(8,128)(2,1)}, u32[]{:S(2)}, u32[]{:S(2)}) collective-permute-start(bf16[128,1024]{1,0:T(8,128)(2,1)S(1)} %copy-done.6), channel_id=1, source_target_pairs={{0,127},{1,126},{2,125},{3,124},{4,123},{5,122},{6,121},{7,120},{8... | collective-permute-start | bytes 786440 | tf_op jit(solution)/shard_map/ppermute | solution.py:704
  67.4 2.4 copy-start.3
  67.5 41.4 %collective-permute-start.13 = (bf16[1024,256]{1,0:T(8,128)(2,1)S(1)}, bf16[1024,256]{1,0:T(8,128)(2,1)}, u32[]{:S(2)}, u32[]{:S(2)}) collective-permute-start(bf16[1024,256]{1,0:T(8,128)(2,1)S(1)} %slice.28), channel_id=1, source_target_pairs={{0,16},{16,32},{32,48},{48,0},{1,17},{17,33},{33,49},{49,1},{2,18}... | collective-permute-start | bytes 1572872 | tf_op jit(solution)/shard_map/ppermute | solution.py:682
  70.9 38.0 %collective-permute-start.15 = (bf16[1024,256]{1,0:T(8,128)(2,1)S(1)}, bf16[1024,256]{1,0:T(8,128)(2,1)S(1)}, u32[]{:S(2)}, u32[]{:S(2)}) collective-permute-start(bf16[1024,256]{1,0:T(8,128)(2,1)S(1)} %slice.29), channel_id=1, source_target_pairs={{0,48},{16,0},{32,16},{48,32},{1,49},{17,1},{33,17},{49,33},{2,50}... | collective-permute-start | bytes 1572872 | tf_op jit(solution)/shard_map/ppermute | solution.py:683
  72.1 36.8 %collective-permute-start.6 = (bf16[1024,256]{1,0:T(8,128)(2,1)S(1)}, bf16[1024,256]{1,0:T(8,128)(2,1)}, u32[]{:S(2)}, u32[]{:S(2)}) collective-permute-start(bf16[1024,256]{1,0:T(8,128)(2,1)S(1)} %slice.25), channel_id=1, source_target_pairs={{0,4},{4,64},{64,68},{68,0},{1,5},{5,65},{65,69},{69,1},{2,6},{6,6... | collective-permute-start | bytes 1572872 | tf_op jit(solution)/shard_map/ppermute | solution.py:682
  73.3 35.6 %collective-permute-start.8 = (bf16[1024,256]{1,0:T(8,128)(2,1)S(1)}, bf16[1024,256]{1,0:T(8,128)(2,1)}, u32[]{:S(2)}, u32[]{:S(2)}) collective-permute-start(bf16[1024,256]{1,0:T(8,128)(2,1)S(1)} %slice.26), channel_id=1, source_target_pairs={{0,68},{4,0},{64,4},{68,64},{1,69},{5,1},{65,5},{69,65},{2,70},{6,... | collective-permute-start | bytes 1572872 | tf_op jit(solution)/shard_map/ppermute | solution.py:683
  108.9 0.8 copy-start.5
  109.7 15.0 %copy-start.4 = (s32[128,8]{0,1:T(8,128)S(1)}, s32[128,8]{0,1:T(8,128)}, u32[]{:S(2)}) copy-start(s32[128,8]{0,1:T(8,128)} %param.18) | copy-start | bytes 12292
  119.0 12.1 %collective-permute-start.16 = (bf16[128,1024]{1,0:T(8,128)(2,1)}, bf16[128,1024]{1,0:T(8,128)(2,1)S(1)}, u32[]{:S(2)}, u32[]{:S(2)}) collective-permute-start(bf16[128,1024]{1,0:T(8,128)(2,1)} %get-tuple-element.36), channel_id=1, source_target_pairs={{0,127},{1,126},{2,125},{3,124},{4,123},{5,122},{6,121},{7,120},{8... | collective-permute-start | bytes 786440 | tf_op jit(solution)/shard_map/ppermute | solution.py:733
  131.2 0.7 copy-start.2
  225.4 62.9 %all-to-all-start.1 = ((bf16[128,144,128]{2,1,0:T(8,128)(2,1)}), bf16[128,144,128]{2,1,0:T(8,128)(2,1)}, u32[]{:S(2)}, u32[]{:S(2)}) async-start(bf16[128,144,128]{2,1,0:T(8,128)(2,1)} %experts_of.1), calls=%async_computation.1 | async-start | bytes 9437184 | tf_op jit(solution)/shard_map/all_to_all | solution.py:671

commit v6 on v5

--- a/solution.py
+++ b/solution.py
@@ -17,7 +17,6 @@
 BLOCK = 128
 BLOCKS = 128
 UNIT = 4
-FAR = 1 << 20
 TILE_HEADS = 4
 AXES = ("zh", "y", "c", "zl", "x")
 TORUS = ("zh", "zl", "y", "x", "c")
@@ -126,28 +125,42 @@
         state_in, refs = refs[:3], refs[3:]
     if last:
         out_refs, refs = refs[:2], refs[2:]
+    else:
+        state_out, refs = refs[:3], refs[3:]
     state, refs = refs[:3], refs[3:]
-    kv_ref, q_ref, base_ref, list_ref, sem_ref = refs
+    kv_ref, q_ref, base_ref, list_ref, tail_ref, kv_sem, q_sem, in_sem, out_sem = refs
+    max_ref, sum_ref, acc_ref = state
     unit_rows = UNIT * BLOCK
-    copies = []
+    half_rows = heads * BLOCK
+
+    def half_copies(which, sources, targets, sems):
+        span = pl.ds(pl.multiple_of(which * half_rows, half_rows), half_rows)
+        return [
+            pltpu.make_async_copy(source.at[span, :], target.at[span, :], sems.at[which, index])
+            for index, (source, target) in enumerate(zip(sources, targets))
+        ]
+
+    copies = [
+        pltpu.make_async_copy(theirs_ref, q_ref.at[0], q_sem.at[0]),
+        pltpu.make_async_copy(own_ref, q_ref.at[1], q_sem.at[1]),
+    ]
     place = 0
     for index, piece in enumerate(piece_refs):
         size = piece.shape[0]
         copies.append(
-            pltpu.make_async_copy(piece, kv_ref.at[pl.ds(place, size), :], sem_ref.at[index])
+            pltpu.make_async_copy(piece, kv_ref.at[pl.ds(place, size), :], kv_sem.at[index])
         )
-        copies[-1].start()
         place += size
-    max_ref, sum_ref, acc_ref = state
+    for copy in copies:
+        copy.start()
     if first:
         max_ref[...] = jnp.full_like(max_ref, -1e30)
         sum_ref[...] = jnp.zeros_like(sum_ref)
         acc_ref[...] = jnp.zeros_like(acc_ref)
     else:
-        for source, target in zip(state_in, state):
-            target[...] = source[...]
-    q_ref[0] = theirs_ref[...]
-    q_ref[1] = own_ref[...]
+        for which in range(2):
+            for copy in half_copies(which, state_in, state, in_sem):
+                copy.start()
     for index, (z_off, y_off, c) in enumerate(units):
         base_ref[index] = first_block((meta_ref[2] + z_off) % 4, (meta_ref[3] + y_off) % 4, c)
     for copy in copies:
@@ -156,28 +169,25 @@
     factor = math.log2(math.e) / math.sqrt(DH)
     rows = tile_heads * BLOCK
     parts = heads // tile_heads
-    keys_len = 2 * unit_rows
 
     @pl.loop(0, 2)
     def _(which):
         block = meta_ref[which]
-
-        def update(u0, u1, masked):
-            starts = [pl.multiple_of(jnp.maximum(u, 0) * unit_rows, unit_rows) for u in (u0, u1)]
+        if not first:
+            for copy in half_copies(which, state_in, state, in_sem):
+                copy.wait()
+
+        def update(taken, masked):
+            keys_len = len(taken) * unit_rows
+            starts = [pl.multiple_of(unit * unit_rows, unit_rows) for unit in taken]
             keys = jnp.concatenate([kv_ref[pl.ds(s, unit_rows), :DH] for s in starts], axis=0)
             vals = jnp.concatenate([kv_ref[pl.ds(s, unit_rows), DH:] for s in starts], axis=0)
             if masked:
-                bases = [jnp.where(u < 0, FAR, base_ref[jnp.maximum(u, 0)]) for u in (u0, u1)]
                 shape = (BLOCK, unit_rows)
                 row_token = lax.broadcasted_iota(jnp.int32, shape, 0)
                 key_token = lax.broadcasted_iota(jnp.int32, shape, 1)
-                allowed = jnp.concatenate(
-                    [
-                        jnp.where(key_token + (base - block) * BLOCK <= row_token, 1, 0)
-                        for base in bases
-                    ],
-                    axis=1,
-                )
+                ahead = (base_ref[taken[0]] - block) * BLOCK
+                allowed = key_token + ahead <= row_token
 
             def scores_of(part):
                 query = jnp.concatenate(
@@ -192,7 +202,7 @@
                 )
                 if masked:
                     scores = jnp.where(
-                        allowed[None] > 0, scores.reshape(tile_heads, BLOCK, keys_len), -1e30
+                        allowed[None], scores.reshape(tile_heads, BLOCK, keys_len), -1e30
                     ).reshape(rows, keys_len)
                 return scores
 
@@ -221,26 +231,33 @@
                 scores = later
 
         count = jnp.int32(0)
-        diagonal = jnp.int32(-1)
+        tail = jnp.int32(0)
         for unit in range(len(units)):
             base = base_ref[unit]
             list_ref[count] = unit
+            tail_ref[tail] = unit
             count = count + jnp.where(base + UNIT <= block, 1, 0)
-            diagonal = jnp.where(
-                jnp.logical_and(base <= block, block < base + UNIT), unit, diagonal
-            )
-        whole = count // 2
-
-        @pl.loop(0, whole)
+            tail = tail + jnp.where(jnp.logical_and(base <= block, block < base + UNIT), 1, 0)
+        pairs = count // 2
+        tail_ref[tail] = list_ref[jnp.maximum(count - 1, 0)]
+        tail = tail + count - 2 * pairs
+
+        @pl.loop(0, pairs)
         def _(step):
-            update(list_ref[2 * step], list_ref[2 * step + 1], False)
-
-        odd = jnp.where(count > 2 * whole, list_ref[jnp.maximum(count - 1, 0)], -1)
-
-        @pl.when(jnp.logical_or(odd >= 0, diagonal >= 0))
-        def _():
-            update(odd, diagonal, True)
-
+            update([list_ref[2 * step], list_ref[2 * step + 1]], False)
+
+        @pl.loop(0, tail)
+        def _(step):
+            update([tail_ref[step]], True)
+
+        if not last:
+            for copy in half_copies(which, state, state_out, out_sem):
+                copy.start()
+
+    if not last:
+        for which in range(2):
+            for copy in half_copies(which, state, state_out, out_sem):
+                copy.wait()
     if last:
         for head in range(2 * heads):
             span = pl.ds(head * BLOCK, BLOCK)
@@ -253,17 +270,22 @@
 def attend(meta, units, theirs, own, pieces, state=None, last=False, tile_heads=TILE_HEADS):
     rows, width = own.shape
     heads = width // DH
+    smem = pl.BlockSpec(memory_space=pltpu.SMEM)
     vmem = pl.BlockSpec(memory_space=pltpu.VMEM)
+    anywhere = pl.BlockSpec(memory_space=pl.ANY)
     states = [(2 * heads * rows, DH)] * 3
-    scratch = [
+    scratch = [pltpu.VMEM(shape, F32) for shape in states] + [
         pltpu.VMEM((len(units) * UNIT * BLOCK, 2 * DH), BF16),
         pltpu.VMEM((2, rows, width), BF16),
         pltpu.SMEM((len(units),), jnp.int32),
         pltpu.SMEM((len(units) + 1,), jnp.int32),
+        pltpu.SMEM((len(units) + 2,), jnp.int32),
         pltpu.SemaphoreType.DMA((len(pieces),)),
+        pltpu.SemaphoreType.DMA((2,)),
+        pltpu.SemaphoreType.DMA((2, 3)),
+        pltpu.SemaphoreType.DMA((2, 3)),
     ]
     if last:
-        scratch = [pltpu.VMEM(shape, F32) for shape in states] + scratch
         out_shape = [jax.ShapeDtypeStruct((rows, width), BF16)] * 2
     else:
         out_shape = [jax.ShapeDtypeStruct(shape, F32) for shape in states]
@@ -280,10 +302,8 @@
     keys_seen = len(units) * UNIT * BLOCK
     return pl.pallas_call(
         kernel,
-        in_specs=[pl.BlockSpec(memory_space=pltpu.SMEM), vmem, vmem]
-        + [pl.BlockSpec(memory_space=pl.ANY)] * len(pieces)
-        + [vmem] * len(state),
-        out_specs=[vmem] * len(out_shape),
+        in_specs=[smem] + [anywhere] * (2 + len(pieces) + len(state)),
+        out_specs=[vmem if last else anywhere] * len(out_shape),
         out_shape=out_shape,
         scratch_shapes=scratch,
         compiler_params=params(),

time: 298 us -> 295 us (0.990)
  Pallas kernels: 85.6 us -> 81.8 us
    pallas_call x3, Pallas kernels: 41.9 us -> 38 us  [attend(): pl.pallas_call(kernel, in_specs=[smem] + [anywhere] * (2 + len(pieces) +...]
  transfers between devices with their start and end apart: 18 -> 18, of which waited for: 7 -> 7; matrix products, arithmetic and copies ran while one was open for 2% -> 2% of each run, Pallas kernels for 14% -> 13%
where the time goes in v6:
time: 295 us; the launch traced here: 291 us
  Pallas kernels  81.8 us (28%)
  waiting for transfers between devices  81.3 us (28%)
  blocking collectives  78.4 us (27%)
  starting transfers between devices  41.3 us (14%)
  local copies, waits for them, and re-layouts  4.81 us (2%)
  other arithmetic  3.35 us (1%)
    all_to_all x1, blocking collectives, exchange(): lax.all_to_all(packed, TORUS, split_axis=0, concat_axis=0, tiled=True)  67.2 us
    all_to_all x1, waiting for transfers between devices, exchange(): lax.all_to_all(packed, TORUS, split_axis=0, concat_axis=0, tiled=True)  53.2 us
    pallas_call x3, Pallas kernels, attend(): pl.pallas_call(kernel, in_specs=[smem] + [anywhere] * (2 + len(pieces) +...  38 us
    pallas_call x1, Pallas kernels, experts_of(): pl.pallas_call(functools.partial(expert_kernel, steps=steps, up_steps=up_...  20.1 us
    ppermute x4, waiting for transfers between devices, ring_near(): left = lax.ppermute(piece, axes, [(i, (i + 1) % 4) for i in range(4)])  18.4 us
    all_gather x1, blocking collectives, local(): row = lax.all_gather(chip, ('x',), axis=0)  11.2 us
    ppermute x1, starting transfers between devices, local(): taken = lax.ppermute(give, AXES, mirror)  9.13 us
    pallas_call x1, Pallas kernels, project(): pl.pallas_call(functools.partial(project_kernel, steps=steps), grid_spec=...  8.03 us
  transfers between devices with their start and end apart: 18, of which 7 were waited for; matrix products, arithmetic and copies ran while one was open for 2% of the time, Pallas kernels for 13%

profile of v6, /device:TPU:9, one launch (start us, length us, event | category | flops | bytes accessed | tf_op | source)
XLA Modules:
  0.0 291.2 jit_solution(18142805038372490162)
XLA Ops:
  0.1 0.3 fusion.2
  0.4 0.8 pad_maximum_fusion.3
  1.1 2.2 rotate_all.1
  3.3 0.7 collective-permute-start.1
  4.0 1.1 collective-permute-done.1
  5.1 0.9 broadcast_select_fusion.1
  6.0 11.2 %all-gather = bf16[1024,256]{1,0:T(8,128)(2,1)S(1)} all-gather(bf16[256,256]{1,0:T(8,128)(2,1)S(1)} %pad_maximum_fusion.2), channel_id=2, replica_groups=mesh['zh'=2,'y'=4,'c'=2,'zl'=2,'x'=4] {'x'}, dimensions={0}, use_global_device_ids=true | all-gather | bytes 655360 | tf_op jit(solution)/shard_map/all_gather | solution.py:730
  17.2 3.8 %collective-permute-start.10 = (bf16[512,256]{1,0:T(8,128)(2,1)S(1)}, bf16[512,256]{1,0:T(8,128)(2,1)S(1)}, u32[]{:S(2)}, u32[]{:S(2)}) collective-permute-start(bf16[512,256]{1,0:T(8,128)(2,1)S(1)} %bitcast.22), channel_id=1, source_target_pairs={{0,68},{4,0},{64,4},{68,64},{1,69},{5,1},{65,5},{69,65},{2,70},{6,... | collective-permute-start | bytes 786440 | tf_op jit(solution)/shard_map/ppermute | solution.py:696
  21.1 0.7 collective-permute-start.9
  21.8 1.3 collective-permute-start.2
  23.1 0.2 collective-permute-start.3
  23.2 7.7 %collective-permute-done.10 = bf16[512,256]{1,0:T(8,128)(2,1)S(1)} collective-permute-done((bf16[512,256]{1,0:T(8,128)(2,1)S(1)}, bf16[512,256]{1,0:T(8,128)(2,1)S(1)}, u32[]{:S(2)}, u32[]{:S(2)}) %collective-permute-start.10) | collective-permute-done | bytes 262176 | tf_op jit(solution)/shard_map/ppermute | solution.py:696
  31.0 2.0 collective-permute-start.4
  33.0 2.8 collective-permute-done.9
  35.8 0.1 pad_maximum_fusion.1.refs_1_
  35.9 1.4 collective-permute-start.12
  37.3 0.2 collective-permute-start.14
  37.5 0.6 collective-permute-done.4
  38.1 0.1 pad_maximum_fusion.refs_0_
  38.2 0.1 collective-permute-start.5
  38.3 3.8 %collective-permute-start.7 = (bf16[2048,256]{1,0:T(8,128)(2,1)S(1)}, bf16[2048,256]{1,0:T(8,128)(2,1)}, u32[]{:S(2)}, u32[]{:S(2)}) collective-permute-start(bf16[2048,256]{1,0:T(8,128)(2,1)S(1)} %pad_maximum_fusion.refs_0_), channel_id=1, source_target_pairs={{0,68},{4,0},{64,4},{68,64},{1,69},{5,1},{65,5},{69,65},{2,70},{6,... | collective-permute-start | bytes 3145736 | tf_op jit(solution)/shard_map/ppermute | solution.py:696
  42.1 9.1 %collective-permute-start = (bf16[128,1024]{1,0:T(8,128)(2,1)S(1)}, bf16[128,1024]{1,0:T(8,128)(2,1)}, u32[]{:S(2)}, u32[]{:S(2)}) collective-permute-start(bf16[128,1024]{1,0:T(8,128)(2,1)S(1)} %copy-done.6), channel_id=1, source_target_pairs={{0,127},{1,126},{2,125},{3,124},{4,123},{5,122},{6,121},{7,120},{8... | collective-permute-start | bytes 786440 | tf_op jit(solution)/shard_map/ppermute | solution.py:724
  51.2 0.6 pad_add_fusion.meta_ref
  51.9 15.5 %collective-permute-done.12.refs_2_ = bf16[2048,256]{1,0:T(8,128)(2,1)S(1)} collective-permute-done((bf16[2048,256]{1,0:T(8,128)(2,1)S(1)}, bf16[2048,256]{1,0:T(8,128)(2,1)S(1)}, u32[]{:S(2)}, u32[]{:S(2)}) %collective-permute-start.12) | collective-permute-done | bytes 1048608 | tf_op jit(solution)/shard_map/ppermute | solution.py:695
  67.5 2.4 collective-permute-start.13
  69.8 1.1 slice.29
  70.9 0.1 collective-permute-start.15
  71.0 1.1 slice.25
  72.1 0.1 collective-permute-start.6
  72.2 1.1 slice.26
  73.3 3.0 %collective-permute-start.8 = (bf16[1024,256]{1,0:T(8,128)(2,1)S(1)}, bf16[1024,256]{1,0:T(8,128)(2,1)}, u32[]{:S(2)}, u32[]{:S(2)}) collective-permute-start(bf16[1024,256]{1,0:T(8,128)(2,1)S(1)} %slice.26), channel_id=1, source_target_pairs={{0,68},{4,0},{64,4},{68,64},{1,69},{5,1},{65,5},{69,65},{2,70},{6,... | collective-permute-start | bytes 1572872 | tf_op jit(solution)/shard_map/ppermute | solution.py:703
  76.3 11.9 %attend_first.1 = (f32[2048,128]{1,0:T(8,128)}, f32[2048,128]{1,0:T(8,128)}, f32[2048,128]{1,0:T(8,128)}) custom-call(s32[4]{0:T(128)} %pad_add_fusion.meta_ref, bf16[128,1024]{1,0:T(8,128)(2,1)} %collective-permute-done.theirs_ref, bf16[128,1024]{1,0:T(8,128)(2,1)} %get-tuple-element.26.own_ref, bf16[2048,256]{1,0:T(8,128)(2,1)} %copy-done.1, ...), custom_call_target="tpu_custom_call" | custom-call | flops 2147483648 | bytes 2097152 | tf_op jit(solution)/shard_map/attend_first/pallas_call | solution.py:303
  88.2 17.7 %attend_more.1 = (f32[2048,128]{1,0:T(8,128)}, f32[2048,128]{1,0:T(8,128)}, f32[2048,128]{1,0:T(8,128)}) custom-call(s32[4]{0:T(128)} %pad_add_fusion.meta_ref, bf16[128,1024]{1,0:T(8,128)(2,1)} %collective-permute-done.theirs_ref, bf16[128,1024]{1,0:T(8,128)(2,1)} %get-tuple-element.26.own_ref, bf16[2048,256]{1,0:T(8,128)(2,1)} %collective-permute-done.5.refs_0_, ...), custom_call_target="tpu_custom_call" | custom-call | flops 4294967296 | bytes 4194304 | tf_op jit(solution)/shard_map/attend_more/pallas_call | solution.py:303
  106.0 0.8 copy-done.5
  106.8 8.4 %attend_last.1 = (bf16[128,1024]{1,0:T(8,128)(2,1)}, bf16[128,1024]{1,0:T(8,128)(2,1)}) custom-call(s32[4]{0:T(128)} %pad_add_fusion.meta_ref, bf16[128,1024]{1,0:T(8,128)(2,1)} %collective-permute-done.theirs_ref, bf16[128,1024]{1,0:T(8,128)(2,1)} %get-tuple-element.26.own_ref, bf16[1024,256]{1,0:T(8,128)(2,1)} %collective-permute-done.6.refs_0_, ...), custom_call_target="tpu_custom_call" | custom-call | flops 2147483648 | bytes 2097152 | tf_op jit(solution)/shard_map/attend_last/pallas_call | solution.py:303
  115.2 5.4 %collective-permute-start.16 = (bf16[128,1024]{1,0:T(8,128)(2,1)}, bf16[128,1024]{1,0:T(8,128)(2,1)S(1)}, u32[]{:S(2)}, u32[]{:S(2)}) collective-permute-start(bf16[128,1024]{1,0:T(8,128)(2,1)} %get-tuple-element.36), channel_id=1, source_target_pairs={{0,127},{1,126},{2,125},{3,124},{4,123},{5,122},{6,121},{7,120},{8... | collective-permute-start | bytes 786440 | tf_op jit(solution)/shard_map/ppermute | solution.py:753
  120.6 0.6 fusion.8.ids_ref
  121.2 1.7 plan.1
  122.9 3.8 %project_own.1.part_ref = f32[128,2048]{1,0:T(8,128)} custom-call(s32[1]{0:T(128)} %bitcast.core_ref, bf16[128,1024]{1,0:T(8,128)(2,1)} %get-tuple-element.35.own_ref, bf16[2048,2048]{1,0:T(8,128)(2,1)} %w_ref.3), custom_call_target="tpu_custom_call" | custom-call | flops 536870912 | bytes 4194304 | tf_op jit(solution)/shard_map/project_own/pallas_call | solution.py:348
  126.7 0.2 collective-permute-done.16.got_ref
  126.9 0.7 copy-done.2
  127.6 8.0 %project.1 = (bf16[128,2048]{1,0:T(8,128)(2,1)}, bf16[128,2048]{1,0:T(8,128)(2,1)}, bf16[128,144,128]{2,1,0:T(8,128)(2,1)}) custom-call(s32[1]{0:T(128)} %bitcast.core_ref, f32[128,2048]{1,0:T(8,128)} %project_own.1.part_ref, bf16[128,1024]{1,0:T(8,128)(2,1)} %copy-done.2, bf16[2048,2048]{1,0:T(8,128)(2,1)} %w_ref.3, bf16[128,2048]{1,0:T(8,128)(2,1)} %hidden_ref.1, ...), custom_call_target="tpu_custom_call" | custom-call | tf_op jit(solution)/shard_map/project/pallas_call | solution.py:498
  135.6 67.2 %all_to_all.10.in_ref = bf16[128,144,128]{2,1,0:T(8,128)(2,1)} all-to-all(bf16[128,144,128]{2,1,0:T(8,128)(2,1)} %get-tuple-element.43), channel_id=1, replica_groups=mesh['zh'=2,'y'=4,'c'=2,'zl'=2,'x'=4] {'zh','zl','y','x','c'}, dimensions={0} | all-to-all | bytes 9437184 | tf_op jit(solution)/shard_map/all_to_all | solution.py:691
  202.8 20.1 %experts_of.1 = bf16[128,144,128]{2,1,0:T(8,128)(2,1)} custom-call(bf16[128,144,128]{2,1,0:T(8,128)(2,1)} %all_to_all.10.in_ref, bf16[2048,768]{1,0:T(8,128)(2,1)} %bitcast.14, bf16[2048,768]{1,0:T(8,128)(2,1)} %bitcast.15, bf16[768,2048]{1,0:T(8,128)(2,1)} %bitcast.16), custom_call_target="tpu_custom_call" | custom-call | tf_op jit(solution)/shard_map/experts_of/pallas_call | solution.py:611
  222.8 7.1 %all-to-all-start.1 = ((bf16[128,144,128]{2,1,0:T(8,128)(2,1)}), bf16[128,144,128]{2,1,0:T(8,128)(2,1)}, u32[]{:S(2)}, u32[]{:S(2)}) async-start(bf16[128,144,128]{2,1,0:T(8,128)(2,1)} %experts_of.1), calls=%async_computation.1 | async-start | bytes 9437184 | tf_op jit(solution)/shard_map/all_to_all | solution.py:691
  229.9 2.6 routes.1
  232.5 53.2 %all-to-all-done.1.in_ref.in_over_ref = bf16[128,144,128]{2,1,0:T(8,128)(2,1)} async-done(((bf16[128,144,128]{2,1,0:T(8,128)(2,1)}), bf16[128,144,128]{2,1,0:T(8,128)(2,1)}, u32[]{:S(2)}, u32[]{:S(2)}) %all-to-all-start.1) | async-done | bytes 4718624 | tf_op jit(solution)/shard_map/all_to_all | solution.py:691
  285.8 5.5 %combine.1 = bf16[128,2048]{1,0:T(8,128)(2,1)} custom-call(bf16[128,1024]{1,0:T(8,128)(2,1)} %get-tuple-element.41.mix_ref, bf16[128,128]{1,0:T(8,128)(2,1)} %get-tuple-element.42.last_ref, bf16[128,144,128]{2,1,0:T(8,128)(2,1)} %all-to-all-done.1.in_ref.in_over_ref, bf16[128,144,128]{2,1,0:T(8,128)(2,1)} %all-to-all-done.1.in_ref.in_over_ref, ...), custom_call_target="tpu_custom_call" | custom-call | tf_op jit(solution)/shard_map/combine/pallas_call | solution.py:672
  (29 shorter events, 0.2 us)
Async XLA Ops:
  3.3 1.8 collective-permute-start.1
  17.2 13.7 %collective-permute-start.10 = (bf16[512,256]{1,0:T(8,128)(2,1)S(1)}, bf16[512,256]{1,0:T(8,128)(2,1)S(1)}, u32[]{:S(2)}, u32[]{:S(2)}) collective-permute-start(bf16[512,256]{1,0:T(8,128)(2,1)S(1)} %bitcast.22), channel_id=1, source_target_pairs={{0,68},{4,0},{64,4},{68,64},{1,69},{5,1},{65,5},{69,65},{2,70},{6,... | collective-permute-start | bytes 786440 | tf_op jit(solution)/shard_map/ppermute | solution.py:696
  21.1 11.9 %collective-permute-start.11 = (bf16[512,256]{1,0:T(8,128)(2,1)S(1)}, bf16[512,256]{1,0:T(8,128)(2,1)S(1)}, u32[]{:S(2)}, u32[]{:S(2)}) collective-permute-start(bf16[512,256]{1,0:T(8,128)(2,1)S(1)} %bitcast.23), channel_id=1, source_target_pairs={{0,64},{4,68},{64,0},{68,4},{1,65},{5,69},{65,1},{69,5},{2,66},{6,... | collective-permute-start | bytes 786440 | tf_op jit(solution)/shard_map/ppermute | solution.py:709
  21.1 14.8 %collective-permute-start.9 = (bf16[512,256]{1,0:T(8,128)(2,1)S(1)}, bf16[512,256]{1,0:T(8,128)(2,1)S(1)}, u32[]{:S(2)}, u32[]{:S(2)}) collective-permute-start(bf16[512,256]{1,0:T(8,128)(2,1)S(1)} %bitcast.24), channel_id=1, source_target_pairs={{0,4},{4,64},{64,68},{68,0},{1,5},{5,65},{65,69},{69,1},{2,6},{6,6... | collective-permute-start | bytes 786440 | tf_op jit(solution)/shard_map/ppermute | solution.py:695
  21.8 20.3 %copy-start.6 = (bf16[128,1024]{1,0:T(8,128)(2,1)S(1)}, bf16[128,1024]{1,0:T(8,128)(2,1)}, u32[]{:S(2)}) copy-start(bf16[128,1024]{1,0:T(8,128)(2,1)} %get-tuple-element.25) | copy-start | bytes 786436
  21.8 15.7 %collective-permute-start.2 = (bf16[512,256]{1,0:T(8,128)(2,1)S(1)}, bf16[512,256]{1,0:T(8,128)(2,1)S(1)}, u32[]{:S(2)}, u32[]{:S(2)}) collective-permute-start(bf16[512,256]{1,0:T(8,128)(2,1)S(1)} %bitcast.18), channel_id=1, source_target_pairs={{0,16},{16,32},{32,48},{48,0},{1,17},{17,33},{33,49},{49,1},{2,18}... | collective-permute-start | bytes 786440 | tf_op jit(solution)/shard_map/ppermute | solution.py:695
  23.1 14.4 %collective-permute-start.3 = (bf16[512,256]{1,0:T(8,128)(2,1)S(1)}, bf16[512,256]{1,0:T(8,128)(2,1)S(1)}, u32[]{:S(2)}, u32[]{:S(2)}) collective-permute-start(bf16[512,256]{1,0:T(8,128)(2,1)S(1)} %bitcast.19), channel_id=1, source_target_pairs={{0,48},{16,0},{32,16},{48,32},{1,49},{17,1},{33,17},{49,33},{2,50}... | collective-permute-start | bytes 786440 | tf_op jit(solution)/shard_map/ppermute | solution.py:696
  31.0 7.1 %collective-permute-start.4 = (bf16[512,256]{1,0:T(8,128)(2,1)S(1)}, bf16[512,256]{1,0:T(8,128)(2,1)S(1)}, u32[]{:S(2)}, u32[]{:S(2)}) collective-permute-start(bf16[512,256]{1,0:T(8,128)(2,1)S(1)} %bitcast.20), channel_id=1, source_target_pairs={{0,32},{16,48},{32,0},{48,16},{1,33},{17,49},{33,1},{49,17},{2,34}... | collective-permute-start | bytes 786440 | tf_op jit(solution)/shard_map/ppermute | solution.py:709
  35.9 35.0 %copy-start = (bf16[2048,256]{1,0:T(8,128)(2,1)}, bf16[2048,256]{1,0:T(8,128)(2,1)S(1)}, u32[]{:S(2)}) copy-start(bf16[2048,256]{1,0:T(8,128)(2,1)S(1)} %pad_maximum_fusion.1.refs_1_) | copy-start | bytes 3145732
  35.9 31.5 %collective-permute-start.12 = (bf16[2048,256]{1,0:T(8,128)(2,1)S(1)}, bf16[2048,256]{1,0:T(8,128)(2,1)S(1)}, u32[]{:S(2)}, u32[]{:S(2)}) collective-permute-start(bf16[2048,256]{1,0:T(8,128)(2,1)S(1)} %pad_maximum_fusion.1.refs_1_), channel_id=1, source_target_pairs={{0,16},{16,32},{32,48},{48,0},{1,17},{17,33},{33,49},{49,1},{2,18}... | collective-permute-start | bytes 3145736 | tf_op jit(solution)/shard_map/ppermute | solution.py:695
  37.3 32.5 %collective-permute-start.14 = (bf16[2048,256]{1,0:T(8,128)(2,1)S(1)}, bf16[2048,256]{1,0:T(8,128)(2,1)}, u32[]{:S(2)}, u32[]{:S(2)}) collective-permute-start(bf16[2048,256]{1,0:T(8,128)(2,1)S(1)} %pad_maximum_fusion.1.refs_1_), channel_id=1, source_target_pairs={{0,48},{16,0},{32,16},{48,32},{1,49},{17,1},{33,17},{49,33},{2,50}... | collective-permute-start | bytes 3145736 | tf_op jit(solution)/shard_map/ppermute | solution.py:696
  38.2 35.1 %copy-start.1 = (bf16[2048,256]{1,0:T(8,128)(2,1)}, bf16[2048,256]{1,0:T(8,128)(2,1)S(1)}, u32[]{:S(2)}) copy-start(bf16[2048,256]{1,0:T(8,128)(2,1)S(1)} %pad_maximum_fusion.refs_0_) | copy-start | bytes 3145732
  38.2 32.8 %collective-permute-start.5 = (bf16[2048,256]{1,0:T(8,128)(2,1)S(1)}, bf16[2048,256]{1,0:T(8,128)(2,1)}, u32[]{:S(2)}, u32[]{:S(2)}) collective-permute-start(bf16[2048,256]{1,0:T(8,128)(2,1)S(1)} %pad_maximum_fusion.refs_0_), channel_id=1, source_target_pairs={{0,4},{4,64},{64,68},{68,0},{1,5},{5,65},{65,69},{69,1},{2,6},{6,6... | collective-permute-start | bytes 3145736 | tf_op jit(solution)/shard_map/ppermute | solution.py:695
  38.3 33.9 %collective-permute-start.7 = (bf16[2048,256]{1,0:T(8,128)(2,1)S(1)}, bf16[2048,256]{1,0:T(8,128)(2,1)}, u32[]{:S(2)}, u32[]{:S(2)}) collective-permute-start(bf16[2048,256]{1,0:T(8,128)(2,1)S(1)} %pad_maximum_fusion.refs_0_), channel_id=1, source_target_pairs={{0,68},{4,0},{64,4},{68,64},{1,69},{5,1},{65,5},{69,65},{2,70},{6,... | collective-permute-start | bytes 3145736 | tf_op jit(solution)/shard_map/ppermute | solution.py:696
  42.1 34.2 %collective-permute-start = (bf16[128,1024]{1,0:T(8,128)(2,1)S(1)}, bf16[128,1024]{1,0:T(8,128)(2,1)}, u32[]{:S(2)}, u32[]{:S(2)}) collective-permute-start(bf16[128,1024]{1,0:T(8,128)(2,1)S(1)} %copy-done.6), channel_id=1, source_target_pairs={{0,127},{1,126},{2,125},{3,124},{4,123},{5,122},{6,121},{7,120},{8... | collective-permute-start | bytes 786440 | tf_op jit(solution)/shard_map/ppermute | solution.py:724
  67.4 2.4 copy-start.3
  67.5 38.5 %collective-permute-start.13 = (bf16[1024,256]{1,0:T(8,128)(2,1)S(1)}, bf16[1024,256]{1,0:T(8,128)(2,1)}, u32[]{:S(2)}, u32[]{:S(2)}) collective-permute-start(bf16[1024,256]{1,0:T(8,128)(2,1)S(1)} %slice.28), channel_id=1, source_target_pairs={{0,16},{16,32},{32,48},{48,0},{1,17},{17,33},{33,49},{49,1},{2,18}... | collective-permute-start | bytes 1572872 | tf_op jit(solution)/shard_map/ppermute | solution.py:702
  70.9 35.1 %collective-permute-start.15 = (bf16[1024,256]{1,0:T(8,128)(2,1)S(1)}, bf16[1024,256]{1,0:T(8,128)(2,1)S(1)}, u32[]{:S(2)}, u32[]{:S(2)}) collective-permute-start(bf16[1024,256]{1,0:T(8,128)(2,1)S(1)} %slice.29), channel_id=1, source_target_pairs={{0,48},{16,0},{32,16},{48,32},{1,49},{17,1},{33,17},{49,33},{2,50}... | collective-permute-start | bytes 1572872 | tf_op jit(solution)/shard_map/ppermute | solution.py:703
  72.1 33.9 %collective-permute-start.6 = (bf16[1024,256]{1,0:T(8,128)(2,1)S(1)}, bf16[1024,256]{1,0:T(8,128)(2,1)}, u32[]{:S(2)}, u32[]{:S(2)}) collective-permute-start(bf16[1024,256]{1,0:T(8,128)(2,1)S(1)} %slice.25), channel_id=1, source_target_pairs={{0,4},{4,64},{64,68},{68,0},{1,5},{5,65},{65,69},{69,1},{2,6},{6,6... | collective-permute-start | bytes 1572872 | tf_op jit(solution)/shard_map/ppermute | solution.py:702
  73.3 32.7 %collective-permute-start.8 = (bf16[1024,256]{1,0:T(8,128)(2,1)S(1)}, bf16[1024,256]{1,0:T(8,128)(2,1)}, u32[]{:S(2)}, u32[]{:S(2)}) collective-permute-start(bf16[1024,256]{1,0:T(8,128)(2,1)S(1)} %slice.26), channel_id=1, source_target_pairs={{0,68},{4,0},{64,4},{68,64},{1,69},{5,1},{65,5},{69,65},{2,70},{6,... | collective-permute-start | bytes 1572872 | tf_op jit(solution)/shard_map/ppermute | solution.py:703
  106.0 0.8 copy-start.5
  106.8 13.8 %copy-start.4 = (s32[128,8]{0,1:T(8,128)S(1)}, s32[128,8]{0,1:T(8,128)}, u32[]{:S(2)}) copy-start(s32[128,8]{0,1:T(8,128)} %param.18) | copy-start | bytes 12292
  115.2 11.7 %collective-permute-start.16 = (bf16[128,1024]{1,0:T(8,128)(2,1)}, bf16[128,1024]{1,0:T(8,128)(2,1)S(1)}, u32[]{:S(2)}, u32[]{:S(2)}) collective-permute-start(bf16[128,1024]{1,0:T(8,128)(2,1)} %get-tuple-element.36), channel_id=1, source_target_pairs={{0,127},{1,126},{2,125},{3,124},{4,123},{5,122},{6,121},{7,120},{8... | collective-permute-start | bytes 786440 | tf_op jit(solution)/shard_map/ppermute | solution.py:753
  126.9 0.7 copy-start.2
  222.8 62.9 %all-to-all-start.1 = ((bf16[128,144,128]{2,1,0:T(8,128)(2,1)}), bf16[128,144,128]{2,1,0:T(8,128)(2,1)}, u32[]{:S(2)}, u32[]{:S(2)}) async-start(bf16[128,144,128]{2,1,0:T(8,128)(2,1)} %experts_of.1), calls=%async_computation.1 | async-start | bytes 9437184 | tf_op jit(solution)/shard_map/all_to_all | solution.py:691

commit v7 on v6

--- a/solution.py
+++ b/solution.py
@@ -691,23 +691,24 @@
     return lax.all_to_all(packed, TORUS, split_axis=0, concat_axis=0, tiled=True)
 
 
-def ring_near(piece, axes):
-    left = lax.ppermute(piece, axes, [(i, (i + 1) % 4) for i in range(4)])
-    right = lax.ppermute(piece, axes, [(i, (i + 3) % 4) for i in range(4)])
-    return left, right
-
-
-def ring_far(left, right, axes):
-    half = left.shape[0] // 2
-    low = lax.ppermute(left[:half], axes, [(i, (i + 1) % 4) for i in range(4)])
-    high = lax.ppermute(right[half:], axes, [(i, (i + 3) % 4) for i in range(4)])
-    return low, high
+def ring_step(piece, axes, by):
+    return lax.ppermute(piece, axes, [(i, (i + by) % 4) for i in range(4)])
 
 
 def ring_gather(piece, axes):
-    left, right = ring_near(piece, axes)
-    far = lax.ppermute(piece, axes, [(i, (i + 2) % 4) for i in range(4)])
-    return jnp.concatenate([piece, left, right, far], axis=0)
+    left, right, far = (ring_step(piece, axes, by) for by in (1, 3, 2))
+    return jnp.concatenate([piece, left], axis=0), jnp.concatenate([right, far], axis=0)
+
+
+def ring_near(halves, axes):
+    top, bottom = halves
+    left_top, right_bottom = ring_step(top, axes, 1), ring_step(bottom, axes, 3)
+    left_bottom, right_top = ring_step(bottom, axes, 1), ring_step(top, axes, 3)
+    return left_top, left_bottom, right_top, right_bottom
+
+
+def ring_far(near, axes):
+    return ring_step(near[0], axes, 1), ring_step(near[3], axes, 3)
 
 
 def local(
@@ -734,8 +735,8 @@
     high = ring_gather(high, RING_Z)
     low_near = ring_near(low, RING_Z)
     high_near = ring_near(high, RING_Y)
-    low_far = ring_far(*low_near, RING_Z)
-    high_far = ring_far(*high_near, RING_Y)
+    low_far = ring_far(low_near, RING_Z)
+    high_far = ring_far(high_near, RING_Y)
 
     def units(order):
         return [(outer, inner, 0) for outer in order for inner in OFFSETS] + [
@@ -745,7 +746,7 @@
     meta = jnp.stack(
         [BLOCKS - 1 - device, device, lax.axis_index(RING_Z), lax.axis_index(RING_Y)]
     ).astype(jnp.int32)
-    state = attend(meta, units((0,)), taken, keep, [low, high])
+    state = attend(meta, units((0,)), taken, keep, [*low, *high])
     state = attend(meta, units((-1, 1)), taken, keep, [*low_near, *high_near], state=state)
     theirs, own = attend(
         meta, units((2,)), taken, keep, [*low_far, *high_far], state=state, last=True

time: 295 us -> 290 us (0.983)
  waiting for transfers between devices: 81.3 us -> 73.1 us
  starting transfers between devices: 41.3 us -> 46.7 us
    ppermute x14 -> x18, waiting for transfers between devices: 26.8 us -> 11.7 us  [ring_step(): return lax.ppermute(piece, axes, [(i, (i + by) % 4) for i in range(4)])]
    ppermute x1, waiting for transfers between devices: 0.01 us -> 7.06 us  [local(): taken = lax.ppermute(give, AXES, mirror)]
    ppermute x14 -> x18, starting transfers between devices: 19 us -> 23 us  [ring_step(): return lax.ppermute(piece, axes, [(i, (i + by) % 4) for i in range(4)])]
    slice x4 -> x0, local copies, waits for them, and re-layouts: 3.27 us -> none  [the longest x2 2.15 us: ring_far(): right[half:]]
  transfers between devices with their start and end apart: 18 -> 22, of which waited for: 7 -> 6; matrix products, arithmetic and copies ran while one was open for 2% -> 0% of each run, Pallas kernels for 13% -> 13%
where the time goes in v7:
time: 290 us; the launch traced here: 286 us
  Pallas kernels  81.7 us (28%)
  blocking collectives  78.3 us (27%)
  waiting for transfers between devices  73.1 us (25%)
  starting transfers between devices  46.7 us (16%)
  other arithmetic  3.24 us (1%)
    all_to_all x1, blocking collectives, exchange(): lax.all_to_all(packed, TORUS, split_axis=0, concat_axis=0, tiled=True)  67.1 us
    all_to_all x1, waiting for transfers between devices, exchange(): lax.all_to_all(packed, TORUS, split_axis=0, concat_axis=0, tiled=True)  53.2 us
    pallas_call x3, Pallas kernels, attend(): pl.pallas_call(kernel, in_specs=[smem] + [anywhere] * (2 + len(pieces) +...  37.8 us
    ppermute x18, starting transfers between devices, ring_step(): return lax.ppermute(piece, axes, [(i, (i + by) % 4) for i in range(4)])  23 us
    pallas_call x1, Pallas kernels, experts_of(): pl.pallas_call(functools.partial(expert_kernel, steps=steps, up_steps=up_...  20.1 us
    ppermute x18, waiting for transfers between devices, ring_step(): return lax.ppermute(piece, axes, [(i, (i + by) % 4) for i in range(4)])  11.7 us
    all_gather x1, blocking collectives, local(): row = lax.all_gather(chip, ('x',), axis=0)  11.2 us
    ppermute x1, starting transfers between devices, local(): taken = lax.ppermute(give, AXES, mirror)  9.05 us
  transfers between devices with their start and end apart: 22, of which 6 were waited for; matrix products, arithmetic and copies ran while one was open for 0% of the time, Pallas kernels for 13%

profile of v7, /device:TPU:9, one launch (start us, length us, event | category | flops | bytes accessed | tf_op | source)
XLA Modules:
  0.0 285.7 jit_solution(6263795477410811545)
XLA Ops:
  0.1 0.3 fusion.2
  0.4 0.8 pad_maximum_fusion.3
  1.1 2.2 rotate_all.1
  3.3 0.7 collective-permute-start.1
  4.0 1.1 collective-permute-done.1
  5.1 0.9 broadcast_select_fusion.1
  6.0 11.2 %all-gather = bf16[1024,256]{1,0:T(8,128)(2,1)S(1)} all-gather(bf16[256,256]{1,0:T(8,128)(2,1)S(1)} %pad_maximum_fusion.2), channel_id=2, replica_groups=mesh['zh'=2,'y'=4,'c'=2,'zl'=2,'x'=4] {'x'}, dimensions={0}, use_global_device_ids=true | all-gather | bytes 655360 | tf_op jit(solution)/shard_map/all_gather | solution.py:731
  17.2 3.8 %collective-permute-start.12 = (bf16[512,256]{1,0:T(8,128)(2,1)S(1)}, bf16[512,256]{1,0:T(8,128)(2,1)S(1)}, u32[]{:S(2)}, u32[]{:S(2)}) collective-permute-start(bf16[512,256]{1,0:T(8,128)(2,1)S(1)} %bitcast.22), channel_id=1, source_target_pairs={{0,68},{4,0},{64,4},{68,64},{1,69},{5,1},{65,5},{69,65},{2,70},{6,... | collective-permute-start | bytes 786440 | tf_op jit(solution)/shard_map/ppermute | solution.py:695
  21.1 0.2 collective-permute-start.5
  21.2 2.3 collective-permute-start.6
  23.6 0.7 collective-permute-start.9
  24.3 6.7 %collective-permute-done.12 = bf16[512,256]{1,0:T(8,128)(2,1)S(1)} collective-permute-done((bf16[512,256]{1,0:T(8,128)(2,1)S(1)}, bf16[512,256]{1,0:T(8,128)(2,1)S(1)}, u32[]{:S(2)}, u32[]{:S(2)}) %collective-permute-start.12) | collective-permute-done | bytes 262176 | tf_op jit(solution)/shard_map/ppermute | solution.py:695
  31.0 1.3 collective-permute-start.2
  32.3 0.2 collective-permute-start.14
  32.6 1.3 collective-permute-start.18
  33.9 0.1 collective-permute-start.16
  34.0 0.9 collective-permute-done.9
  35.0 9.1 %collective-permute-start = (bf16[128,1024]{1,0:T(8,128)(2,1)}, bf16[128,1024]{1,0:T(8,128)(2,1)S(1)}, u32[]{:S(2)}, u32[]{:S(2)}) collective-permute-start(bf16[128,1024]{1,0:T(8,128)(2,1)} %get-tuple-element.25), channel_id=1, source_target_pairs={{0,127},{1,126},{2,125},{3,124},{4,123},{5,122},{6,121},{7,120},{8... | collective-permute-start | bytes 786440 | tf_op jit(solution)/shard_map/ppermute | solution.py:725
  44.1 0.1 collective-permute-start.7
  44.2 7.1 %collective-permute-done.theirs_ref = bf16[128,1024]{1,0:T(8,128)(2,1)S(1)} collective-permute-done((bf16[128,1024]{1,0:T(8,128)(2,1)}, bf16[128,1024]{1,0:T(8,128)(2,1)S(1)}, u32[]{:S(2)}, u32[]{:S(2)}) %collective-permute-start) | collective-permute-done | bytes 262176 | tf_op jit(solution)/shard_map/ppermute | solution.py:725
  51.3 1.5 collective-permute-start.19
  52.8 0.8 collective-permute-start.3
  53.5 0.8 copy-done.8
  54.3 2.8 collective-permute-start.17
  57.1 0.6 pad_add_fusion.meta_ref
  57.7 2.5 collective-permute-start.15
  60.2 4.1 %collective-permute-done.10.refs_4_ = bf16[1024,256]{1,0:T(8,128)(2,1)} collective-permute-done((bf16[1024,256]{1,0:T(8,128)(2,1)S(1)}, bf16[1024,256]{1,0:T(8,128)(2,1)}, u32[]{:S(2)}, u32[]{:S(2)}) %collective-permute-start.10) | collective-permute-done | bytes 524320 | tf_op jit(solution)/shard_map/ppermute | solution.py:695
  64.3 3.2 %collective-permute-start.8 = (bf16[1024,256]{1,0:T(8,128)(2,1)}, bf16[1024,256]{1,0:T(8,128)(2,1)}, u32[]{:S(2)}, u32[]{:S(2)}) collective-permute-start(bf16[1024,256]{1,0:T(8,128)(2,1)} %collective-permute-done.7.refs_3_), channel_id=1, source_target_pairs={{0,68},{4,0},{64,4},{68,64},{1,69},{5,1},{65,5},{69,65},{2,70},{6,... | collective-permute-start | bytes 1572872 | tf_op jit(solution)/shard_map/ppermute | solution.py:695
  67.5 2.3 collective-permute-start.11
  69.8 0.0 collective-permute-start.4
  69.8 11.9 %attend_first.1 = (f32[2048,128]{1,0:T(8,128)}, f32[2048,128]{1,0:T(8,128)}, f32[2048,128]{1,0:T(8,128)}) custom-call(s32[4]{0:T(128)} %pad_add_fusion.meta_ref, bf16[128,1024]{1,0:T(8,128)(2,1)} %copy-done.10, bf16[128,1024]{1,0:T(8,128)(2,1)} %get-tuple-element.26.own_ref, bf16[1024,256]{1,0:T(8,128)(2,1)} %copy-done.1, bf16[1024,256]{1,0:T(8,128)(2,1)} %copy-done.4, ...), custom_call_target="tpu_custom_call" | custom-call | flops 2147483648 | bytes 2097152 | tf_op jit(solution)/shard_map/attend_first/pallas_call | solution.py:303
  81.8 17.7 %attend_more.1 = (f32[2048,128]{1,0:T(8,128)}, f32[2048,128]{1,0:T(8,128)}, f32[2048,128]{1,0:T(8,128)}) custom-call(s32[4]{0:T(128)} %pad_add_fusion.meta_ref, bf16[128,1024]{1,0:T(8,128)(2,1)} %copy-done.10, bf16[128,1024]{1,0:T(8,128)(2,1)} %get-tuple-element.26.own_ref, bf16[1024,256]{1,0:T(8,128)(2,1)} %collective-permute-done.3.refs_0_, ...), custom_call_target="tpu_custom_call" | custom-call | flops 4294967296 | bytes 4194304 | tf_op jit(solution)/shard_map/attend_more/pallas_call | solution.py:303
  99.5 0.0 copy-start.5
  99.5 0.0 copy-start.9
  99.6 0.8 copy-done.9
  100.3 8.2 %attend_last.1 = (bf16[128,1024]{1,0:T(8,128)(2,1)}, bf16[128,1024]{1,0:T(8,128)(2,1)}) custom-call(s32[4]{0:T(128)} %pad_add_fusion.meta_ref, bf16[128,1024]{1,0:T(8,128)(2,1)} %copy-done.10, bf16[128,1024]{1,0:T(8,128)(2,1)} %get-tuple-element.26.own_ref, bf16[1024,256]{1,0:T(8,128)(2,1)} %collective-permute-done.4.refs_0_, ...), custom_call_target="tpu_custom_call" | custom-call | flops 2147483648 | bytes 2097152 | tf_op jit(solution)/shard_map/attend_last/pallas_call | solution.py:303
  108.6 6.8 %collective-permute-start.20 = (bf16[128,1024]{1,0:T(8,128)(2,1)}, bf16[128,1024]{1,0:T(8,128)(2,1)S(1)}, u32[]{:S(2)}, u32[]{:S(2)}) collective-permute-start(bf16[128,1024]{1,0:T(8,128)(2,1)} %get-tuple-element.36), channel_id=1, source_target_pairs={{0,127},{1,126},{2,125},{3,124},{4,123},{5,122},{6,121},{7,120},{8... | collective-permute-start | bytes 786440 | tf_op jit(solution)/shard_map/ppermute | solution.py:754
  115.4 0.6 fusion.8.ids_ref
  116.0 1.7 plan.1
  117.7 3.7 %project_own.1.part_ref = f32[128,2048]{1,0:T(8,128)} custom-call(s32[1]{0:T(128)} %bitcast.core_ref, bf16[128,1024]{1,0:T(8,128)(2,1)} %get-tuple-element.35.own_ref, bf16[2048,2048]{1,0:T(8,128)(2,1)} %w_ref.3), custom_call_target="tpu_custom_call" | custom-call | flops 536870912 | bytes 4194304 | tf_op jit(solution)/shard_map/project_own/pallas_call | solution.py:348
  121.4 0.7 copy-done.2
  122.1 8.1 %project.1 = (bf16[128,2048]{1,0:T(8,128)(2,1)}, bf16[128,2048]{1,0:T(8,128)(2,1)}, bf16[128,144,128]{2,1,0:T(8,128)(2,1)}) custom-call(s32[1]{0:T(128)} %bitcast.core_ref, f32[128,2048]{1,0:T(8,128)} %project_own.1.part_ref, bf16[128,1024]{1,0:T(8,128)(2,1)} %copy-done.2, bf16[2048,2048]{1,0:T(8,128)(2,1)} %w_ref.3, bf16[128,2048]{1,0:T(8,128)(2,1)} %hidden_ref.1, ...), custom_call_target="tpu_custom_call" | custom-call | tf_op jit(solution)/shard_map/project/pallas_call | solution.py:498
  130.2 67.1 %all_to_all.10.in_ref = bf16[128,144,128]{2,1,0:T(8,128)(2,1)} all-to-all(bf16[128,144,128]{2,1,0:T(8,128)(2,1)} %get-tuple-element.43), channel_id=1, replica_groups=mesh['zh'=2,'y'=4,'c'=2,'zl'=2,'x'=4] {'zh','zl','y','x','c'}, dimensions={0} | all-to-all | bytes 9437184 | tf_op jit(solution)/shard_map/all_to_all | solution.py:691
  197.2 20.1 %experts_of.1 = bf16[128,144,128]{2,1,0:T(8,128)(2,1)} custom-call(bf16[128,144,128]{2,1,0:T(8,128)(2,1)} %all_to_all.10.in_ref, bf16[2048,768]{1,0:T(8,128)(2,1)} %bitcast.14, bf16[2048,768]{1,0:T(8,128)(2,1)} %bitcast.15, bf16[768,2048]{1,0:T(8,128)(2,1)} %bitcast.16), custom_call_target="tpu_custom_call" | custom-call | tf_op jit(solution)/shard_map/experts_of/pallas_call | solution.py:611
  217.4 7.1 %all-to-all-start.1 = ((bf16[128,144,128]{2,1,0:T(8,128)(2,1)}), bf16[128,144,128]{2,1,0:T(8,128)(2,1)}, u32[]{:S(2)}, u32[]{:S(2)}) async-start(bf16[128,144,128]{2,1,0:T(8,128)(2,1)} %experts_of.1), calls=%async_computation.1 | async-start | bytes 9437184 | tf_op jit(solution)/shard_map/all_to_all | solution.py:691
  224.4 2.6 routes.1
  227.1 53.2 %all-to-all-done.1.in_ref.in_over_ref = bf16[128,144,128]{2,1,0:T(8,128)(2,1)} async-done(((bf16[128,144,128]{2,1,0:T(8,128)(2,1)}), bf16[128,144,128]{2,1,0:T(8,128)(2,1)}, u32[]{:S(2)}, u32[]{:S(2)}) %all-to-all-start.1) | async-done | bytes 4718624 | tf_op jit(solution)/shard_map/all_to_all | solution.py:691
  280.3 5.5 %combine.1 = bf16[128,2048]{1,0:T(8,128)(2,1)} custom-call(bf16[128,1024]{1,0:T(8,128)(2,1)} %get-tuple-element.41.mix_ref, bf16[128,128]{1,0:T(8,128)(2,1)} %get-tuple-element.42.last_ref, bf16[128,144,128]{2,1,0:T(8,128)(2,1)} %all-to-all-done.1.in_ref.in_over_ref, bf16[128,144,128]{2,1,0:T(8,128)(2,1)} %all-to-all-done.1.in_ref.in_over_ref, ...), custom_call_target="tpu_custom_call" | custom-call | tf_op jit(solution)/shard_map/combine/pallas_call | solution.py:672
  (45 shorter events, 0.3 us)
Async XLA Ops:
  3.3 1.8 collective-permute-start.1
  17.2 13.7 %collective-permute-start.12 = (bf16[512,256]{1,0:T(8,128)(2,1)S(1)}, bf16[512,256]{1,0:T(8,128)(2,1)S(1)}, u32[]{:S(2)}, u32[]{:S(2)}) collective-permute-start(bf16[512,256]{1,0:T(8,128)(2,1)S(1)} %bitcast.22), channel_id=1, source_target_pairs={{0,68},{4,0},{64,4},{68,64},{1,69},{5,1},{65,5},{69,65},{2,70},{6,... | collective-permute-start | bytes 786440 | tf_op jit(solution)/shard_map/ppermute | solution.py:695
  21.1 11.2 %collective-permute-start.13 = (bf16[512,256]{1,0:T(8,128)(2,1)S(1)}, bf16[512,256]{1,0:T(8,128)(2,1)S(1)}, u32[]{:S(2)}, u32[]{:S(2)}) collective-permute-start(bf16[512,256]{1,0:T(8,128)(2,1)S(1)} %bitcast.23), channel_id=1, source_target_pairs={{0,64},{4,68},{64,0},{68,4},{1,65},{5,69},{65,1},{69,5},{2,66},{6,... | collective-permute-start | bytes 786440 | tf_op jit(solution)/shard_map/ppermute | solution.py:695
  21.1 11.5 %collective-permute-start.5 = (bf16[512,256]{1,0:T(8,128)(2,1)S(1)}, bf16[512,256]{1,0:T(8,128)(2,1)S(1)}, u32[]{:S(2)}, u32[]{:S(2)}) collective-permute-start(bf16[512,256]{1,0:T(8,128)(2,1)S(1)} %bitcast.18), channel_id=1, source_target_pairs={{0,48},{16,0},{32,16},{48,32},{1,49},{17,1},{33,17},{49,33},{2,50}... | collective-permute-start | bytes 786440 | tf_op jit(solution)/shard_map/ppermute | solution.py:695
  21.2 12.7 %collective-permute-start.6 = (bf16[512,256]{1,0:T(8,128)(2,1)S(1)}, bf16[512,256]{1,0:T(8,128)(2,1)S(1)}, u32[]{:S(2)}, u32[]{:S(2)}) collective-permute-start(bf16[512,256]{1,0:T(8,128)(2,1)S(1)} %bitcast.19), channel_id=1, source_target_pairs={{0,32},{16,48},{32,0},{48,16},{1,33},{17,49},{33,1},{49,17},{2,34}... | collective-permute-start | bytes 786440 | tf_op jit(solution)/shard_map/ppermute | solution.py:695
  23.6 11.4 %collective-permute-start.9 = (bf16[512,256]{1,0:T(8,128)(2,1)S(1)}, bf16[512,256]{1,0:T(8,128)(2,1)S(1)}, u32[]{:S(2)}, u32[]{:S(2)}) collective-permute-start(bf16[512,256]{1,0:T(8,128)(2,1)S(1)} %bitcast.24), channel_id=1, source_target_pairs={{0,4},{4,64},{64,68},{68,0},{1,5},{5,65},{65,69},{69,1},{2,6},{6,6... | collective-permute-start | bytes 786440 | tf_op jit(solution)/shard_map/ppermute | solution.py:695
  31.0 13.1 %collective-permute-start.2 = (bf16[512,256]{1,0:T(8,128)(2,1)S(1)}, bf16[512,256]{1,0:T(8,128)(2,1)S(1)}, u32[]{:S(2)}, u32[]{:S(2)}) collective-permute-start(bf16[512,256]{1,0:T(8,128)(2,1)S(1)} %bitcast.20), channel_id=1, source_target_pairs={{0,16},{16,32},{32,48},{48,0},{1,17},{17,33},{33,49},{49,1},{2,18}... | collective-permute-start | bytes 786440 | tf_op jit(solution)/shard_map/ppermute | solution.py:695
  32.3 37.5 %copy-start.3 = (bf16[1024,256]{1,0:T(8,128)(2,1)}, bf16[1024,256]{1,0:T(8,128)(2,1)S(1)}, u32[]{:S(2)}) copy-start(bf16[1024,256]{1,0:T(8,128)(2,1)S(1)} %constant_dynamic-update-slice_fusion.2.refs_3_) | copy-start | bytes 1572868
  32.3 18.9 %collective-permute-start.14 = (bf16[1024,256]{1,0:T(8,128)(2,1)S(1)}, bf16[1024,256]{1,0:T(8,128)(2,1)S(1)}, u32[]{:S(2)}, u32[]{:S(2)}) collective-permute-start(bf16[1024,256]{1,0:T(8,128)(2,1)S(1)} %constant_dynamic-update-slice_fusion.2.refs_3_), channel_id=1, source_target_pairs={{0,48},{16,0},{32,16},{48,32},{1,49},{17,1},{33,17},{49,33},{2,50}... | collective-permute-start | bytes 1572872 | tf_op jit(solution)/shard_map/ppermute | solution.py:695
  32.6 20.2 %collective-permute-start.18 = (bf16[1024,256]{1,0:T(8,128)(2,1)S(1)}, bf16[1024,256]{1,0:T(8,128)(2,1)S(1)}, u32[]{:S(2)}, u32[]{:S(2)}) collective-permute-start(bf16[1024,256]{1,0:T(8,128)(2,1)S(1)} %constant_dynamic-update-slice_fusion.2.refs_3_), channel_id=1, source_target_pairs={{0,16},{16,32},{32,48},{48,0},{1,17},{17,33},{33,49},{49,1},{2,18}... | collective-permute-start | bytes 1572872 | tf_op jit(solution)/shard_map/ppermute | solution.py:695
  33.9 35.9 %copy-start.4 = (bf16[1024,256]{1,0:T(8,128)(2,1)}, bf16[1024,256]{1,0:T(8,128)(2,1)S(1)}, u32[]{:S(2)}) copy-start(bf16[1024,256]{1,0:T(8,128)(2,1)S(1)} %constant_dynamic-update-slice_fusion.refs_1_) | copy-start | bytes 1572868
  33.9 19.6 %collective-permute-start.16 = (bf16[1024,256]{1,0:T(8,128)(2,1)S(1)}, bf16[1024,256]{1,0:T(8,128)(2,1)S(1)}, u32[]{:S(2)}, u32[]{:S(2)}) collective-permute-start(bf16[1024,256]{1,0:T(8,128)(2,1)S(1)} %constant_dynamic-update-slice_fusion.refs_1_), channel_id=1, source_target_pairs={{0,4},{4,64},{64,68},{68,0},{1,5},{5,65},{65,69},{69,1},{2,6},{6,6... | collective-permute-start | bytes 1572872 | tf_op jit(solution)/shard_map/ppermute | solution.py:695
  35.0 16.3 %collective-permute-start = (bf16[128,1024]{1,0:T(8,128)(2,1)}, bf16[128,1024]{1,0:T(8,128)(2,1)S(1)}, u32[]{:S(2)}, u32[]{:S(2)}) collective-permute-start(bf16[128,1024]{1,0:T(8,128)(2,1)} %get-tuple-element.25), channel_id=1, source_target_pairs={{0,127},{1,126},{2,125},{3,124},{4,123},{5,122},{6,121},{7,120},{8... | collective-permute-start | bytes 786440 | tf_op jit(solution)/shard_map/ppermute | solution.py:725
  44.0 25.8 %copy-start = (bf16[1024,256]{1,0:T(8,128)(2,1)}, bf16[1024,256]{1,0:T(8,128)(2,1)S(1)}, u32[]{:S(2)}) copy-start(bf16[1024,256]{1,0:T(8,128)(2,1)S(1)} %pad_maximum_fusion.1.refs_2_) | copy-start | bytes 1572868
  44.1 13.6 %collective-permute-start.7 = (bf16[1024,256]{1,0:T(8,128)(2,1)S(1)}, bf16[1024,256]{1,0:T(8,128)(2,1)}, u32[]{:S(2)}, u32[]{:S(2)}) collective-permute-start(bf16[1024,256]{1,0:T(8,128)(2,1)S(1)} %constant_dynamic-update-slice_fusion.refs_1_), channel_id=1, source_target_pairs={{0,68},{4,0},{64,4},{68,64},{1,69},{5,1},{65,5},{69,65},{2,70},{6,... | collective-permute-start | bytes 1572872 | tf_op jit(solution)/shard_map/ppermute | solution.py:695
  44.2 25.6 %copy-start.1 = (bf16[1024,256]{1,0:T(8,128)(2,1)}, bf16[1024,256]{1,0:T(8,128)(2,1)S(1)}, u32[]{:S(2)}) copy-start(bf16[1024,256]{1,0:T(8,128)(2,1)S(1)} %pad_maximum_fusion.refs_0_) | copy-start | bytes 1572868
  51.3 18.6 %copy-start.10 = (bf16[128,1024]{1,0:T(8,128)(2,1)}, bf16[128,1024]{1,0:T(8,128)(2,1)S(1)}, u32[]{:S(2)}) copy-start(bf16[128,1024]{1,0:T(8,128)(2,1)S(1)} %collective-permute-done.theirs_ref) | copy-start | bytes 786436
  51.3 13.0 %collective-permute-start.10 = (bf16[1024,256]{1,0:T(8,128)(2,1)S(1)}, bf16[1024,256]{1,0:T(8,128)(2,1)}, u32[]{:S(2)}, u32[]{:S(2)}) collective-permute-start(bf16[1024,256]{1,0:T(8,128)(2,1)S(1)} %pad_maximum_fusion.1.refs_2_), channel_id=1, source_target_pairs={{0,16},{16,32},{32,48},{48,0},{1,17},{17,33},{33,49},{49,1},{2,18}... | collective-permute-start | bytes 1572872 | tf_op jit(solution)/shard_map/ppermute | solution.py:695
  51.3 30.5 %copy-start.6 = (bf16[1024,256]{1,0:T(8,128)(2,1)}, bf16[1024,256]{1,0:T(8,128)(2,1)S(1)}, u32[]{:S(2)}) copy-start(bf16[1024,256]{1,0:T(8,128)(2,1)S(1)} %collective-permute-done.14.refs_7_) | copy-start | bytes 1572868
  51.3 16.2 %collective-permute-start.19 = (bf16[1024,256]{1,0:T(8,128)(2,1)S(1)}, bf16[1024,256]{1,0:T(8,128)(2,1)}, u32[]{:S(2)}, u32[]{:S(2)}) collective-permute-start(bf16[1024,256]{1,0:T(8,128)(2,1)S(1)} %pad_maximum_fusion.1.refs_2_), channel_id=1, source_target_pairs={{0,48},{16,0},{32,16},{48,32},{1,49},{17,1},{33,17},{49,33},{2,50}... | collective-permute-start | bytes 1572872 | tf_op jit(solution)/shard_map/ppermute | solution.py:695
  52.7 29.0 %copy-start.7 = (bf16[1024,256]{1,0:T(8,128)(2,1)}, bf16[1024,256]{1,0:T(8,128)(2,1)S(1)}, u32[]{:S(2)}) copy-start(bf16[1024,256]{1,0:T(8,128)(2,1)S(1)} %collective-permute-done.18.refs_5_) | copy-start | bytes 1572868
  52.8 17.0 %collective-permute-start.3 = (bf16[1024,256]{1,0:T(8,128)(2,1)S(1)}, bf16[1024,256]{1,0:T(8,128)(2,1)}, u32[]{:S(2)}, u32[]{:S(2)}) collective-permute-start(bf16[1024,256]{1,0:T(8,128)(2,1)S(1)} %pad_maximum_fusion.refs_0_), channel_id=1, source_target_pairs={{0,4},{4,64},{64,68},{68,0},{1,5},{5,65},{65,69},{69,1},{2,6},{6,6... | collective-permute-start | bytes 1572872 | tf_op jit(solution)/shard_map/ppermute | solution.py:695
  53.5 0.8 copy-start.8
  54.3 27.4 %collective-permute-start.17 = (bf16[1024,256]{1,0:T(8,128)(2,1)S(1)}, bf16[1024,256]{1,0:T(8,128)(2,1)}, u32[]{:S(2)}, u32[]{:S(2)}) collective-permute-start(bf16[1024,256]{1,0:T(8,128)(2,1)S(1)} %pad_maximum_fusion.refs_0_), channel_id=1, source_target_pairs={{0,68},{4,0},{64,4},{68,64},{1,69},{5,1},{65,5},{69,65},{2,70},{6,... | collective-permute-start | bytes 1572872 | tf_op jit(solution)/shard_map/ppermute | solution.py:695
  57.7 41.8 %collective-permute-start.15 = (bf16[1024,256]{1,0:T(8,128)(2,1)S(1)}, bf16[1024,256]{1,0:T(8,128)(2,1)S(1)}, u32[]{:S(2)}, u32[]{:S(2)}) collective-permute-start(bf16[1024,256]{1,0:T(8,128)(2,1)S(1)} %collective-permute-done.14.refs_7_), channel_id=1, source_target_pairs={{0,48},{16,0},{32,16},{48,32},{1,49},{17,1},{33,17},{49,33},{2,50}... | collective-permute-start | bytes 1572872 | tf_op jit(solution)/shard_map/ppermute | solution.py:695
  64.3 35.3 %collective-permute-start.8 = (bf16[1024,256]{1,0:T(8,128)(2,1)}, bf16[1024,256]{1,0:T(8,128)(2,1)}, u32[]{:S(2)}, u32[]{:S(2)}) collective-permute-start(bf16[1024,256]{1,0:T(8,128)(2,1)} %collective-permute-done.7.refs_3_), channel_id=1, source_target_pairs={{0,68},{4,0},{64,4},{68,64},{1,69},{5,1},{65,5},{69,65},{2,70},{6,... | collective-permute-start | bytes 1572872 | tf_op jit(solution)/shard_map/ppermute | solution.py:695
  67.5 32.1 %collective-permute-start.11 = (bf16[1024,256]{1,0:T(8,128)(2,1)}, bf16[1024,256]{1,0:T(8,128)(2,1)}, u32[]{:S(2)}, u32[]{:S(2)}) collective-permute-start(bf16[1024,256]{1,0:T(8,128)(2,1)} %collective-permute-done.10.refs_4_), channel_id=1, source_target_pairs={{0,16},{16,32},{32,48},{48,0},{1,17},{17,33},{33,49},{49,1},{2,18}... | collective-permute-start | bytes 1572872 | tf_op jit(solution)/shard_map/ppermute | solution.py:695
  69.8 29.8 %collective-permute-start.4 = (bf16[1024,256]{1,0:T(8,128)(2,1)}, bf16[1024,256]{1,0:T(8,128)(2,1)}, u32[]{:S(2)}, u32[]{:S(2)}) collective-permute-start(bf16[1024,256]{1,0:T(8,128)(2,1)} %collective-permute-done.3.refs_0_), channel_id=1, source_target_pairs={{0,4},{4,64},{64,68},{68,0},{1,5},{5,65},{65,69},{69,1},{2,6},{6,6... | collective-permute-start | bytes 1572872 | tf_op jit(solution)/shard_map/ppermute | solution.py:695
  99.5 15.9 %copy-start.5 = (s32[128,8]{0,1:T(8,128)S(1)}, s32[128,8]{0,1:T(8,128)}, u32[]{:S(2)}) copy-start(s32[128,8]{0,1:T(8,128)} %param.18) | copy-start | bytes 12292
  99.5 0.8 copy-start.9
  108.6 12.9 %collective-permute-start.20 = (bf16[128,1024]{1,0:T(8,128)(2,1)}, bf16[128,1024]{1,0:T(8,128)(2,1)S(1)}, u32[]{:S(2)}, u32[]{:S(2)}) collective-permute-start(bf16[128,1024]{1,0:T(8,128)(2,1)} %get-tuple-element.36), channel_id=1, source_target_pairs={{0,127},{1,126},{2,125},{3,124},{4,123},{5,122},{6,121},{7,120},{8... | collective-permute-start | bytes 786440 | tf_op jit(solution)/shard_map/ppermute | solution.py:754
  121.4 0.7 copy-start.2
  217.4 62.9 %all-to-all-start.1 = ((bf16[128,144,128]{2,1,0:T(8,128)(2,1)}), bf16[128,144,128]{2,1,0:T(8,128)(2,1)}, u32[]{:S(2)}, u32[]{:S(2)}) async-start(bf16[128,144,128]{2,1,0:T(8,128)(2,1)} %experts_of.1), calls=%async_computation.1 | async-start | bytes 9437184 | tf_op jit(solution)/shard_map/all_to_all | solution.py:691
